TPU v7x, 768 devices: a whole 4x8x12 slice. The times are simulated.
768 devices in a mesh: src: 12 (over x, z_lo), rcv: 64 (over z_hi, y, core).
Axes of the slice: x: 4, y: 8, z: 12 (z_hi: 4, z_lo: 3; z = z_hi * 3 + z_lo), core: 2. Of those that a mesh axis runs over, the one named last changes fastest.
Arguments:
- record: bfloat16 [1, 2, 6144, 6144], P(None, None, 'rcv', 'src'), may hold values from -6 to 6
- panel_offset: int32 [768], replicated, may hold values from 0 to 7
Outputs:
- primaries: bfloat16 [1, 2, 6144, 6144], P(None, None, 'rcv', 'src')
- multiples: bfloat16 [1, 2, 6144, 6144], P(None, None, 'rcv', 'src')
Inputs may be any that keep to these rules, and one draw needn't show every extreme that they name: Panel station j is 8 * j + panel_offset[j].
All inputs are finite; a program needn't handle non-finite values.
Results may differ from a plain program's by a relative error of at most 0.003.
The roundings to bfloat16 on the way count: a program that leaves them out, or rounds other values in their place, can miss the bound.
Values may be sent and summed in bfloat16 or wider, within the bound.
No kernel may reach another device: no remote copies, remote signals or barrier semaphores. Data moves between devices by JAX's collectives and lax.ppermute only.
A program may use at most 32 MiB of HBM per device.

v0:
```python
import jax
import jax.numpy as jnp
from jax import lax
from jax.sharding import PartitionSpec as P

STRIDE = 8
REACH = 4
SWEEPS = 2


weight_eps = 1e-06


def extended(cells, sides, width, closed):
    for axis, dim in sides:
        count = lax.axis_size(axis)
        ends = count if closed else count - 1
        head = lax.slice_in_dim(cells, 0, width, axis=dim)
        tail = lax.slice_in_dim(cells, cells.shape[dim] - width, cells.shape[dim], axis=dim)
        cells = jnp.concatenate(
            [
                lax.ppermute(tail, axis, [(i, (i + 1) % count) for i in range(ends)]),
                cells,
                lax.ppermute(head, axis, [((i + 1) % count, i) for i in range(ends)]),
            ],
            axis=dim,
        )
    return cells


def copy_for_each(value, axis):
    copies = jnp.broadcast_to(value, (lax.axis_size(axis), *value.shape))
    return lax.all_to_all(copies, axis, split_axis=0, concat_axis=0, tiled=True)


def joined_along(pieces, dim):
    lengths = list(pieces.shape[1:])
    lengths[dim] *= pieces.shape[0]
    return jnp.moveaxis(pieces, 0, dim).reshape(lengths)


def gathered_copies(value, axis, dim):
    pieces = copy_for_each(value, axis)
    return joined_along(pieces, dim)


def reorder_keys(values, rcv_count, src_count):
    full_shape = values.shape
    grouped = values.reshape(
        full_shape[:-1] + (rcv_count, src_count, full_shape[-1] // (rcv_count * src_count))
    )
    return jnp.swapaxes(grouped, -3, -2).reshape(full_shape)


def average_pair(first_part, second_part):
    return ((first_part.astype(jnp.float32) + second_part.astype(jnp.float32)) * 0.5).astype(
        jnp.bfloat16
    )


def cross_dot(left_mat, right_mat):
    return lax.dot_general(
        left_mat, right_mat, (((2,), (2,)), ((0,), (0,))), preferred_element_type=jnp.float32
    )


def predict_block(right_side, left_side):
    right_real = right_side[:, 0]
    right_imag = right_side[:, 1]
    left_real = left_side[:, 0]
    left_imag = left_side[:, 1]
    pred_real = cross_dot(right_real, left_real) - cross_dot(right_imag, left_imag)
    pred_imag = cross_dot(right_real, left_imag) + cross_dot(right_imag, left_real)
    return jnp.stack([pred_real, pred_imag], axis=1)


def neighbour_sum(partial_terms, src_count, rcv_pos, rcv_count):
    freq_count, chan_count, rcv_cols, src_rows = partial_terms.shape
    run_len = rcv_cols // src_count
    runs_view = partial_terms.reshape(freq_count, chan_count, src_count, run_len, src_rows)
    padded = extended(runs_view.astype(jnp.bfloat16), (("rcv", 3),), REACH, True).astype(
        runs_view.dtype
    )
    lower_rim = padded[:, :, :, :REACH]
    middle = padded[:, :, :, REACH : REACH + run_len]
    upper_rim = padded[:, :, :, REACH + run_len :]
    zero_rim = jnp.zeros_like(lower_rim[:, :, :1])
    lower_rim = jnp.where(
        rcv_pos == 0, jnp.concatenate([zero_rim, lower_rim[:, :, :-1]], axis=2), lower_rim
    )
    upper_rim = jnp.where(
        rcv_pos == rcv_count - 1,
        jnp.concatenate([upper_rim[:, :, 1:], zero_rim], axis=2),
        upper_rim,
    )
    padded = jnp.concatenate([lower_rim, middle, upper_rim], axis=3)
    recv_total = padded[:, :, :, 0:run_len]
    for shift_pos in range(1, 2 * REACH + 1):
        recv_total = recv_total + padded[:, :, :, shift_pos : shift_pos + run_len]
    recv_total = recv_total.reshape(freq_count, chan_count, rcv_cols, src_rows)
    src_padded = extended(recv_total.astype(jnp.bfloat16), (("src", 3),), REACH, False).astype(
        recv_total.dtype
    )
    box_totals = src_padded[..., 0:src_rows]
    for shift_pos in range(1, 2 * REACH + 1):
        box_totals = box_totals + src_padded[..., shift_pos : shift_pos + src_rows]
    return box_totals


def run_sweeps(data_bf, pred_bf, summer):
    data_f32 = data_bf.astype(jnp.float32)
    pred_f32 = pred_bf.astype(jnp.float32)
    data_real = data_f32[:, 0]
    data_imag = data_f32[:, 1]
    pred_real = pred_f32[:, 0]
    pred_imag = pred_f32[:, 1]
    err_real = data_real
    err_imag = data_imag
    for sweep_step in range(SWEEPS):
        weight = 1.5 - jnp.tanh(err_real * err_real + err_imag * err_imag)
        partial_terms = jnp.stack(
            [
                weight * (pred_real * data_real + pred_imag * data_imag),
                weight * (pred_real * data_imag - pred_imag * data_real),
                weight * (pred_real * pred_real + pred_imag * pred_imag),
            ],
            axis=1,
        )
        box_totals = summer(partial_terms)
        denom = box_totals[:, 2] + weight_eps
        gain_real = box_totals[:, 0] / denom
        gain_imag = box_totals[:, 1] / denom
        err_real = data_real - (gain_real * pred_real - gain_imag * pred_imag)
        err_imag = data_imag - (gain_real * pred_imag + gain_imag * pred_real)
    return jnp.stack([err_real, err_imag], axis=1)


def shards(record, panel_offset):
    src_count = lax.axis_size("src")
    rcv_count = lax.axis_size("rcv")
    src_pos = lax.axis_index("src")
    rcv_pos = lax.axis_index("rcv")
    rcv_cols = record.shape[2]
    src_rows = record.shape[3]
    run_len = rcv_cols // src_count
    per_run = run_len // STRIDE
    panel_len = panel_offset.shape[0]
    run_ids = jnp.arange(src_count, dtype=jnp.int32)[:, None]
    within = jnp.arange(per_run, dtype=jnp.int32)[None, :]
    col_groups = (src_rows * run_ids + run_len * rcv_pos) // STRIDE + within
    col_index = (run_len * run_ids + STRIDE * within + jnp.take(panel_offset, col_groups)).reshape(
        -1
    )
    row_groups = jnp.arange(src_rows // STRIDE, dtype=jnp.int32)
    row_index = STRIDE * row_groups + jnp.take(
        panel_offset, src_rows // STRIDE * src_pos + row_groups
    )
    col_piece = jnp.swapaxes(jnp.take(record, col_index, axis=2), 2, 3)
    row_piece = jnp.take(record, row_index, axis=3)
    own_front = reorder_keys(
        lax.all_to_all(col_piece, "rcv", split_axis=2, concat_axis=3, tiled=True),
        rcv_count,
        src_count,
    )
    own_behind = lax.all_to_all(row_piece, "src", split_axis=2, concat_axis=3, tiled=True)
    owned_rows = average_pair(own_front, own_behind)
    right_side = gathered_copies(owned_rows, "src", 2)
    prediction = predict_block(right_side, lax.all_gather(owned_rows, "rcv", axis=2, tiled=True))
    pred_round = lax.optimization_barrier(prediction.astype(jnp.bfloat16))
    multiples = (prediction * panel_len ** (-0.5)).astype(jnp.bfloat16)

    def runs_total(partial_terms):
        return neighbour_sum(partial_terms, src_count, rcv_pos, rcv_count)

    primaries = run_sweeps(record, pred_round, runs_total).astype(jnp.bfloat16)
    return (primaries, multiples)


def solution(mesh):
    in_specs = (P(None, None, "rcv", "src"), P())
    out_specs = (P(None, None, "rcv", "src"), P(None, None, "rcv", "src"))
    return jax.shard_map(shards, mesh=mesh, in_specs=in_specs, out_specs=out_specs, check_vma=False)
```

profile of v0, /device:TPU:61, one launch (start us, length us, event | category | flops | bytes accessed | tf_op | source)
XLA Modules:
  0.0 222.0 jit_solution(953655327701816450)
XLA Ops:
  7.2 0.6 copy-done
  7.9 0.7 gather_fusion.2
  8.6 1.1 copy.48
  9.7 0.6 gather_fusion.3
  10.4 0.1 broadcast_select_fusion
  10.5 0.1 copy.42
  10.6 0.7 reshape.1072
  11.4 7.9 %all-to-all-start.1 = ((bf16[12,2,512]{2,1,0:T(2,128)(2,1)}), bf16[12,2,512]{2,1,0:T(2,128)(2,1)S(1)}, u32[]{:S(2)}, u32[]{:S(2)}) async-start(bf16[12,2,512]{2,1,0:T(2,128)(2,1)} %reshape.1072), calls=%async_computation.1 | async-start | bytes 49152 | tf_op jit(solution)/shard_map/all_to_all | solution.py:165
  19.2 0.6 gather_fusion
  20.0 0.2 copy.53
  20.2 0.6 gather_fusion.1
  20.9 0.9 copy.38
  21.8 1.6 all-to-all-done.1
  23.4 21.6 %all-to-all-start = ((bf16[1,2,512,12]{3,1,0,2:T(2,128)(2,1)}), bf16[1,2,512,12]{3,1,0,2:T(2,128)(2,1)S(1)}, u32[]{:S(2)}, u32[]{:S(2)}) async-start(bf16[1,2,512,12]{3,1,0,2:T(2,128)(2,1)} %copy.38), calls=%async_computation | async-start | bytes 524288 | tf_op jit(solution)/shard_map/all_to_all | solution.py:161
  45.0 0.1 reshape.1073
  45.2 16.1 %all-to-all-done = bf16[1,2,512,12]{3,1,0,2:T(2,128)(2,1)S(1)} async-done(((bf16[1,2,512,12]{3,1,0,2:T(2,128)(2,1)}), bf16[1,2,512,12]{3,1,0,2:T(2,128)(2,1)S(1)}, u32[]{:S(2)}, u32[]{:S(2)}) %all-to-all-start) | async-done | bytes 24608 | tf_op jit(solution)/shard_map/all_to_all | solution.py:161
  61.3 0.2 copy.39
  61.4 0.4 reshape.1069
  61.9 0.3 copy.40
  62.2 0.1 reshape.1027
  62.3 0.6 multiply_convert_fusion.7
  63.2 0.8 broadcast_in_dim.40
  63.9 5.5 %all-to-all-start.2 = ((bf16[12,1,2,8,768]{4,3,2,1,0:T(8,128)(2,1)}), bf16[12,1,2,8,768]{4,3,2,1,0:T(8,128)(2,1)S(1)}, u32[]{:S(2)}, u32[]{:S(2)}) async-start(bf16[12,1,2,8,768]{4,3,2,1,0:T(8,128)(2,1)} %broadcast_in_dim.40), calls=%async_computation.2 | async-start | bytes 589824 | tf_op jit(solution)/shard_map/all_to_all | solution.py:33
  69.4 5.9 %all-to-all-done.2 = bf16[12,1,2,8,768]{4,3,2,1,0:T(8,128)(2,1)S(1)} async-done(((bf16[12,1,2,8,768]{4,3,2,1,0:T(8,128)(2,1)}), bf16[12,1,2,8,768]{4,3,2,1,0:T(8,128)(2,1)S(1)}, u32[]{:S(2)}, u32[]{:S(2)}) %all-to-all-start.2) | async-done | bytes 294944 | tf_op jit(solution)/shard_map/all_to_all | solution.py:33
  75.4 72.5 %all-gather.2.cloned.1.call-done = bf16[1,2,512,768]{3,2,1,0:T(8,128)(2,1)} async-done(((bf16[1,2,8,768]{3,2,1,0:T(8,128)(2,1)}), bf16[1,2,512,768]{3,2,1,0:T(8,128)(2,1)}) %all-gather.2.cloned.1.call-update) | async-done | bytes 1572880 | tf_op jit(solution)/shard_map/all_gather | solution.py:168
  147.9 1.6 fusion.3
  149.5 1.5 fusion.2
  151.0 0.4 fusion
  151.4 0.4 fusion.1
  151.9 0.1 multiply_convert_fusion.5
  152.0 0.1 fusion.51
  152.2 4.2 %collective-permute-start = (bf16[1,3,12,4,512]{4,3,2,1,0:T(4,128)(2,1)S(1)}, bf16[1,3,12,4,512]{4,3,2,1,0:T(4,128)(2,1)S(1)}, u32[]{:S(2)}, u32[]{:S(2)}) collective-permute-start(bf16[1,3,12,4,512]{4,3,2,1,0:T(4,128)(2,1)S(1)} %get-tuple-element.27), channel_id=1, source_target_pairs={{0,1},{1,2},{2,3},{3,4},{4,5},{5,6},{6,7},{7,8},{8,9},{9,10},{10,1... | collective-permute-start | bytes 442376 | tf_op jit(solution)/shard_map/ppermute | solution.py:22
  156.4 1.9 collective-permute-start.1
  158.4 0.1 collective-permute-done
  158.5 8.4 %collective-permute-done.1 = bf16[1,3,12,4,512]{4,3,2,1,0:T(4,128)(2,1)S(1)} collective-permute-done((bf16[1,3,12,4,512]{4,3,2,1,0:T(4,128)(2,1)S(1)}, bf16[1,3,12,4,512]{4,3,2,1,0:T(4,128)(2,1)S(1)}, u32[]{:S(2)}, u32[]{:S(2)}) %collective-permute-start.1) | collective-permute-done | bytes 147488 | tf_op jit(solution)/shard_map/ppermute | solution.py:24
  166.9 0.3 maximum_convert_fusion
  167.2 0.1 fusion.47
  167.3 0.1 slice.304
  167.4 0.2 slice_select_fusion.3
  167.6 0.9 fusion.35
  168.6 9.2 %collective-permute-start.2 = (bf16[1,3,96,4]{3,2,1,0:T(8,128)(2,1)S(1)}, bf16[1,3,96,4]{3,2,1,0:T(8,128)(2,1)S(1)}, u32[]{:S(2)}, u32[]{:S(2)}) collective-permute-start(bf16[1,3,96,4]{3,2,1,0:T(8,128)(2,1)S(1)} %get-tuple-element.25), channel_id=1, source_target_pairs={{0,64},{64,128},{128,192},{192,256},{256,320},{320,384},{384,448},... | collective-permute-start | bytes 6920 | tf_op jit(solution)/shard_map/ppermute | solution.py:22
  177.8 1.9 collective-permute-start.3
  179.8 3.2 %collective-permute-done.3 = bf16[1,3,96,4]{3,2,1,0:T(8,128)(2,1)S(1)} collective-permute-done((bf16[1,3,96,4]{3,2,1,0:T(8,128)(2,1)S(1)}, bf16[1,3,96,4]{3,2,1,0:T(8,128)(2,1)S(1)}, u32[]{:S(2)}, u32[]{:S(2)}) %collective-permute-start.3) | collective-permute-done | bytes 2336 | tf_op jit(solution)/shard_map/ppermute | solution.py:24
  182.9 0.2 maximum_convert_fusion.2
  183.2 1.3 slice_add_fusion.8
  184.5 0.2 multiply_convert_fusion.3
  184.8 0.1 fusion.49
  184.9 4.4 %collective-permute-start.4 = (bf16[1,3,12,4,512]{4,3,2,1,0:T(4,128)(2,1)S(1)}, bf16[1,3,12,4,512]{4,3,2,1,0:T(4,128)(2,1)S(1)}, u32[]{:S(2)}, u32[]{:S(2)}) collective-permute-start(bf16[1,3,12,4,512]{4,3,2,1,0:T(4,128)(2,1)S(1)} %get-tuple-element.23), channel_id=1, source_target_pairs={{0,1},{1,2},{2,3},{3,4},{4,5},{5,6},{6,7},{7,8},{8,9},{9,10},{10,1... | collective-permute-start | bytes 442376 | tf_op jit(solution)/shard_map/ppermute | solution.py:22
  189.3 1.9 collective-permute-start.5
  191.3 1.7 collective-permute-done.4
  193.0 8.0 %collective-permute-done.5 = bf16[1,3,12,4,512]{4,3,2,1,0:T(4,128)(2,1)S(1)} collective-permute-done((bf16[1,3,12,4,512]{4,3,2,1,0:T(4,128)(2,1)S(1)}, bf16[1,3,12,4,512]{4,3,2,1,0:T(4,128)(2,1)S(1)}, u32[]{:S(2)}, u32[]{:S(2)}) %collective-permute-start.5) | collective-permute-done | bytes 147488 | tf_op jit(solution)/shard_map/ppermute | solution.py:24
  201.0 0.3 maximum_convert_fusion.1
  201.3 0.1 fusion.46
  201.4 0.1 slice.337
  201.5 0.2 slice_select_fusion.1
  201.7 0.9 fusion.36
  202.8 4.9 %collective-permute-start.6 = (bf16[1,3,96,4]{3,2,1,0:T(8,128)(2,1)S(1)}, bf16[1,3,96,4]{3,2,1,0:T(8,128)(2,1)S(1)}, u32[]{:S(2)}, u32[]{:S(2)}) collective-permute-start(bf16[1,3,96,4]{3,2,1,0:T(8,128)(2,1)S(1)} %get-tuple-element.21), channel_id=1, source_target_pairs={{0,64},{64,128},{128,192},{192,256},{256,320},{320,384},{384,448},... | collective-permute-start | bytes 6920 | tf_op jit(solution)/shard_map/ppermute | solution.py:22
  207.7 3.0 %collective-permute-start.7 = (bf16[1,3,96,4]{3,2,1,0:T(8,128)(2,1)S(1)}, bf16[1,3,96,4]{3,2,1,0:T(8,128)(2,1)S(1)}, u32[]{:S(2)}, u32[]{:S(2)}) collective-permute-start(bf16[1,3,96,4]{3,2,1,0:T(8,128)(2,1)S(1)} %get-tuple-element.22), channel_id=1, source_target_pairs={{64,0},{128,64},{192,128},{256,192},{320,256},{384,320},{448,384},... | collective-permute-start | bytes 6920 | tf_op jit(solution)/shard_map/ppermute | solution.py:24
  210.7 0.7 multiply_convert_fusion
  211.4 1.4 collective-permute-done.7
  212.8 0.2 maximum_convert_fusion.3
  213.0 1.3 slice_add_fusion
  214.3 0.1 subtract_convert_fusion.1
  214.4 0.7 pad_maximum_fusion.7
  (37 shorter events, 1.1 us)
Async XLA Ops:
  7.2 0.7 copy-start
  7.2 12.8 %copy-start.1 = (bf16[1,2,96,512]{3,2,1,0:T(8,128)(2,1)S(1)}, bf16[1,2,96,512]{3,2,1,0:T(8,128)(2,1)}, u32[]{:S(2)}) copy-start(bf16[1,2,96,512]{3,2,1,0:T(8,128)(2,1)} %param.2) | copy-start | bytes 589828
  11.4 12.0 %all-to-all-start.1 = ((bf16[12,2,512]{2,1,0:T(2,128)(2,1)}), bf16[12,2,512]{2,1,0:T(2,128)(2,1)S(1)}, u32[]{:S(2)}, u32[]{:S(2)}) async-start(bf16[12,2,512]{2,1,0:T(2,128)(2,1)} %reshape.1072), calls=%async_computation.1 | async-start | bytes 49152 | tf_op jit(solution)/shard_map/all_to_all | solution.py:165
  23.4 37.9 %all-to-all-start = ((bf16[1,2,512,12]{3,1,0,2:T(2,128)(2,1)}), bf16[1,2,512,12]{3,1,0,2:T(2,128)(2,1)S(1)}, u32[]{:S(2)}, u32[]{:S(2)}) async-start(bf16[1,2,512,12]{3,1,0,2:T(2,128)(2,1)} %copy.38), calls=%async_computation | async-start | bytes 524288 | tf_op jit(solution)/shard_map/all_to_all | solution.py:161
  44.9 103.0 %all-gather.2.cloned.1.call-start = ((), (), s32[]{:S(2)}) async-start(), calls=%async_computation.3 | async-start | bytes 1597440 | tf_op jit(solution)/shard_map/all_gather | solution.py:168
  63.9 11.5 %all-to-all-start.2 = ((bf16[12,1,2,8,768]{4,3,2,1,0:T(8,128)(2,1)}), bf16[12,1,2,8,768]{4,3,2,1,0:T(8,128)(2,1)S(1)}, u32[]{:S(2)}, u32[]{:S(2)}) async-start(bf16[12,1,2,8,768]{4,3,2,1,0:T(8,128)(2,1)} %broadcast_in_dim.40), calls=%async_computation.2 | async-start | bytes 589824 | tf_op jit(solution)/shard_map/all_to_all | solution.py:33
  147.9 3.1 %copy-start.2 = (bf16[1,2,512,768]{3,2,1,0:T(8,128)(2,1)S(1)}, bf16[1,2,512,768]{3,2,1,0:T(8,128)(2,1)}, u32[]{:S(2)}) copy-start(bf16[1,2,512,768]{3,2,1,0:T(8,128)(2,1)} %all-gather.2.cloned.1.call-done) | copy-start | bytes 4718596
  152.2 6.3 %collective-permute-start = (bf16[1,3,12,4,512]{4,3,2,1,0:T(4,128)(2,1)S(1)}, bf16[1,3,12,4,512]{4,3,2,1,0:T(4,128)(2,1)S(1)}, u32[]{:S(2)}, u32[]{:S(2)}) collective-permute-start(bf16[1,3,12,4,512]{4,3,2,1,0:T(4,128)(2,1)S(1)} %get-tuple-element.27), channel_id=1, source_target_pairs={{0,1},{1,2},{2,3},{3,4},{4,5},{5,6},{6,7},{7,8},{8,9},{9,10},{10,1... | collective-permute-start | bytes 442376 | tf_op jit(solution)/shard_map/ppermute | solution.py:22
  156.4 10.5 %collective-permute-start.1 = (bf16[1,3,12,4,512]{4,3,2,1,0:T(4,128)(2,1)S(1)}, bf16[1,3,12,4,512]{4,3,2,1,0:T(4,128)(2,1)S(1)}, u32[]{:S(2)}, u32[]{:S(2)}) collective-permute-start(bf16[1,3,12,4,512]{4,3,2,1,0:T(4,128)(2,1)S(1)} %get-tuple-element.28), channel_id=1, source_target_pairs={{1,0},{2,1},{3,2},{4,3},{5,4},{6,5},{7,6},{8,7},{9,8},{10,9},{11,1... | collective-permute-start | bytes 442376 | tf_op jit(solution)/shard_map/ppermute | solution.py:24
  168.6 11.2 %collective-permute-start.2 = (bf16[1,3,96,4]{3,2,1,0:T(8,128)(2,1)S(1)}, bf16[1,3,96,4]{3,2,1,0:T(8,128)(2,1)S(1)}, u32[]{:S(2)}, u32[]{:S(2)}) collective-permute-start(bf16[1,3,96,4]{3,2,1,0:T(8,128)(2,1)S(1)} %get-tuple-element.25), channel_id=1, source_target_pairs={{0,64},{64,128},{128,192},{192,256},{256,320},{320,384},{384,448},... | collective-permute-start | bytes 6920 | tf_op jit(solution)/shard_map/ppermute | solution.py:22
  177.8 5.1 %collective-permute-start.3 = (bf16[1,3,96,4]{3,2,1,0:T(8,128)(2,1)S(1)}, bf16[1,3,96,4]{3,2,1,0:T(8,128)(2,1)S(1)}, u32[]{:S(2)}, u32[]{:S(2)}) collective-permute-start(bf16[1,3,96,4]{3,2,1,0:T(8,128)(2,1)S(1)} %get-tuple-element.26), channel_id=1, source_target_pairs={{64,0},{128,64},{192,128},{256,192},{320,256},{384,320},{448,384},... | collective-permute-start | bytes 6920 | tf_op jit(solution)/shard_map/ppermute | solution.py:24
  184.9 8.1 %collective-permute-start.4 = (bf16[1,3,12,4,512]{4,3,2,1,0:T(4,128)(2,1)S(1)}, bf16[1,3,12,4,512]{4,3,2,1,0:T(4,128)(2,1)S(1)}, u32[]{:S(2)}, u32[]{:S(2)}) collective-permute-start(bf16[1,3,12,4,512]{4,3,2,1,0:T(4,128)(2,1)S(1)} %get-tuple-element.23), channel_id=1, source_target_pairs={{0,1},{1,2},{2,3},{3,4},{4,5},{5,6},{6,7},{7,8},{8,9},{9,10},{10,1... | collective-permute-start | bytes 442376 | tf_op jit(solution)/shard_map/ppermute | solution.py:22
  189.3 11.7 %collective-permute-start.5 = (bf16[1,3,12,4,512]{4,3,2,1,0:T(4,128)(2,1)S(1)}, bf16[1,3,12,4,512]{4,3,2,1,0:T(4,128)(2,1)S(1)}, u32[]{:S(2)}, u32[]{:S(2)}) collective-permute-start(bf16[1,3,12,4,512]{4,3,2,1,0:T(4,128)(2,1)S(1)} %get-tuple-element.24), channel_id=1, source_target_pairs={{1,0},{2,1},{3,2},{4,3},{5,4},{6,5},{7,6},{8,7},{9,8},{10,9},{11,1... | collective-permute-start | bytes 442376 | tf_op jit(solution)/shard_map/ppermute | solution.py:24
  202.8 8.6 %collective-permute-start.6 = (bf16[1,3,96,4]{3,2,1,0:T(8,128)(2,1)S(1)}, bf16[1,3,96,4]{3,2,1,0:T(8,128)(2,1)S(1)}, u32[]{:S(2)}, u32[]{:S(2)}) collective-permute-start(bf16[1,3,96,4]{3,2,1,0:T(8,128)(2,1)S(1)} %get-tuple-element.21), channel_id=1, source_target_pairs={{0,64},{64,128},{128,192},{192,256},{256,320},{320,384},{384,448},... | collective-permute-start | bytes 6920 | tf_op jit(solution)/shard_map/ppermute | solution.py:22
  207.7 5.1 %collective-permute-start.7 = (bf16[1,3,96,4]{3,2,1,0:T(8,128)(2,1)S(1)}, bf16[1,3,96,4]{3,2,1,0:T(8,128)(2,1)S(1)}, u32[]{:S(2)}, u32[]{:S(2)}) collective-permute-start(bf16[1,3,96,4]{3,2,1,0:T(8,128)(2,1)S(1)} %get-tuple-element.22), channel_id=1, source_target_pairs={{64,0},{128,64},{192,128},{256,192},{320,256},{384,320},{448,384},... | collective-permute-start | bytes 6920 | tf_op jit(solution)/shard_map/ppermute | solution.py:24
Sparse Core Ops, SparseCore 0:
  63.1 84.7 all-gather.1
where the time goes:
time: 223 us; the launch traced here: 222 us
  waiting for transfers between devices  119 us (53%)
  starting transfers between devices  66.5 us (30%)
  between operations  14.5 us (7%)
  local copies, waits for them, and re-layouts  9.32 us (4%)
  other arithmetic  8.95 us (4%)
  matrix products  3.85 us (2%)
    all_gather x1, waiting for transfers between devices, shards(): lax.all_gather(owned_rows, 'rcv', axis=2, tiled=True)  72.5 us
    ppermute x4, starting transfers between devices, extended(): lax.ppermute(tail, axis, [(i, (i + 1) % count) for i in range(ends)])  22.8 us
    all_to_all x1, starting transfers between devices, shards(): lax.all_to_all(col_piece, 'rcv', split_axis=2, concat_axis=3, tiled=True)  21.6 us
    ppermute x4, waiting for transfers between devices, extended(): lax.ppermute(head, axis, [((i + 1) % count, i) for i in range(ends)])  21 us
    all_to_all x1, waiting for transfers between devices, shards(): lax.all_to_all(col_piece, 'rcv', split_axis=2, concat_axis=3, tiled=True)  16.1 us
    ppermute x4, starting transfers between devices, extended(): lax.ppermute(head, axis, [((i + 1) % count, i) for i in range(ends)])  8.71 us
    all_to_all x1, starting transfers between devices, shards(): lax.all_to_all(row_piece, 'src', split_axis=2, concat_axis=3, tiled=True)  7.87 us
    all_to_all x1, waiting for transfers between devices, copy_for_each(): return lax.all_to_all(copies, axis, split_axis=0, concat_axis=0, tiled=True)  5.93 us
  transfers between devices with their start and end apart: 12, of which 10 were waited for; matrix products, arithmetic and copies ran while one was open for 2% of the time, Pallas kernels for 0%

commit v1 on v0

v1 whole, which is shorter than its diff:
```python
import jax
import jax.numpy as jnp
from jax import lax
from jax.experimental import pallas as pl
from jax.experimental.pallas import tpu as pltpu
from jax.sharding import PartitionSpec as P

NZ, NY, NC = 4, 8, 2
NP = NY * NC
NA = 12
TILES = 3 * NZ
EXT = 640
STRIDE = 8
REACH = 4
EPS = 1e-6
F32, BF16 = jnp.float32, jnp.bfloat16


def vmem(count):
    return [pl.BlockSpec(memory_space=pltpu.VMEM)] * count


def smem(count):
    return [pl.BlockSpec(memory_space=pltpu.SMEM)] * count


def pick_kernel(pos, panel, rec, to_rcv, to_src):
    src, rcv = pos[0], pos[1]
    lane = lax.broadcasted_iota(jnp.int32, (1, 128), 1)
    slot = lane % 8
    key_part, key_pos = slot // 4, 16 * (slot % 4) + lane // 8
    offset = jnp.zeros((1, 128), jnp.int32)
    for g in range(64):
        offset = jnp.where(key_pos == g, panel[64 * src + g], offset)
    key_row = STRIDE * key_pos + offset
    rows = lax.broadcasted_iota(jnp.int32, (512, 128), 0)
    total = jnp.zeros((96, 128), F32)
    for part in range(2):
        chosen = ((rows == key_row) & (key_part == part)).astype(F32).astype(BF16)
        total += jnp.dot(rec[part], chosen, preferred_element_type=F32)
    to_src[...] = total.astype(BF16).reshape(NA, 8, 128)
    run, run_part, run_z = (lane % 32) // 2, lane % 2, lane // 32
    offset = jnp.zeros((1, 128), jnp.int32)
    for a in range(NA):
        offset = jnp.where(run == a, panel[64 * a + rcv], offset)
    col = jnp.where(run < NA, STRIDE * run + offset, -1)
    rows = lax.broadcasted_iota(jnp.int32, (96, 128), 0)
    total = jnp.zeros((128, 128), F32)
    for z in range(NZ):
        for part in range(2):
            chosen = ((rows == col) & (run_part == part) & (run_z == z)).astype(F32).astype(BF16)
            total += lax.dot_general(
                rec[part, :, 128 * z : 128 * z + 128],
                chosen,
                (((0,), (0,)), ((), ())),
                preferred_element_type=F32,
            )
    to_rcv[...] = total.astype(BF16).reshape(NP, 8, 128)


def order_kernel(from_rcv, from_src, out):
    lane = lax.broadcasted_iota(jnp.int32, (8, 128), 1)
    rcv_tiles = [from_rcv[p].astype(F32) for p in range(NP)]
    tiles = []
    for z in range(NZ):
        for third in range(3):
            acc = jnp.zeros((8, 128), F32)
            for p in range(NP):
                shift = (8 * p - 32 * z - 8 * third) % 128
                moved = pltpu.roll(rcv_tiles[p], shift, 1) if shift else rcv_tiles[p]
                acc = jnp.where(lane // 8 == p, moved, acc)
            tiles.append(acc)
    src_tiles = [from_src[a].astype(F32) for a in range(NA)]
    for z in range(NZ):
        for third in range(3):
            acc = jnp.zeros((8, 128), F32)
            for j in range(8):
                shift = (j - (4 * (j % 2) + z)) % 128
                tile = src_tiles[4 * third + j // 2]
                moved = pltpu.roll(tile, shift, 1) if shift else tile
                acc = jnp.where(lane % 8 == j, moved, acc)
            tiles.append(acc)
    for n, tile in enumerate(tiles):
        tile = tile.astype(BF16)
        for z in range(NZ):
            out[z, n] = tile


def average_kernel(pos, pieces, rows, own):
    for z in range(NZ):
        for tile in range(TILES):
            front = pieces[tile // 3, 3 * z + tile % 3].astype(F32)
            behind = pieces[z, TILES + tile].astype(F32)
            rows[z, tile] = ((front + behind) * 0.5).astype(BF16)
    own[...] = rows[pos[1] // NP]


def windows_rows(x, count):
    two = x[:-1] + x[1:]
    four = two[:-2] + two[2:]
    eight = four[:-4] + four[4:]
    return eight[:count] + x[8 : 8 + count]


def windows_lanes(x):
    two = x + pltpu.roll(x, EXT - 1, 1)
    four = two + pltpu.roll(two, EXT - 2, 1)
    eight = four + pltpu.roll(four, EXT - 4, 1)
    return pltpu.roll(eight + pltpu.roll(x, EXT - 8, 1), 4, 1)


def final_kernel(pos, rec, rec_lo, rec_hi, sr, sr_lo, sr_hi, ss, sp, row_hi, row_lo, prim, mult, a_re, a_im, b_rows, pred):
    rcv = pos[1]
    core = rcv % 2
    first, last = (rcv == 0).astype(jnp.int32), (rcv == NZ * NP - 1).astype(jnp.int32)
    lane = lax.broadcasted_iota(jnp.int32, (24, 128), 1)
    even = lane % 2 == 0

    def spread(a, _):
        lo, hi = jnp.maximum(a - first, 0), jnp.minimum(a + last, NA - 1)
        keep_lo = (a - first >= 0).astype(F32)
        keep_hi = (a + last <= NA - 1).astype(F32)
        for t in range(TILES):
            x = jnp.concatenate(
                [sr_lo[lo, t].astype(F32) * keep_lo, sr[a, t].astype(F32), sr_hi[hi, t].astype(F32) * keep_hi], axis=0
            )
            a_re[a, :, 128 * t : 128 * t + 128] = jnp.where(even, x, -x)
            a_im[a, :, 128 * t : 128 * t + 128] = jnp.where(even, pltpu.roll(x, 127, 1), pltpu.roll(x, 1, 1))
        return 0

    lax.fori_loop(0, NA, spread, 0)

    def gather(z, _):
        for t in range(TILES):
            mine, theirs = ss[:, z, t].astype(F32), sp[:, z, t].astype(F32)
            zero = jnp.where(core == 0, mine, theirs)
            one = jnp.where(core == 0, theirs, mine)
            x = jnp.stack([zero, one], axis=1).reshape(128, 128)
            b_rows[z, :, 128 * t : 128 * t + 128] = x.astype(BF16)
        return 0

    lax.fori_loop(0, NZ, gather, 0)
    for t in range(TILES):
        x = jnp.concatenate([row_hi[t].astype(F32), jnp.zeros((112, 128), F32), row_lo[t].astype(F32)], axis=0)
        b_rows[NZ, :, 128 * t : 128 * t + 128] = x.astype(BF16)
    left_re = a_re[...].reshape(24 * NA, 128 * TILES).astype(BF16)
    left_im = a_im[...].reshape(24 * NA, 128 * TILES).astype(BF16)
    for n in range(NZ + 1):
        right = b_rows[n]
        for part, left in enumerate((left_re, left_im)):
            value = lax.dot_general(left, right, (((1,), (1,)), ((), ())), preferred_element_type=F32)
            pred[part, :, :, 128 * n : 128 * n + 128] = value.reshape(NA, 24, 128)

    def sweep(a, _):
        lo, hi = jnp.maximum(a - first, 0), jnp.minimum(a + last, NA - 1)
        keep_lo = (a - first >= 0).astype(F32)
        keep_hi = (a + last <= NA - 1).astype(F32)
        data, guess = [], []
        for part in range(2):
            data.append(
                jnp.concatenate(
                    [rec_lo[part, lo].astype(F32) * keep_lo, rec[part, a].astype(F32), rec_hi[part, hi].astype(F32) * keep_hi],
                    axis=0,
                )
            )
            full = pred[part, a]
            mult[part, a] = (full[8:16, :512] * (768.0 ** -0.5)).astype(BF16)
            guess.append(full.astype(BF16).astype(F32))
        dr, di = data
        pr, pi = guess
        terms = [pr * dr + pi * di, pr * di - pi * dr, pr * pr + pi * pi]
        weight = 1.5 - jnp.tanh(dr * dr + di * di)
        num_re, num_im, den = [windows_lanes(windows_rows(weight * q, 16)) for q in terms]
        den = den + EPS
        gain_re, gain_im = num_re / den, num_im / den
        dr, di, pr, pi = [v[4:20] for v in (dr, di, pr, pi)]
        er = dr - (gain_re * pr - gain_im * pi)
        ei = di - (gain_re * pi + gain_im * pr)
        weight = 1.5 - jnp.tanh(er * er + ei * ei)
        num_re, num_im, den = [windows_lanes(windows_rows(weight * q[4:20], 8)) for q in terms]
        den = den + EPS
        gain_re, gain_im = num_re / den, num_im / den
        dr, di, pr, pi = [v[4:12] for v in (dr, di, pr, pi)]
        prim[0, a] = (dr - (gain_re * pr - gain_im * pi))[:, :512].astype(BF16)
        prim[1, a] = (di - (gain_re * pi + gain_im * pr))[:, :512].astype(BF16)
        return 0

    lax.fori_loop(0, NA, sweep, 0)


def shape(*dims):
    return jax.ShapeDtypeStruct(dims, BF16)


def ring(count, step, closed):
    return [(n, (n + step) % count) for n in range(count) if closed or 0 <= n + step < count]


def shards(record, panel_offset):
    src_count, rcv_count = lax.axis_size("src"), lax.axis_size("rcv")
    src, rcv = lax.axis_index("src"), lax.axis_index("rcv")
    pos = jnp.stack([src, rcv]).astype(jnp.int32)
    rec = record[0]
    plane = [[z * NP + p for p in range(NP)] for z in range(NZ)]
    column = [[z * NP + p for z in range(NZ)] for p in range(NP)]
    line = [[z * NP + y * NC + c for y in range(NY)] for z in range(NZ) for c in range(NC)]
    swap = [(n, n ^ 1) for n in range(rcv_count)]

    def exchange(x, axis, groups=None):
        return lax.all_to_all(x, axis, split_axis=0, concat_axis=0, tiled=True, axis_index_groups=groups)

    def copies(x, count, axis, groups=None):
        return exchange(jnp.broadcast_to(x, (count, *x.shape)), axis, groups)

    next_src = lax.ppermute(rec[:, :, :128], "src", ring(src_count, -1, False))
    last_src = lax.ppermute(rec[:, :, 384:], "src", ring(src_count, 1, False))
    lane = lax.broadcasted_iota(jnp.int32, (1, 1, 128), 2)
    rim = jnp.where(lane < 8, next_src, jnp.where(lane >= 120, last_src, jnp.zeros_like(last_src)))
    wide = jnp.concatenate([rec, rim], axis=2).reshape(2, NA, 8, EXT)
    wide_lo = lax.ppermute(wide, "rcv", ring(rcv_count, 1, True))
    wide_hi = lax.ppermute(wide, "rcv", ring(rcv_count, -1, True))

    to_rcv, to_src = pl.pallas_call(
        pick_kernel,
        out_shape=(shape(NP, 8, 128), shape(NA, 8, 128)),
        in_specs=smem(2) + vmem(1),
        out_specs=vmem(2),
    )(pos, panel_offset, rec)
    from_src = exchange(to_src, "src")
    from_rcv = exchange(to_rcv, "rcv", plane)
    message = pl.pallas_call(
        order_kernel, out_shape=shape(NZ, 2 * TILES, 8, 128), in_specs=vmem(2), out_specs=vmem(1)[0]
    )(from_rcv, from_src)
    pieces = exchange(message, "rcv", column)
    rows, own = pl.pallas_call(
        average_kernel,
        out_shape=(shape(NZ, TILES, 8, 128), shape(TILES, 8, 128)),
        in_specs=smem(1) + vmem(1),
        out_specs=vmem(2),
    )(pos, pieces)
    sr = copies(own, src_count, "src")
    ss = copies(rows, NY, "rcv", line)
    sr_lo = lax.ppermute(sr, "rcv", ring(rcv_count, 1, True))
    sr_hi = lax.ppermute(sr, "rcv", ring(rcv_count, -1, True))
    sp = lax.ppermute(ss, "rcv", swap)
    even_core = rcv % 2 == 0
    row_first = jnp.where(even_core, ss[0, 0], sp[0, 0])
    row_last = jnp.where(even_core, sp[NY - 1, NZ - 1], ss[NY - 1, NZ - 1])
    row_hi = lax.ppermute(row_first, "src", ring(src_count, -1, False))
    row_lo = lax.ppermute(row_last, "src", ring(src_count, 1, False))
    prim, mult = pl.pallas_call(
        final_kernel,
        out_shape=(shape(2, NA, 8, 512), shape(2, NA, 8, 512)),
        in_specs=smem(1) + vmem(10),
        out_specs=vmem(2),
        scratch_shapes=[
            pltpu.VMEM((NA, 24, 128 * TILES), F32),
            pltpu.VMEM((NA, 24, 128 * TILES), F32),
            pltpu.VMEM((NZ + 1, 128, 128 * TILES), BF16),
            pltpu.VMEM((2, NA, 24, EXT), F32),
        ],
    )(pos, wide, wide_lo, wide_hi, sr, sr_lo, sr_hi, ss, sp, row_hi, row_lo)
    return prim.reshape(record.shape), mult.reshape(record.shape)


def solution(mesh):
    in_specs = (P(None, None, "rcv", "src"), P())
    out_specs = (P(None, None, "rcv", "src"), P(None, None, "rcv", "src"))
    return jax.shard_map(shards, mesh=mesh, in_specs=in_specs, out_specs=out_specs, check_vma=False)
```

time: 223 us -> 153 us (0.69)
  waiting for transfers between devices: 119 us -> 4.14 us
  blocking collectives: 0 us -> 68.8 us
  Pallas kernels: 0 us -> 21.4 us
  between operations: 14.5 us -> 0.96 us
  starting transfers between devices: 66.5 us -> 53.9 us
  other arithmetic: 8.95 us -> 0.71 us
  local copies, waits for them, and re-layouts: 9.32 us -> 2.51 us
  matrix products: 3.85 us -> 0 us
    all_gather x1 -> x0, waiting for transfers between devices: 72.5 us -> none  [shards(): lax.all_gather(owned_rows, 'rcv', axis=2, tiled=True)]
    all_to_all x0 -> x4, blocking collectives: none -> 68.8 us  [exchange(): lax.all_to_all(x, axis, split_axis=0, concat_axis=0, tiled=True, axis_ind...]
    all_to_all x3 -> x1, starting transfers between devices: 34.9 us -> 4.61 us  [exchange(): lax.all_to_all(x, axis, split_axis=0, concat_axis=0, tiled=True, axis_ind...]
    all_to_all x3 -> x1, waiting for transfers between devices: 23.6 us -> 0.01 us  [exchange(): lax.all_to_all(x, axis, split_axis=0, concat_axis=0, tiled=True, axis_ind...]
    pallas_call x0 -> x4, Pallas kernels: none -> 21.4 us  [the longest x1 16.3 us: shards(): pl.pallas_call(final_kernel, out_shape=(shape(2, NA, 8, 512), shape(2, NA...]
    ppermute x8 -> x9, waiting for transfers between devices: 22.8 us -> 4.14 us  [the longest x1 2.54 us: shards(): row_hi = lax.ppermute(row_first, 'src', ring(src_count, -1, False))]
    ppermute x8 -> x9, starting transfers between devices: 31.5 us -> 49.3 us  [the longest x1 12.3 us: shards(): sr_lo = lax.ppermute(sr, 'rcv', ring(rcv_count, 1, True))]
    convert_element_type x13 -> x0, other arithmetic: 4.3 us -> none  [the longest x2 1.86 us: neighbour_sum(): recv_total.astype(jnp.bfloat16)]
  transfers between devices with their start and end apart: 12 -> 10, of which waited for: 10 -> 3; matrix products, arithmetic and copies ran while one was open for 2% -> 0% of each run, Pallas kernels for 0% -> 0%
where the time goes in v1:
time: 153 us; the launch traced here: 152 us
  blocking collectives  68.8 us (45%)
  starting transfers between devices  53.9 us (35%)
  Pallas kernels  21.4 us (14%)
  waiting for transfers between devices  4.14 us (3%)
  local copies, waits for them, and re-layouts  2.51 us (2%)
    all_to_all x4, blocking collectives, exchange(): lax.all_to_all(x, axis, split_axis=0, concat_axis=0, tiled=True, axis_ind...  68.8 us
    pallas_call x1, Pallas kernels, shards(): pl.pallas_call(final_kernel, out_shape=(shape(2, NA, 8, 512), shape(2, NA...  16.3 us
    ppermute x1, starting transfers between devices, shards(): sr_lo = lax.ppermute(sr, 'rcv', ring(rcv_count, 1, True))  12.3 us
    ppermute x1, starting transfers between devices, shards(): sp = lax.ppermute(ss, 'rcv', swap)  7.67 us
    ppermute x1, starting transfers between devices, shards(): wide_lo = lax.ppermute(wide, 'rcv', ring(rcv_count, 1, True))  7.55 us
    ppermute x1, starting transfers between devices, shards(): row_hi = lax.ppermute(row_first, 'src', ring(src_count, -1, False))  6.61 us
    all_to_all x1, starting transfers between devices, exchange(): lax.all_to_all(x, axis, split_axis=0, concat_axis=0, tiled=True, axis_ind...  4.61 us
    ppermute x1, starting transfers between devices, shards(): next_src = lax.ppermute(rec[:, :, :128], 'src', ring(src_count, -1, False))  3.98 us
  transfers between devices with their start and end apart: 10, of which 3 were waited for; matrix products, arithmetic and copies ran while one was open for 0% of the time, Pallas kernels for 0%

profile of v1, /device:TPU:61, one launch (start us, length us, event | category | flops | bytes accessed | tf_op | source)
XLA Modules:
  0.0 152.4 jit_solution(14525936053659730058)
XLA Ops:
  0.6 0.7 pad_add_fusion.pos
  1.3 1.9 %shard_map.41 = (bf16[16,8,128]{2,1,0:T(8,128)(2,1)}, bf16[12,8,128]{2,1,0:T(8,128)(2,1)}) custom-call(s32[2]{0:T(128)} %pad_add_fusion.pos, s32[768]{0:T(1024)} %panel.1, bf16[2,96,512]{2,1,0:T(8,128)(2,1)} %bitcast.12), custom_call_target="tpu_custom_call" | custom-call | tf_op jit(solution)/shard_map/pallas_call | solution.py:223
  3.2 0.0 copy-start.12
  3.2 12.5 %all_to_all.25.from_rcv = bf16[16,8,128]{2,1,0:T(8,128)(2,1)} all-to-all(bf16[16,8,128]{2,1,0:T(8,128)(2,1)} %get-tuple-element.8), channel_id=1, replica_groups={{0,1,2,3,4,5,6,7,8,9,10,11,12,13,14,15},{16,17,18,19,20,21,22,23,24,25,..., dimensions={0} | all-to-all | bytes 65536 | tf_op jit(solution)/shard_map/all_to_all | solution.py:210
  15.7 0.0 copy-done.12
  15.7 13.3 %all_to_all.26.from_src = bf16[12,8,128]{2,1,0:T(8,128)(2,1)} all-to-all(bf16[12,8,128]{2,1,0:T(8,128)(2,1)S(1)} %copy-done.12), channel_id=1, replica_groups=mesh['src'=12,'rcv'=64] {'src'}, dimensions={0} | all-to-all | bytes 49152 | tf_op jit(solution)/shard_map/all_to_all | solution.py:210
  29.0 1.6 %shard_map.42 = bf16[4,24,8,128]{3,2,1,0:T(8,128)(2,1)} custom-call(bf16[16,8,128]{2,1,0:T(8,128)(2,1)} %all_to_all.25.from_rcv, bf16[12,8,128]{2,1,0:T(8,128)(2,1)} %all_to_all.26.from_src), custom_call_target="tpu_custom_call" | custom-call | tf_op jit(solution)/shard_map/pallas_call | solution.py:231
  30.6 23.5 %all_to_all.27.pieces = bf16[4,24,8,128]{3,2,1,0:T(8,128)(2,1)} all-to-all(bf16[4,24,8,128]{3,2,1,0:T(8,128)(2,1)} %shard_map.42), channel_id=1, replica_groups={{0,16,32,48},{1,17,33,49},{2,18,34,50},{3,19,35,51},{4,20,36,52},{5,21,..., dimensions={0} | all-to-all | bytes 393216 | tf_op jit(solution)/shard_map/all_to_all | solution.py:210
  54.1 1.6 %shard_map.43 = (bf16[4,12,8,128]{3,2,1,0:T(8,128)(2,1)}, bf16[12,8,128]{2,1,0:T(8,128)(2,1)}) custom-call(s32[2]{0:T(128)} %pad_add_fusion.pos, bf16[4,24,8,128]{3,2,1,0:T(8,128)(2,1)} %all_to_all.27.pieces), custom_call_target="tpu_custom_call" | custom-call | tf_op jit(solution)/shard_map/pallas_call | solution.py:235
  55.7 1.0 broadcast_in_dim.26
  56.7 0.0 copy-start.11
  56.7 19.5 %all_to_all.28.ss = bf16[8,4,12,8,128]{4,3,2,1,0:T(8,128)(2,1)S(1)} all-to-all(bf16[8,4,12,8,128]{4,3,2,1,0:T(8,128)(2,1)S(1)} %broadcast_in_dim.26), channel_id=1, replica_groups={{0,2,4,6,8,10,12,14},{1,3,5,7,9,11,13,15},{16,18,20,22,24,26,28,30},{17..., dimensions={0} | all-to-all | bytes 1572864 | tf_op jit(solution)/shard_map/all_to_all | solution.py:210
  76.3 0.0 copy-start
  76.3 0.0 copy-done.11
  76.3 0.8 broadcast_in_dim.25
  77.1 0.0 copy-start.1
  77.1 4.6 %all-to-all-start.3 = ((bf16[12,12,8,128]{3,2,1,0:T(8,128)(2,1)}), bf16[12,12,8,128]{3,2,1,0:T(8,128)(2,1)S(1)}, u32[]{:S(2)}, u32[]{:S(2)}) async-start(bf16[12,12,8,128]{3,2,1,0:T(8,128)(2,1)} %broadcast_in_dim.25), calls=%async_computation.3 | async-start | bytes 589824 | tf_op jit(solution)/shard_map/all_to_all | solution.py:210
  81.7 7.7 %collective-permute-start.6 = (bf16[8,4,12,8,128]{4,3,2,1,0:T(8,128)(2,1)S(1)}, bf16[8,4,12,8,128]{4,3,2,1,0:T(8,128)(2,1)S(1)}, u32[]{:S(2)}, u32[]{:S(2)}) collective-permute-start(bf16[8,4,12,8,128]{4,3,2,1,0:T(8,128)(2,1)S(1)} %all_to_all.28.ss), channel_id=1, source_target_pairs={{0,1},{1,0},{2,3},{3,2},{4,5},{5,4},{6,7},{7,6},{8,9},{9,8},{10,11... | collective-permute-start | bytes 2359304 | tf_op jit(solution)/shard_map/ppermute | solution.py:245
  89.4 0.0 copy-done.1
  89.5 3.1 %collective-permute-start.1 = (bf16[2,96,128]{2,1,0:T(8,128)(2,1)S(1)}, bf16[2,96,128]{2,1,0:T(8,128)(2,1)S(1)}, u32[]{:S(2)}, u32[]{:S(2)}) collective-permute-start(bf16[2,96,128]{2,1,0:T(8,128)(2,1)S(1)} %get-tuple-element.16), channel_id=1, source_target_pairs={{0,64},{64,128},{128,192},{192,256},{256,320},{320,384},{384,448},... | collective-permute-start | bytes 147464 | tf_op jit(solution)/shard_map/ppermute | solution.py:216
  92.6 4.0 %collective-permute-start = (bf16[2,96,128]{2,1,0:T(8,128)(2,1)S(1)}, bf16[2,96,128]{2,1,0:T(8,128)(2,1)S(1)}, u32[]{:S(2)}, u32[]{:S(2)}) collective-permute-start(bf16[2,96,128]{2,1,0:T(8,128)(2,1)S(1)} %get-tuple-element.17), channel_id=1, source_target_pairs={{64,0},{128,64},{192,128},{256,192},{320,256},{384,320},{448,384},... | collective-permute-start | bytes 147464 | tf_op jit(solution)/shard_map/ppermute | solution.py:215
  96.6 0.0 collective-permute-done.1
  96.6 1.1 collective-permute-done
  97.7 0.0 all-to-all-done.3.sr
  97.7 0.0 copy-start.2
  97.7 3.1 %collective-permute-start.5 = (bf16[12,12,8,128]{3,2,1,0:T(8,128)(2,1)S(1)}, bf16[12,12,8,128]{3,2,1,0:T(8,128)(2,1)S(1)}, u32[]{:S(2)}, u32[]{:S(2)}) collective-permute-start(bf16[12,12,8,128]{3,2,1,0:T(8,128)(2,1)S(1)} %all-to-all-done.3.sr), channel_id=1, source_target_pairs={{0,63},{1,0},{2,1},{3,2},{4,3},{5,4},{6,5},{7,6},{8,7},{9,8},{10,9... | collective-permute-start | bytes 884744 | tf_op jit(solution)/shard_map/ppermute | solution.py:244
  100.8 12.3 %collective-permute-start.4 = (bf16[12,12,8,128]{3,2,1,0:T(8,128)(2,1)S(1)}, bf16[12,12,8,128]{3,2,1,0:T(8,128)(2,1)S(1)}, u32[]{:S(2)}, u32[]{:S(2)}) collective-permute-start(bf16[12,12,8,128]{3,2,1,0:T(8,128)(2,1)S(1)} %all-to-all-done.3.sr), channel_id=1, source_target_pairs={{0,1},{1,2},{2,3},{3,4},{4,5},{5,6},{6,7},{7,8},{8,9},{9,10},{10,1... | collective-permute-start | bytes 884744 | tf_op jit(solution)/shard_map/ppermute | solution.py:243
  113.1 0.0 copy-start.3
  113.1 1.9 %collective-permute-start.3 = (bf16[2,12,8,640]{3,2,1,0:T(8,128)(2,1)S(1)}, bf16[2,12,8,640]{3,2,1,0:T(8,128)(2,1)S(1)}, u32[]{:S(2)}, u32[]{:S(2)}) collective-permute-start(bf16[2,12,8,640]{3,2,1,0:T(8,128)(2,1)S(1)} %pad_maximum_fusion.rec), channel_id=1, source_target_pairs={{0,63},{1,0},{2,1},{3,2},{4,3},{5,4},{6,5},{7,6},{8,7},{9,8},{10,9... | collective-permute-start | bytes 737288 | tf_op jit(solution)/shard_map/ppermute | solution.py:221
  115.1 7.5 %collective-permute-start.2 = (bf16[2,12,8,640]{3,2,1,0:T(8,128)(2,1)S(1)}, bf16[2,12,8,640]{3,2,1,0:T(8,128)(2,1)S(1)}, u32[]{:S(2)}, u32[]{:S(2)}) collective-permute-start(bf16[2,12,8,640]{3,2,1,0:T(8,128)(2,1)S(1)} %pad_maximum_fusion.rec), channel_id=1, source_target_pairs={{0,1},{1,2},{2,3},{3,4},{4,5},{5,6},{6,7},{7,8},{8,9},{9,10},{10,1... | collective-permute-start | bytes 737288 | tf_op jit(solution)/shard_map/ppermute | solution.py:220
  122.6 0.0 collective-permute-done.6.sp
  122.6 0.0 copy-done
  122.6 0.0 copy-start.4
  122.7 0.0 copy-done.2
  122.7 3.1 %collective-permute-start.8 = (bf16[12,8,128]{2,1,0:T(8,128)(2,1)S(1)}, bf16[12,8,128]{2,1,0:T(8,128)(2,1)S(1)}, u32[]{:S(2)}, u32[]{:S(2)}) collective-permute-start(bf16[12,8,128]{2,1,0:T(8,128)(2,1)S(1)} %get-tuple-element.14), channel_id=1, source_target_pairs={{0,64},{64,128},{128,192},{192,256},{256,320},{320,384},{384,448},... | collective-permute-start | bytes 73736 | tf_op jit(solution)/shard_map/ppermute | solution.py:250
  125.8 0.5 collective-permute-done.3.rec_hi
  126.2 0.0 copy-start.7
  126.2 6.6 %collective-permute-start.7 = (bf16[12,8,128]{2,1,0:T(8,128)(2,1)S(1)}, bf16[12,8,128]{2,1,0:T(8,128)(2,1)S(1)}, u32[]{:S(2)}, u32[]{:S(2)}) collective-permute-start(bf16[12,8,128]{2,1,0:T(8,128)(2,1)S(1)} %get-tuple-element.15), channel_id=1, source_target_pairs={{64,0},{128,64},{192,128},{256,192},{320,256},{384,320},{448,384},... | collective-permute-start | bytes 73736 | tf_op jit(solution)/shard_map/ppermute | solution.py:249
  132.9 0.0 collective-permute-done.2.rec_lo
  132.9 0.0 copy-start.8
  132.9 0.0 collective-permute-done.5.sr_hi
  132.9 0.0 copy-start.5
  132.9 0.0 collective-permute-done.4.sr_lo
  132.9 0.0 copy-start.6
  132.9 0.0 collective-permute-done.8.row_lo
  132.9 0.0 copy-start.9
  132.9 2.5 %collective-permute-done.7.row_hi = bf16[12,8,128]{2,1,0:T(8,128)(2,1)S(1)} collective-permute-done((bf16[12,8,128]{2,1,0:T(8,128)(2,1)S(1)}, bf16[12,8,128]{2,1,0:T(8,128)(2,1)S(1)}, u32[]{:S(2)}, u32[]{:S(2)}) %collective-permute-start.7) | collective-permute-done | bytes 24608 | tf_op jit(solution)/shard_map/ppermute | solution.py:249
  135.5 0.0 copy-done.3
  135.5 0.0 copy-done.4
  135.5 0.0 copy-done.7
  135.5 0.0 copy-done.8
  135.5 0.0 copy-done.5
  135.5 0.0 copy-done.6
  135.5 0.0 copy-done.9
  135.5 0.0 copy-start.10
  135.5 0.6 copy-done.10
  136.1 16.3 %shard_map.44 = (bf16[2,12,8,512]{3,2,1,0:T(8,128)(2,1)}, bf16[2,12,8,512]{3,2,1,0:T(8,128)(2,1)}) custom-call(s32[2]{0:T(128)} %pad_add_fusion.pos, bf16[2,12,8,640]{3,2,1,0:T(8,128)(2,1)} %copy-done.3, bf16[2,12,8,640]{3,2,1,0:T(8,128)(2,1)} %copy-done.8, bf16[2,12,8,640]{3,2,1,0:T(8,128)(2,1)} %copy-done.7, bf16[12,12,8,128]{3,2,1,0:T(8,128)(2,1)} %copy-done.2, ...), custom_call_target="tpu_custom_call" | custom-call | tf_op jit(solution)/shard_map/pallas_call | solution.py:251
  (5 shorter events, 0.1 us)
Async XLA Ops:
  3.2 12.5 %copy-start.12 = (bf16[12,8,128]{2,1,0:T(8,128)(2,1)S(1)}, bf16[12,8,128]{2,1,0:T(8,128)(2,1)}, u32[]{:S(2)}) copy-start(bf16[12,8,128]{2,1,0:T(8,128)(2,1)} %get-tuple-element.9) | copy-start | bytes 73732
  56.7 19.6 %copy-start.11 = (bf16[12,8,128]{2,1,0:T(8,128)(2,1)S(1)}, bf16[12,8,128]{2,1,0:T(8,128)(2,1)}, u32[]{:S(2)}) copy-start(bf16[12,8,128]{2,1,0:T(8,128)(2,1)} %get-tuple-element.10) | copy-start | bytes 73732
  76.3 46.3 %copy-start = (bf16[8,4,12,8,128]{4,3,2,1,0:T(8,128)(2,1)}, bf16[8,4,12,8,128]{4,3,2,1,0:T(8,128)(2,1)S(1)}, u32[]{:S(2)}) copy-start(bf16[8,4,12,8,128]{4,3,2,1,0:T(8,128)(2,1)S(1)} %all_to_all.28.ss) | copy-start | bytes 2359300
  77.1 12.3 %copy-start.1 = (bf16[1,2,96,512]{3,2,1,0:T(8,128)(2,1)S(1)}, bf16[1,2,96,512]{3,2,1,0:T(8,128)(2,1)}, u32[]{:S(2)}) copy-start(bf16[1,2,96,512]{3,2,1,0:T(8,128)(2,1)} %param.2) | copy-start | bytes 589828
  77.1 20.6 %all-to-all-start.3 = ((bf16[12,12,8,128]{3,2,1,0:T(8,128)(2,1)}), bf16[12,12,8,128]{3,2,1,0:T(8,128)(2,1)S(1)}, u32[]{:S(2)}, u32[]{:S(2)}) async-start(bf16[12,12,8,128]{3,2,1,0:T(8,128)(2,1)} %broadcast_in_dim.25), calls=%async_computation.3 | async-start | bytes 589824 | tf_op jit(solution)/shard_map/all_to_all | solution.py:210
  81.7 40.9 %collective-permute-start.6 = (bf16[8,4,12,8,128]{4,3,2,1,0:T(8,128)(2,1)S(1)}, bf16[8,4,12,8,128]{4,3,2,1,0:T(8,128)(2,1)S(1)}, u32[]{:S(2)}, u32[]{:S(2)}) collective-permute-start(bf16[8,4,12,8,128]{4,3,2,1,0:T(8,128)(2,1)S(1)} %all_to_all.28.ss), channel_id=1, source_target_pairs={{0,1},{1,0},{2,3},{3,2},{4,5},{5,4},{6,7},{7,6},{8,9},{9,8},{10,11... | collective-permute-start | bytes 2359304 | tf_op jit(solution)/shard_map/ppermute | solution.py:245
  89.5 7.1 %collective-permute-start.1 = (bf16[2,96,128]{2,1,0:T(8,128)(2,1)S(1)}, bf16[2,96,128]{2,1,0:T(8,128)(2,1)S(1)}, u32[]{:S(2)}, u32[]{:S(2)}) collective-permute-start(bf16[2,96,128]{2,1,0:T(8,128)(2,1)S(1)} %get-tuple-element.16), channel_id=1, source_target_pairs={{0,64},{64,128},{128,192},{192,256},{256,320},{320,384},{384,448},... | collective-permute-start | bytes 147464 | tf_op jit(solution)/shard_map/ppermute | solution.py:216
  92.6 5.1 %collective-permute-start = (bf16[2,96,128]{2,1,0:T(8,128)(2,1)S(1)}, bf16[2,96,128]{2,1,0:T(8,128)(2,1)S(1)}, u32[]{:S(2)}, u32[]{:S(2)}) collective-permute-start(bf16[2,96,128]{2,1,0:T(8,128)(2,1)S(1)} %get-tuple-element.17), channel_id=1, source_target_pairs={{64,0},{128,64},{192,128},{256,192},{320,256},{384,320},{448,384},... | collective-permute-start | bytes 147464 | tf_op jit(solution)/shard_map/ppermute | solution.py:215
  97.7 24.9 %copy-start.2 = (bf16[12,12,8,128]{3,2,1,0:T(8,128)(2,1)}, bf16[12,12,8,128]{3,2,1,0:T(8,128)(2,1)S(1)}, u32[]{:S(2)}) copy-start(bf16[12,12,8,128]{3,2,1,0:T(8,128)(2,1)S(1)} %all-to-all-done.3.sr) | copy-start | bytes 884740
  97.7 35.1 %collective-permute-start.5 = (bf16[12,12,8,128]{3,2,1,0:T(8,128)(2,1)S(1)}, bf16[12,12,8,128]{3,2,1,0:T(8,128)(2,1)S(1)}, u32[]{:S(2)}, u32[]{:S(2)}) collective-permute-start(bf16[12,12,8,128]{3,2,1,0:T(8,128)(2,1)S(1)} %all-to-all-done.3.sr), channel_id=1, source_target_pairs={{0,63},{1,0},{2,1},{3,2},{4,3},{5,4},{6,5},{7,6},{8,7},{9,8},{10,9... | collective-permute-start | bytes 884744 | tf_op jit(solution)/shard_map/ppermute | solution.py:244
  100.8 32.1 %collective-permute-start.4 = (bf16[12,12,8,128]{3,2,1,0:T(8,128)(2,1)S(1)}, bf16[12,12,8,128]{3,2,1,0:T(8,128)(2,1)S(1)}, u32[]{:S(2)}, u32[]{:S(2)}) collective-permute-start(bf16[12,12,8,128]{3,2,1,0:T(8,128)(2,1)S(1)} %all-to-all-done.3.sr), channel_id=1, source_target_pairs={{0,1},{1,2},{2,3},{3,4},{4,5},{5,6},{6,7},{7,8},{8,9},{9,10},{10,1... | collective-permute-start | bytes 884744 | tf_op jit(solution)/shard_map/ppermute | solution.py:243
  113.1 22.4 %copy-start.3 = (bf16[2,12,8,640]{3,2,1,0:T(8,128)(2,1)}, bf16[2,12,8,640]{3,2,1,0:T(8,128)(2,1)S(1)}, u32[]{:S(2)}) copy-start(bf16[2,12,8,640]{3,2,1,0:T(8,128)(2,1)S(1)} %pad_maximum_fusion.rec) | copy-start | bytes 737284
  113.1 13.1 %collective-permute-start.3 = (bf16[2,12,8,640]{3,2,1,0:T(8,128)(2,1)S(1)}, bf16[2,12,8,640]{3,2,1,0:T(8,128)(2,1)S(1)}, u32[]{:S(2)}, u32[]{:S(2)}) collective-permute-start(bf16[2,12,8,640]{3,2,1,0:T(8,128)(2,1)S(1)} %pad_maximum_fusion.rec), channel_id=1, source_target_pairs={{0,63},{1,0},{2,1},{3,2},{4,3},{5,4},{6,5},{7,6},{8,7},{9,8},{10,9... | collective-permute-start | bytes 737288 | tf_op jit(solution)/shard_map/ppermute | solution.py:221
  115.1 17.8 %collective-permute-start.2 = (bf16[2,12,8,640]{3,2,1,0:T(8,128)(2,1)S(1)}, bf16[2,12,8,640]{3,2,1,0:T(8,128)(2,1)S(1)}, u32[]{:S(2)}, u32[]{:S(2)}) collective-permute-start(bf16[2,12,8,640]{3,2,1,0:T(8,128)(2,1)S(1)} %pad_maximum_fusion.rec), channel_id=1, source_target_pairs={{0,1},{1,2},{2,3},{3,4},{4,5},{5,6},{6,7},{7,8},{8,9},{9,10},{10,1... | collective-permute-start | bytes 737288 | tf_op jit(solution)/shard_map/ppermute | solution.py:220
  122.6 12.8 %copy-start.4 = (bf16[8,4,12,8,128]{4,3,2,1,0:T(8,128)(2,1)}, bf16[8,4,12,8,128]{4,3,2,1,0:T(8,128)(2,1)S(1)}, u32[]{:S(2)}) copy-start(bf16[8,4,12,8,128]{4,3,2,1,0:T(8,128)(2,1)S(1)} %collective-permute-done.6.sp) | copy-start | bytes 2359300
  122.7 10.2 %collective-permute-start.8 = (bf16[12,8,128]{2,1,0:T(8,128)(2,1)S(1)}, bf16[12,8,128]{2,1,0:T(8,128)(2,1)S(1)}, u32[]{:S(2)}, u32[]{:S(2)}) collective-permute-start(bf16[12,8,128]{2,1,0:T(8,128)(2,1)S(1)} %get-tuple-element.14), channel_id=1, source_target_pairs={{0,64},{64,128},{128,192},{192,256},{256,320},{320,384},{384,448},... | collective-permute-start | bytes 73736 | tf_op jit(solution)/shard_map/ppermute | solution.py:250
  126.2 9.2 %copy-start.7 = (bf16[2,12,8,640]{3,2,1,0:T(8,128)(2,1)}, bf16[2,12,8,640]{3,2,1,0:T(8,128)(2,1)S(1)}, u32[]{:S(2)}) copy-start(bf16[2,12,8,640]{3,2,1,0:T(8,128)(2,1)S(1)} %collective-permute-done.3.rec_hi) | copy-start | bytes 737284
  126.2 9.2 %collective-permute-start.7 = (bf16[12,8,128]{2,1,0:T(8,128)(2,1)S(1)}, bf16[12,8,128]{2,1,0:T(8,128)(2,1)S(1)}, u32[]{:S(2)}, u32[]{:S(2)}) collective-permute-start(bf16[12,8,128]{2,1,0:T(8,128)(2,1)S(1)} %get-tuple-element.15), channel_id=1, source_target_pairs={{64,0},{128,64},{192,128},{256,192},{320,256},{384,320},{448,384},... | collective-permute-start | bytes 73736 | tf_op jit(solution)/shard_map/ppermute | solution.py:249
  132.9 2.6 %copy-start.8 = (bf16[2,12,8,640]{3,2,1,0:T(8,128)(2,1)}, bf16[2,12,8,640]{3,2,1,0:T(8,128)(2,1)S(1)}, u32[]{:S(2)}) copy-start(bf16[2,12,8,640]{3,2,1,0:T(8,128)(2,1)S(1)} %collective-permute-done.2.rec_lo) | copy-start | bytes 737284
  132.9 2.6 %copy-start.5 = (bf16[12,12,8,128]{3,2,1,0:T(8,128)(2,1)}, bf16[12,12,8,128]{3,2,1,0:T(8,128)(2,1)S(1)}, u32[]{:S(2)}) copy-start(bf16[12,12,8,128]{3,2,1,0:T(8,128)(2,1)S(1)} %collective-permute-done.5.sr_hi) | copy-start | bytes 884740
  132.9 2.6 %copy-start.6 = (bf16[12,12,8,128]{3,2,1,0:T(8,128)(2,1)}, bf16[12,12,8,128]{3,2,1,0:T(8,128)(2,1)S(1)}, u32[]{:S(2)}) copy-start(bf16[12,12,8,128]{3,2,1,0:T(8,128)(2,1)S(1)} %collective-permute-done.4.sr_lo) | copy-start | bytes 884740
  132.9 2.6 %copy-start.9 = (bf16[12,8,128]{2,1,0:T(8,128)(2,1)}, bf16[12,8,128]{2,1,0:T(8,128)(2,1)S(1)}, u32[]{:S(2)}) copy-start(bf16[12,8,128]{2,1,0:T(8,128)(2,1)S(1)} %collective-permute-done.8.row_lo) | copy-start | bytes 73732
  135.5 0.6 copy-start.10

commit v2 on v1

v2 whole, which is shorter than its diff:
```python
import jax
import jax.numpy as jnp
from jax import lax
from jax.experimental import pallas as pl
from jax.experimental.pallas import tpu as pltpu
from jax.sharding import PartitionSpec as P

NZ, NY, NC = 4, 8, 2
NP = NY * NC
NA = 12
TILES = 3 * NZ
EXT = 640
STRIDE = 8
REACH = 4
EPS = 1e-6
F32, BF16 = jnp.float32, jnp.bfloat16


def vmem(count):
    return [pl.BlockSpec(memory_space=pltpu.VMEM)] * count


def smem(count):
    return [pl.BlockSpec(memory_space=pltpu.SMEM)] * count


def pick_behind_kernel(pos, panel, rec, to_src):
    lane = lax.broadcasted_iota(jnp.int32, (1, 128), 1)
    early = pos[0] < 8
    key_part = jnp.where(early, lane % 8 // 4, lane // 64)
    key_pos = 16 * (lane % 4) + jnp.where(early, lane // 8, lane % 64 // 4)
    offset = jnp.zeros((1, 128), jnp.int32)
    for g in range(64):
        offset = jnp.where(key_pos == g, panel[64 * pos[0] + g], offset)
    key_row = STRIDE * key_pos + offset
    rows = lax.broadcasted_iota(jnp.int32, (512, 128), 0)
    total = jnp.zeros((96, 128), F32)
    for part in range(2):
        chosen = ((rows == key_row) & (key_part == part)).astype(F32).astype(BF16)
        total += jnp.dot(rec[part], chosen, preferred_element_type=F32)
    to_src[...] = total.astype(BF16).reshape(NA, 8, 128)


def pick_front_kernel(pos, panel, rec, to_rcv):
    lane = lax.broadcasted_iota(jnp.int32, (1, 128), 1)
    kind, slot, run_z = lane % 32 // 8, lane % 8, lane // 32
    run = jnp.where(kind < 2, slot, jnp.where(kind == 2, 8 + slot % 4, NA))
    run_part = jnp.where(kind < 2, kind, slot // 4)
    offset = jnp.zeros((1, 128), jnp.int32)
    for a in range(NA):
        offset = jnp.where(run == a, panel[64 * a + pos[1]], offset)
    col = jnp.where(run < NA, STRIDE * run + offset, -1)
    rows = lax.broadcasted_iota(jnp.int32, (96, 128), 0)
    total = jnp.zeros((128, 128), F32)
    for z in range(NZ):
        for part in range(2):
            chosen = ((rows == col) & (run_part == part) & (run_z == z)).astype(F32).astype(BF16)
            total += lax.dot_general(
                rec[part, :, 128 * z : 128 * z + 128],
                chosen,
                (((0,), (0,)), ((), ())),
                preferred_element_type=F32,
            )
    to_rcv[...] = total.astype(BF16).reshape(NP, 8, 128)


def turned(x, shift):
    return pltpu.roll(x, shift % 128, 1) if shift % 128 else x


def order_behind_kernel(from_src, behind):
    lane = lax.broadcasted_iota(jnp.int32, (8, 128), 1)
    tiles = [from_src[a].astype(F32) for a in range(NA)]
    for part in range(2):
        for pair in range(2):
            for kind in range(2):
                acc = jnp.zeros((8, 128), F32)
                for a in range(8):
                    acc = jnp.where(lane % 8 == a, turned(tiles[a], a - (4 * part + 2 * pair + kind)), acc)
                behind[6 * part + 3 * pair + kind] = acc.astype(BF16)
            acc = jnp.zeros((8, 128), F32)
            for odd in range(2):
                for a in range(8, NA):
                    shift = 64 * (odd - part) + a - 8 - (2 * pair + odd)
                    acc = jnp.where((lane // 64 == odd) & (lane % 4 == a - 8), turned(tiles[a], shift), acc)
            behind[6 * part + 3 * pair + 2] = acc.astype(BF16)


def order_kernel(pos, from_rcv, behind, out):
    lane = lax.broadcasted_iota(jnp.int32, (8, 128), 1)
    tiles = [from_rcv[p].astype(F32) for p in range(NP)]
    odd = pos[1] // NP % 2 == 1
    for z in range(NZ):
        for kind in range(3):
            acc = jnp.zeros((8, 128), F32)
            for p in range(NP):
                if kind < 2:
                    acc = jnp.where(lane // 8 == p, turned(tiles[p], 8 * p - 32 * z - 8 * kind), acc)
                else:
                    for part in range(2):
                        shift = 64 * part + 4 * p - 32 * z - 16 - 4 * part
                        acc = jnp.where(lane // 4 == 16 * part + p, turned(tiles[p], shift), acc)
            if kind == 2:
                acc = jnp.where(odd, pltpu.roll(acc, 64, 1), acc)
            tile = acc.astype(BF16)
            for copy in range(NZ):
                out[copy, 3 * z + kind] = tile
    for copy in range(NZ):
        out[copy, TILES:] = behind[...]


def average_kernel(pos, pieces, rows, own):
    low = lax.broadcasted_iota(jnp.int32, (8, 128), 1) < 64
    for z in range(NZ):
        for tile in range(TILES):
            part, pair, kind = tile // 6, tile % 6 // 3, tile % 3
            if kind < 2:
                front = pieces[2 * pair + kind, 3 * z + part].astype(F32)
            else:
                even, odd = [pieces[2 * pair + n, 3 * z + 2].astype(F32) for n in range(2)]
                front = pltpu.roll(jnp.where(low, odd, even), 64, 1) if part else jnp.where(low, even, odd)
            rows[z, tile] = ((front + pieces[z, TILES + tile].astype(F32)) * 0.5).astype(BF16)
    own[...] = rows[pos[1] // NP]


def bounds(rcv):
    return (rcv == 0).astype(jnp.int32), (rcv == NZ * NP - 1).astype(jnp.int32)


def sides(core, partner, beyond):
    return jnp.where(core == 0, beyond, partner), jnp.where(core == 0, partner, beyond)


def neighbours(a, first, last):
    keep_lo = (a - first >= 0).astype(F32)
    keep_hi = (a + last <= NA - 1).astype(F32)
    return jnp.maximum(a - first, 0), jnp.minimum(a + last, NA - 1), keep_lo, keep_hi


def windows_rows(x, count):
    two = x[:-1] + x[1:]
    four = two[:-2] + two[2:]
    eight = four[:-4] + four[4:]
    return eight[:count] + x[8 : 8 + count]


def windows_lanes(source, target, band, pairs):
    count = EXT // 128
    rows = source.shape[0] * source.shape[1] * source.shape[2]
    tiles = []
    for n in range(count):
        x = source[:, :, :, 128 * n : 128 * n + 128].reshape(rows, 128)
        high = x.astype(BF16)
        tiles.append((high, (x - high.astype(F32)).astype(BF16)))
    for n in pairs:
        width = min(2, count - n)
        total = jnp.zeros((rows, 128 * width), F32)
        for half in range(2):
            near = jnp.concatenate([tiles[(n + m) % count][half] for m in range(-1, width + 1)], axis=1)
            total += jnp.dot(near, band[: 128 * (width + 2), : 128 * width], preferred_element_type=F32)
        target[:, :, :, 128 * n : 128 * (n + width)] = total.reshape(*target.shape[:3], 128 * width)


def final_kernel(pos, rec, rec_partner, rec_beyond, sr, ss, sp, row_hi, row_lo, prim, mult, a_rows, b_rows, pred, once, box):
    rcv = pos[1]
    core = rcv % 2
    first, last = bounds(rcv)

    def gather(z, _):
        for t in range(TILES):
            mine, theirs = ss[:, z, t].astype(F32), sp[:, z, t].astype(F32)
            zero = jnp.where(core == 0, mine, theirs)
            one = jnp.where(core == 0, theirs, mine)
            x = jnp.stack([zero, one], axis=1).reshape(128, 128)
            b_rows[z, :, 128 * t : 128 * t + 128] = x.astype(BF16)
        return 0

    lax.fori_loop(0, NZ, gather, 0)
    for t in range(TILES):
        x = jnp.concatenate([row_hi[t].astype(F32), jnp.zeros((112, 128), F32), row_lo[t].astype(F32)], axis=0)
        b_rows[NZ, :, 128 * t : 128 * t + 128] = x.astype(BF16)

    def spread(a, _):
        lo, hi, keep_lo, keep_hi = neighbours(a, first, last)
        for t in range(TILES):
            x = jnp.concatenate(
                [sr[lo, 0, t].astype(F32) * keep_lo, sr[a, 1, t].astype(F32), sr[hi, 2, t].astype(F32) * keep_hi], axis=0
            )
            a_rows[a, :, 128 * t : 128 * t + 128] = x.astype(BF16)
        return 0

    lax.fori_loop(0, NA, spread, 0, unroll=2)
    half = 64 * TILES
    left = a_rows[...].reshape(24 * NA, 128 * TILES)
    left = left[:, :half], left[:, half:]

    def times(x, y):
        return lax.dot_general(x, y, (((1,), (1,)), ((), ())), preferred_element_type=F32)

    for n in range(NZ + 1):
        right = b_rows[n, :, :half], b_rows[n, :, half:]
        value = times(left[0], right[0]) - times(left[1], right[1])
        pred[0, :, :, 128 * n : 128 * n + 128] = value.reshape(NA, 24, 128)
        value = times(left[0], right[1]) + times(left[1], right[0])
        pred[1, :, :, 128 * n : 128 * n + 128] = value.reshape(NA, 24, 128)

    def data_of(a):
        lo, hi, keep_lo, keep_hi = neighbours(a, first, last)
        data = []
        for part in range(2):
            below, _ = sides(core, rec_partner[part, lo].astype(F32), rec_beyond[part, lo].astype(F32))
            _, above = sides(core, rec_partner[part, hi].astype(F32), rec_beyond[part, hi].astype(F32))
            data.append(jnp.concatenate([below * keep_lo, rec[part, a].astype(F32), above * keep_hi], axis=0))
        return data

    def terms_of(dr, di, pr, pi):
        return pr * dr + pi * di, pr * di - pi * dr, pr * pr + pi * pi

    def subtract(dr, di, pr, pi, sums):
        den = sums[2] + EPS
        gain_re, gain_im = sums[0] / den, sums[1] / den
        return dr - (gain_re * pr - gain_im * pi), di - (gain_re * pi + gain_im * pr)

    def first_sweep(a, _):
        dr, di = data_of(a)
        guess = []
        for part in range(2):
            full = pred[part, a]
            mult[part, a] = (full[8:16, :512] * (768.0 ** -0.5)).astype(BF16)
            full = full.astype(BF16).astype(F32)
            pred[part, a] = full
            guess.append(full)
        weight = 1.5 - jnp.tanh(dr * dr + di * di)
        for n, q in enumerate(terms_of(dr, di, *guess)):
            once[n, a] = windows_rows(weight * q, 16)
        return 0

    lax.fori_loop(0, NA, first_sweep, 0, unroll=2)
    far = lax.broadcasted_iota(jnp.int32, (512, 256), 0) - lax.broadcasted_iota(jnp.int32, (512, 256), 1) - 128
    band = (jnp.abs(far) <= REACH).astype(F32).astype(BF16)
    windows_lanes(once, box, band, (0, 2, 4))

    def second_sweep(a, _):
        dr, di = [v[4:20] for v in data_of(a)]
        pr, pi = pred[0, a, 4:20], pred[1, a, 4:20]
        er, ei = subtract(dr, di, pr, pi, [box[n, a] for n in range(3)])
        weight = 1.5 - jnp.tanh(er * er + ei * ei)
        for n, q in enumerate(terms_of(dr, di, pr, pi)):
            once[n, a, :8] = windows_rows(weight * q, 8)
        return 0

    lax.fori_loop(0, NA, second_sweep, 0, unroll=2)
    windows_lanes(once.at[:, :, :8], box.at[:, :, :8], band, (0, 2))

    def finish(a, _):
        dr, di = rec[0, a, :, :512].astype(F32), rec[1, a, :, :512].astype(F32)
        pr, pi = pred[0, a, 8:16, :512], pred[1, a, 8:16, :512]
        er, ei = subtract(dr, di, pr, pi, [box[n, a, :8, :512] for n in range(3)])
        prim[0, a], prim[1, a] = er.astype(BF16), ei.astype(BF16)
        return 0

    lax.fori_loop(0, NA, finish, 0, unroll=2)


def shape(*dims):
    return jax.ShapeDtypeStruct(dims, BF16)


def ring(count, step, closed):
    return [(n, (n + step) % count) for n in range(count) if closed or 0 <= n + step < count]


def block(record, panel_offset):
    src_count, rcv_count = lax.axis_size("src"), lax.axis_size("rcv")
    src, rcv = lax.axis_index("src"), lax.axis_index("rcv")
    pos = jnp.stack([src, rcv]).astype(jnp.int32)
    rec = record[0]
    plane = [[z * NP + p for p in range(NP)] for z in range(NZ)]
    column = [[z * NP + p for z in range(NZ)] for p in range(NP)]
    line = [[z * NP + y * NC + c for y in range(NY)] for z in range(NZ) for c in range(NC)]
    swap = [(n, n ^ 1) for n in range(rcv_count)]
    beyond = [(n, (n + (1 if n % 2 else -1)) % rcv_count) for n in range(rcv_count)]

    def exchange(x, axis, groups=None):
        return lax.all_to_all(x, axis, split_axis=0, concat_axis=0, tiled=True, axis_index_groups=groups)

    def copies(x, count, axis, groups=None):
        return exchange(jnp.broadcast_to(x, (count, *x.shape)), axis, groups)

    def kernel(body, outs, scalars, arrays, scratch=(), flops=1 << 20, moved=1 << 20):
        return pl.pallas_call(
            body,
            out_shape=outs,
            in_specs=smem(len(scalars)) + vmem(len(arrays)),
            out_specs=jax.tree.map(lambda _: vmem(1)[0], outs),
            scratch_shapes=scratch,
            cost_estimate=pl.CostEstimate(flops=flops, bytes_accessed=moved, transcendentals=0),
        )(*scalars, *arrays)

    to_src = kernel(pick_behind_kernel, shape(NA, 8, 128), (pos, panel_offset), (rec,))
    from_src = exchange(to_src, "src")
    to_rcv = kernel(pick_front_kernel, shape(NP, 8, 128), (pos, panel_offset), (rec,))
    from_rcv = exchange(to_rcv, "rcv", plane)
    behind = kernel(order_behind_kernel, shape(TILES, 8, 128), (), (from_src,))
    message = kernel(order_kernel, shape(NZ, 2 * TILES, 8, 128), (pos,), (from_rcv, behind))
    pieces = exchange(message, "rcv", column)
    held, _ = lax.optimization_barrier((rec, from_rcv))
    first_tile, last_tile = held[:, :, :128], held[:, :, 384:]
    next_src = lax.ppermute(first_tile, "src", ring(src_count, -1, False))
    last_src = lax.ppermute(last_tile, "src", ring(src_count, 1, False))
    lane = lax.broadcasted_iota(jnp.int32, (1, 1, 128), 2)
    rim = jnp.where(lane < 8, next_src, jnp.where(lane >= 120, last_src, jnp.zeros_like(last_src)))
    wide = jnp.concatenate([rec, rim], axis=2).reshape(2, NA, 8, EXT)
    pieces, wide = lax.optimization_barrier((pieces, wide))
    rows, own = kernel(average_kernel, (shape(NZ, TILES, 8, 128), shape(TILES, 8, 128)), (pos,), (pieces,))
    ss = copies(rows, NY, "rcv", line)
    near = own
    own_partner = lax.ppermute(near, "rcv", swap)
    own_beyond = lax.ppermute(near, "rcv", beyond)
    wide_partner = lax.ppermute(wide, "rcv", swap)
    wide_beyond = lax.ppermute(wide, "rcv", beyond)
    even_core = rcv % 2 == 0
    own = jnp.stack(
        [jnp.where(even_core, own_beyond, own_partner), own, jnp.where(even_core, own_partner, own_beyond)]
    )
    ss, own, wide_partner, wide_beyond = lax.optimization_barrier((ss, own, wide_partner, wide_beyond))
    sr = copies(own, src_count, "src")
    sp = lax.ppermute(ss, "rcv", swap)
    row_first = jnp.where(even_core, ss[0, 0], sp[0, 0])
    row_last = jnp.where(even_core, sp[NY - 1, NZ - 1], ss[NY - 1, NZ - 1])
    row_hi = lax.ppermute(row_first, "src", ring(src_count, -1, False))
    row_lo = lax.ppermute(row_last, "src", ring(src_count, 1, False))
    prim, mult = kernel(
        final_kernel,
        (shape(2, NA, 8, 512),) * 2,
        (pos,),
        (wide, wide_partner, wide_beyond, sr, ss, sp, row_hi, row_lo),
        [
            pltpu.VMEM((NA, 24, 128 * TILES), BF16),
            pltpu.VMEM((NZ + 1, 128, 128 * TILES), BF16),
            pltpu.VMEM((2, NA, 24, EXT), F32),
            pltpu.VMEM((3, NA, 16, EXT), F32),
            pltpu.VMEM((3, NA, 16, EXT), F32),
        ],
    )
    return prim.reshape(record.shape), mult.reshape(record.shape)


def solution(mesh):
    in_specs = (P(None, None, "rcv", "src"), P())
    out_specs = (P(None, None, "rcv", "src"), P(None, None, "rcv", "src"))
    return jax.shard_map(block, mesh=mesh, in_specs=in_specs, out_specs=out_specs, check_vma=False)
```

time: 153 us -> 135 us (0.88)
  the two profiles are of different devices: /device:TPU:61 before, /device:TPU:6 now
where the time goes in v2:
time: 135 us; the launch traced here: 134 us
  starting transfers between devices  73.9 us (55%)
  waiting for transfers between devices  33.3 us (25%)
  Pallas kernels  19.2 us (14%)
  local copies, waits for them, and re-layouts  5.89 us (4%)
    all_to_all x5, starting transfers between devices, exchange(): lax.all_to_all(x, axis, split_axis=0, concat_axis=0, tiled=True, axis_ind...  44.1 us
    pallas_call x6, Pallas kernels, kernel(): pl.pallas_call(body, out_shape=outs, in_specs=smem(len(scalars)) + vmem(l...  19.2 us
    all_to_all x5, waiting for transfers between devices, exchange(): lax.all_to_all(x, axis, split_axis=0, concat_axis=0, tiled=True, axis_ind...  17.3 us
    ppermute x1, waiting for transfers between devices, block(): wide_beyond = lax.ppermute(wide, 'rcv', beyond)  8.16 us
    ppermute x1, starting transfers between devices, block(): wide_beyond = lax.ppermute(wide, 'rcv', beyond)  6.27 us
    ppermute x1, waiting for transfers between devices, block(): row_lo = lax.ppermute(row_last, 'src', ring(src_count, 1, False))  5.57 us
    ppermute x1, starting transfers between devices, block(): row_hi = lax.ppermute(row_first, 'src', ring(src_count, -1, False))  4.56 us
    ppermute x1, starting transfers between devices, block(): next_src = lax.ppermute(first_tile, 'src', ring(src_count, -1, False))  4.56 us
  transfers between devices with their start and end apart: 14, of which 5 were waited for; matrix products, arithmetic and copies ran while one was open for 0% of the time, Pallas kernels for 4%

profile of v2, /device:TPU:6, one launch (start us, length us, event | category | flops | bytes accessed | tf_op | source)
XLA Modules:
  0.0 133.8 jit_solution(2488467650462001381)
XLA Ops:
  0.6 0.6 pad_add_fusion.pos
  1.2 1.8 %shard_map.41 = bf16[16,8,128]{2,1,0:T(8,128)(2,1)} custom-call(s32[2]{0:T(128)} %pad_add_fusion.pos, s32[768]{0:T(1024)} %panel.3, bf16[2,96,512]{2,1,0:T(8,128)(2,1)} %bitcast.17), custom_call_target="tpu_custom_call" | custom-call | flops 1048576 | bytes 1048576 | tf_op jit(solution)/shard_map/pallas_call | solution.py:291
  3.0 0.0 copy-start.2
  3.0 7.3 %all-to-all-start = ((bf16[16,8,128]{2,1,0:T(8,128)(2,1)}), bf16[16,8,128]{2,1,0:T(8,128)(2,1)S(1)}, u32[]{:S(2)}, u32[]{:S(2)}) async-start(bf16[16,8,128]{2,1,0:T(8,128)(2,1)} %shard_map.41), calls=%async_computation | async-start | bytes 65536 | tf_op jit(solution)/shard_map/all_to_all | solution.py:285
  10.4 1.8 %shard_map.42 = bf16[12,8,128]{2,1,0:T(8,128)(2,1)} custom-call(s32[2]{0:T(128)} %pad_add_fusion.pos, s32[768]{0:T(1024)} %panel.3, bf16[2,96,512]{2,1,0:T(8,128)(2,1)} %bitcast.18), custom_call_target="tpu_custom_call" | custom-call | flops 1048576 | bytes 1048576 | tf_op jit(solution)/shard_map/pallas_call | solution.py:291
  12.2 5.9 %all-to-all-done.from_rcv = bf16[16,8,128]{2,1,0:T(8,128)(2,1)S(1)} async-done(((bf16[16,8,128]{2,1,0:T(8,128)(2,1)}), bf16[16,8,128]{2,1,0:T(8,128)(2,1)S(1)}, u32[]{:S(2)}, u32[]{:S(2)}) %all-to-all-start) | async-done | bytes 32800 | tf_op jit(solution)/shard_map/all_to_all | solution.py:285
  18.0 0.0 copy-start.8
  18.0 9.1 %all-to-all-start.1 = ((bf16[12,8,128]{2,1,0:T(8,128)(2,1)}), bf16[12,8,128]{2,1,0:T(8,128)(2,1)S(1)}, u32[]{:S(2)}, u32[]{:S(2)}) async-start(bf16[12,8,128]{2,1,0:T(8,128)(2,1)} %shard_map.42), calls=%async_computation.1 | async-start | bytes 49152 | tf_op jit(solution)/shard_map/all_to_all | solution.py:285
  27.1 0.0 copy-done.2
  27.2 0.0 copy-done.8
  27.2 4.6 %collective-permute-start = (bf16[2,96,128]{2,1,0:T(8,128)(2,1)S(1)}, bf16[2,96,128]{2,1,0:T(8,128)(2,1)S(1)}, u32[]{:S(2)}, u32[]{:S(2)}) collective-permute-start(bf16[2,96,128]{2,1,0:T(8,128)(2,1)S(1)} %get-tuple-element.27), channel_id=1, source_target_pairs={{64,0},{128,64},{192,128},{256,192},{320,256},{384,320},{448,384},... | collective-permute-start | bytes 147464 | tf_op jit(solution)/shard_map/ppermute | solution.py:309
  31.7 1.9 %collective-permute-start.1 = (bf16[2,96,128]{2,1,0:T(8,128)(2,1)S(1)}, bf16[2,96,128]{2,1,0:T(8,128)(2,1)S(1)}, u32[]{:S(2)}, u32[]{:S(2)}) collective-permute-start(bf16[2,96,128]{2,1,0:T(8,128)(2,1)S(1)} %get-tuple-element.26), channel_id=1, source_target_pairs={{0,64},{64,128},{128,192},{192,256},{256,320},{320,384},{384,448},... | collective-permute-start | bytes 147464 | tf_op jit(solution)/shard_map/ppermute | solution.py:310
  33.7 0.0 all-to-all-done.1.from_src
  33.7 0.0 copy-start.9
  33.7 0.6 copy-done.9
  34.3 1.5 %shard_map.43.behind = bf16[12,8,128]{2,1,0:T(8,128)(2,1)} custom-call(bf16[12,8,128]{2,1,0:T(8,128)(2,1)} %copy-done.9), custom_call_target="tpu_custom_call" | custom-call | flops 1048576 | bytes 1048576 | tf_op jit(solution)/shard_map/pallas_call | solution.py:291
  35.8 1.8 %shard_map.44 = bf16[4,24,8,128]{3,2,1,0:T(8,128)(2,1)} custom-call(s32[2]{0:T(128)} %pad_add_fusion.pos, bf16[16,8,128]{2,1,0:T(8,128)(2,1)} %copy-done.8, bf16[12,8,128]{2,1,0:T(8,128)(2,1)} %shard_map.43.behind), custom_call_target="tpu_custom_call" | custom-call | flops 1048576 | bytes 1048576 | tf_op jit(solution)/shard_map/pallas_call | solution.py:291
  37.5 13.8 %all-to-all-start.2 = ((bf16[4,24,8,128]{3,2,1,0:T(8,128)(2,1)}), bf16[4,24,8,128]{3,2,1,0:T(8,128)(2,1)S(1)}, u32[]{:S(2)}, u32[]{:S(2)}) async-start(bf16[4,24,8,128]{3,2,1,0:T(8,128)(2,1)} %shard_map.44), calls=%async_computation.2 | async-start | bytes 393216 | tf_op jit(solution)/shard_map/all_to_all | solution.py:285
  51.4 0.0 collective-permute-done
  51.4 0.0 collective-permute-done.1
  51.4 0.0 copy-start.3
  51.4 11.4 %all-to-all-done.2.pieces = bf16[4,24,8,128]{3,2,1,0:T(8,128)(2,1)S(1)} async-done(((bf16[4,24,8,128]{3,2,1,0:T(8,128)(2,1)}), bf16[4,24,8,128]{3,2,1,0:T(8,128)(2,1)S(1)}, u32[]{:S(2)}, u32[]{:S(2)}) %all-to-all-start.2) | async-done | bytes 196640 | tf_op jit(solution)/shard_map/all_to_all | solution.py:285
  62.8 0.0 copy-start.5
  62.8 0.7 copy-done.5
  63.5 1.7 %shard_map.45 = (bf16[4,12,8,128]{3,2,1,0:T(8,128)(2,1)}, bf16[12,8,128]{2,1,0:T(8,128)(2,1)}) custom-call(s32[2]{0:T(128)} %pad_add_fusion.pos, bf16[4,24,8,128]{3,2,1,0:T(8,128)(2,1)} %copy-done.5), custom_call_target="tpu_custom_call" | custom-call | flops 1048576 | bytes 1048576 | tf_op jit(solution)/shard_map/pallas_call | solution.py:291
  65.2 1.9 %broadcast_in_dim.25 = bf16[8,4,12,8,128]{4,3,2,1,0:T(8,128)(2,1)} broadcast(bf16[4,12,8,128]{3,2,1,0:T(8,128)(2,1)} %get-tuple-element.16), dimensions={1,2,3,4} | broadcast | bytes 884736 | tf_op jit(solution)/shard_map/broadcast_in_dim | solution.py:288
  67.1 0.0 copy-start.12
  67.1 3.7 %all-to-all-start.3 = ((bf16[8,4,12,8,128]{4,3,2,1,0:T(8,128)(2,1)}), bf16[8,4,12,8,128]{4,3,2,1,0:T(8,128)(2,1)S(1)}, u32[]{:S(2)}, u32[]{:S(2)}) async-start(bf16[8,4,12,8,128]{4,3,2,1,0:T(8,128)(2,1)} %broadcast_in_dim.25), calls=%async_computation.3 | async-start | bytes 1572864 | tf_op jit(solution)/shard_map/all_to_all | solution.py:285
  70.7 0.0 copy-done.12
  70.8 4.4 %collective-permute-start.2 = (bf16[12,8,128]{2,1,0:T(8,128)(2,1)S(1)}, bf16[12,8,128]{2,1,0:T(8,128)(2,1)S(1)}, u32[]{:S(2)}, u32[]{:S(2)}) collective-permute-start(bf16[12,8,128]{2,1,0:T(8,128)(2,1)S(1)} %copy-done.12), channel_id=1, source_target_pairs={{0,63},{1,2},{2,1},{3,4},{4,3},{5,6},{6,5},{7,8},{8,7},{9,10},{10,... | collective-permute-start | bytes 73736 | tf_op jit(solution)/shard_map/ppermute | solution.py:319
  75.2 1.9 %collective-permute-start.3 = (bf16[12,8,128]{2,1,0:T(8,128)(2,1)S(1)}, bf16[12,8,128]{2,1,0:T(8,128)(2,1)S(1)}, u32[]{:S(2)}, u32[]{:S(2)}) collective-permute-start(bf16[12,8,128]{2,1,0:T(8,128)(2,1)S(1)} %copy-done.12), channel_id=1, source_target_pairs={{0,1},{1,0},{2,3},{3,2},{4,5},{5,4},{6,7},{7,6},{8,9},{9,8},{10,11... | collective-permute-start | bytes 73736 | tf_op jit(solution)/shard_map/ppermute | solution.py:318
  77.1 2.4 %collective-permute-start.4 = (bf16[2,12,8,640]{3,2,1,0:T(8,128)(2,1)S(1)}, bf16[2,12,8,640]{3,2,1,0:T(8,128)(2,1)S(1)}, u32[]{:S(2)}, u32[]{:S(2)}) collective-permute-start(bf16[2,12,8,640]{3,2,1,0:T(8,128)(2,1)S(1)} %pad_maximum_fusion.rec), channel_id=1, source_target_pairs={{0,1},{1,0},{2,3},{3,2},{4,5},{5,4},{6,7},{7,6},{8,9},{9,8},{10,11... | collective-permute-start | bytes 737288 | tf_op jit(solution)/shard_map/ppermute | solution.py:320
  79.5 0.0 copy-done.3
  79.5 6.3 %collective-permute-start.5 = (bf16[2,12,8,640]{3,2,1,0:T(8,128)(2,1)S(1)}, bf16[2,12,8,640]{3,2,1,0:T(8,128)(2,1)S(1)}, u32[]{:S(2)}, u32[]{:S(2)}) collective-permute-start(bf16[2,12,8,640]{3,2,1,0:T(8,128)(2,1)S(1)} %pad_maximum_fusion.rec), channel_id=1, source_target_pairs={{0,63},{1,2},{2,1},{3,4},{4,3},{5,6},{6,5},{7,8},{8,7},{9,10},{10,... | collective-permute-start | bytes 737288 | tf_op jit(solution)/shard_map/ppermute | solution.py:321
  85.8 0.0 collective-permute-done.2
  85.8 0.0 collective-permute-done.3
  85.9 0.0 collective-permute-done.4.rec_partner
  85.9 0.0 copy-start.6
  85.9 8.2 %collective-permute-done.5.rec_beyond = bf16[2,12,8,640]{3,2,1,0:T(8,128)(2,1)S(1)} collective-permute-done((bf16[2,12,8,640]{3,2,1,0:T(8,128)(2,1)S(1)}, bf16[2,12,8,640]{3,2,1,0:T(8,128)(2,1)S(1)}, u32[]{:S(2)}, u32[]{:S(2)}) %collective-permute-start.5) | collective-permute-done | bytes 245792 | tf_op jit(solution)/shard_map/ppermute | solution.py:321
  94.1 0.0 copy-start.7
  94.1 0.0 all-to-all-done.3.ss
  94.1 0.0 copy-start.1
  94.1 1.1 broadcast_in_dim.26
  95.2 0.0 copy-done.6
  95.2 0.0 copy-done.7
  95.2 10.1 %all-to-all-start.4 = ((bf16[12,3,12,8,128]{4,3,2,1,0:T(8,128)(2,1)}), bf16[12,3,12,8,128]{4,3,2,1,0:T(8,128)(2,1)S(1)}, u32[]{:S(2)}, u32[]{:S(2)}) async-start(bf16[12,3,12,8,128]{4,3,2,1,0:T(8,128)(2,1)} %broadcast_in_dim.26), calls=%async_computation.4 | async-start | bytes 1769472 | tf_op jit(solution)/shard_map/all_to_all | solution.py:285
  105.3 1.9 %collective-permute-start.6 = (bf16[8,4,12,8,128]{4,3,2,1,0:T(8,128)(2,1)S(1)}, bf16[8,4,12,8,128]{4,3,2,1,0:T(8,128)(2,1)S(1)}, u32[]{:S(2)}, u32[]{:S(2)}) collective-permute-start(bf16[8,4,12,8,128]{4,3,2,1,0:T(8,128)(2,1)S(1)} %all-to-all-done.3.ss), channel_id=1, source_target_pairs={{0,1},{1,0},{2,3},{3,2},{4,5},{5,4},{6,7},{7,6},{8,9},{9,8},{10,11... | collective-permute-start | bytes 2359304 | tf_op jit(solution)/shard_map/ppermute | solution.py:328
  107.3 2.3 %collective-permute-done.6.sp = bf16[8,4,12,8,128]{4,3,2,1,0:T(8,128)(2,1)S(1)} collective-permute-done((bf16[8,4,12,8,128]{4,3,2,1,0:T(8,128)(2,1)S(1)}, bf16[8,4,12,8,128]{4,3,2,1,0:T(8,128)(2,1)S(1)}, u32[]{:S(2)}, u32[]{:S(2)}) %collective-permute-start.6) | collective-permute-done | bytes 786464 | tf_op jit(solution)/shard_map/ppermute | solution.py:328
  109.5 0.0 copy-done.1
  109.5 0.0 copy-start.4
  109.5 4.6 %collective-permute-start.7 = (bf16[12,8,128]{2,1,0:T(8,128)(2,1)S(1)}, bf16[12,8,128]{2,1,0:T(8,128)(2,1)S(1)}, u32[]{:S(2)}, u32[]{:S(2)}) collective-permute-start(bf16[12,8,128]{2,1,0:T(8,128)(2,1)S(1)} %get-tuple-element.25), channel_id=1, source_target_pairs={{64,0},{128,64},{192,128},{256,192},{320,256},{384,320},{448,384},... | collective-permute-start | bytes 73736 | tf_op jit(solution)/shard_map/ppermute | solution.py:331
  114.1 1.9 %collective-permute-start.8 = (bf16[12,8,128]{2,1,0:T(8,128)(2,1)S(1)}, bf16[12,8,128]{2,1,0:T(8,128)(2,1)S(1)}, u32[]{:S(2)}, u32[]{:S(2)}) collective-permute-start(bf16[12,8,128]{2,1,0:T(8,128)(2,1)S(1)} %get-tuple-element.24), channel_id=1, source_target_pairs={{0,64},{64,128},{128,192},{192,256},{256,320},{320,384},{384,448},... | collective-permute-start | bytes 73736 | tf_op jit(solution)/shard_map/ppermute | solution.py:332
  116.0 0.0 collective-permute-done.7.row_hi
  116.0 0.0 copy-start.10
  116.1 5.6 %collective-permute-done.8.row_lo = bf16[12,8,128]{2,1,0:T(8,128)(2,1)S(1)} collective-permute-done((bf16[12,8,128]{2,1,0:T(8,128)(2,1)S(1)}, bf16[12,8,128]{2,1,0:T(8,128)(2,1)S(1)}, u32[]{:S(2)}, u32[]{:S(2)}) %collective-permute-start.8) | collective-permute-done | bytes 24608 | tf_op jit(solution)/shard_map/ppermute | solution.py:332
  121.6 0.0 copy-start.11
  121.6 0.0 all-to-all-done.4.sr
  121.6 0.0 copy-done.4
  121.6 0.0 copy-done.10
  121.6 0.6 copy-done.11
  122.2 0.0 copy-start
  122.2 0.9 copy-done
  123.2 10.7 %shard_map.46 = (bf16[2,12,8,512]{3,2,1,0:T(8,128)(2,1)}, bf16[2,12,8,512]{3,2,1,0:T(8,128)(2,1)}) custom-call(s32[2]{0:T(128)} %pad_add_fusion.pos, bf16[2,12,8,640]{3,2,1,0:T(8,128)(2,1)} %copy-done.3, bf16[2,12,8,640]{3,2,1,0:T(8,128)(2,1)} %copy-done.6, bf16[2,12,8,640]{3,2,1,0:T(8,128)(2,1)} %copy-done.7, bf16[12,3,12,8,128]{4,3,2,1,0:T(8,128)(2,1)} %copy-done, ...), custom_call_target="tpu_custom_call" | custom-call | flops 1048576 | bytes 1048576 | tf_op jit(solution)/shard_map/pallas_call | solution.py:291
  (7 shorter events, 0.1 us)
Async XLA Ops:
  3.0 24.1 %copy-start.2 = (bf16[1,2,96,512]{3,2,1,0:T(8,128)(2,1)S(1)}, bf16[1,2,96,512]{3,2,1,0:T(8,128)(2,1)}, u32[]{:S(2)}) copy-start(bf16[1,2,96,512]{3,2,1,0:T(8,128)(2,1)} %param.2) | copy-start | bytes 589828
  3.0 15.0 %all-to-all-start = ((bf16[16,8,128]{2,1,0:T(8,128)(2,1)}), bf16[16,8,128]{2,1,0:T(8,128)(2,1)S(1)}, u32[]{:S(2)}, u32[]{:S(2)}) async-start(bf16[16,8,128]{2,1,0:T(8,128)(2,1)} %shard_map.41), calls=%async_computation | async-start | bytes 65536 | tf_op jit(solution)/shard_map/all_to_all | solution.py:285
  18.0 9.1 %copy-start.8 = (bf16[16,8,128]{2,1,0:T(8,128)(2,1)}, bf16[16,8,128]{2,1,0:T(8,128)(2,1)S(1)}, u32[]{:S(2)}) copy-start(bf16[16,8,128]{2,1,0:T(8,128)(2,1)S(1)} %all-to-all-done.from_rcv) | copy-start | bytes 98308
  18.0 15.6 %all-to-all-start.1 = ((bf16[12,8,128]{2,1,0:T(8,128)(2,1)}), bf16[12,8,128]{2,1,0:T(8,128)(2,1)S(1)}, u32[]{:S(2)}, u32[]{:S(2)}) async-start(bf16[12,8,128]{2,1,0:T(8,128)(2,1)} %shard_map.42), calls=%async_computation.1 | async-start | bytes 49152 | tf_op jit(solution)/shard_map/all_to_all | solution.py:285
  27.2 24.2 %collective-permute-start = (bf16[2,96,128]{2,1,0:T(8,128)(2,1)S(1)}, bf16[2,96,128]{2,1,0:T(8,128)(2,1)S(1)}, u32[]{:S(2)}, u32[]{:S(2)}) collective-permute-start(bf16[2,96,128]{2,1,0:T(8,128)(2,1)S(1)} %get-tuple-element.27), channel_id=1, source_target_pairs={{64,0},{128,64},{192,128},{256,192},{320,256},{384,320},{448,384},... | collective-permute-start | bytes 147464 | tf_op jit(solution)/shard_map/ppermute | solution.py:309
  31.7 19.6 %collective-permute-start.1 = (bf16[2,96,128]{2,1,0:T(8,128)(2,1)S(1)}, bf16[2,96,128]{2,1,0:T(8,128)(2,1)S(1)}, u32[]{:S(2)}, u32[]{:S(2)}) collective-permute-start(bf16[2,96,128]{2,1,0:T(8,128)(2,1)S(1)} %get-tuple-element.26), channel_id=1, source_target_pairs={{0,64},{64,128},{128,192},{192,256},{256,320},{320,384},{384,448},... | collective-permute-start | bytes 147464 | tf_op jit(solution)/shard_map/ppermute | solution.py:310
  33.7 0.6 copy-start.9
  37.5 25.3 %all-to-all-start.2 = ((bf16[4,24,8,128]{3,2,1,0:T(8,128)(2,1)}), bf16[4,24,8,128]{3,2,1,0:T(8,128)(2,1)S(1)}, u32[]{:S(2)}, u32[]{:S(2)}) async-start(bf16[4,24,8,128]{3,2,1,0:T(8,128)(2,1)} %shard_map.44), calls=%async_computation.2 | async-start | bytes 393216 | tf_op jit(solution)/shard_map/all_to_all | solution.py:285
  51.4 28.1 %copy-start.3 = (bf16[2,12,8,640]{3,2,1,0:T(8,128)(2,1)}, bf16[2,12,8,640]{3,2,1,0:T(8,128)(2,1)S(1)}, u32[]{:S(2)}) copy-start(bf16[2,12,8,640]{3,2,1,0:T(8,128)(2,1)S(1)} %pad_maximum_fusion.rec) | copy-start | bytes 737284
  62.8 0.7 copy-start.5
  67.1 3.7 %copy-start.12 = (bf16[12,8,128]{2,1,0:T(8,128)(2,1)S(1)}, bf16[12,8,128]{2,1,0:T(8,128)(2,1)}, u32[]{:S(2)}) copy-start(bf16[12,8,128]{2,1,0:T(8,128)(2,1)} %get-tuple-element.17) | copy-start | bytes 73732
  67.1 27.0 %all-to-all-start.3 = ((bf16[8,4,12,8,128]{4,3,2,1,0:T(8,128)(2,1)}), bf16[8,4,12,8,128]{4,3,2,1,0:T(8,128)(2,1)S(1)}, u32[]{:S(2)}, u32[]{:S(2)}) async-start(bf16[8,4,12,8,128]{4,3,2,1,0:T(8,128)(2,1)} %broadcast_in_dim.25), calls=%async_computation.3 | async-start | bytes 1572864 | tf_op jit(solution)/shard_map/all_to_all | solution.py:285
  70.8 15.1 %collective-permute-start.2 = (bf16[12,8,128]{2,1,0:T(8,128)(2,1)S(1)}, bf16[12,8,128]{2,1,0:T(8,128)(2,1)S(1)}, u32[]{:S(2)}, u32[]{:S(2)}) collective-permute-start(bf16[12,8,128]{2,1,0:T(8,128)(2,1)S(1)} %copy-done.12), channel_id=1, source_target_pairs={{0,63},{1,2},{2,1},{3,4},{4,3},{5,6},{6,5},{7,8},{8,7},{9,10},{10,... | collective-permute-start | bytes 73736 | tf_op jit(solution)/shard_map/ppermute | solution.py:319
  75.2 10.7 %collective-permute-start.3 = (bf16[12,8,128]{2,1,0:T(8,128)(2,1)S(1)}, bf16[12,8,128]{2,1,0:T(8,128)(2,1)S(1)}, u32[]{:S(2)}, u32[]{:S(2)}) collective-permute-start(bf16[12,8,128]{2,1,0:T(8,128)(2,1)S(1)} %copy-done.12), channel_id=1, source_target_pairs={{0,1},{1,0},{2,3},{3,2},{4,5},{5,4},{6,7},{7,6},{8,9},{9,8},{10,11... | collective-permute-start | bytes 73736 | tf_op jit(solution)/shard_map/ppermute | solution.py:318
  77.1 8.8 %collective-permute-start.4 = (bf16[2,12,8,640]{3,2,1,0:T(8,128)(2,1)S(1)}, bf16[2,12,8,640]{3,2,1,0:T(8,128)(2,1)S(1)}, u32[]{:S(2)}, u32[]{:S(2)}) collective-permute-start(bf16[2,12,8,640]{3,2,1,0:T(8,128)(2,1)S(1)} %pad_maximum_fusion.rec), channel_id=1, source_target_pairs={{0,1},{1,0},{2,3},{3,2},{4,5},{5,4},{6,7},{7,6},{8,9},{9,8},{10,11... | collective-permute-start | bytes 737288 | tf_op jit(solution)/shard_map/ppermute | solution.py:320
  79.5 14.5 %collective-permute-start.5 = (bf16[2,12,8,640]{3,2,1,0:T(8,128)(2,1)S(1)}, bf16[2,12,8,640]{3,2,1,0:T(8,128)(2,1)S(1)}, u32[]{:S(2)}, u32[]{:S(2)}) collective-permute-start(bf16[2,12,8,640]{3,2,1,0:T(8,128)(2,1)S(1)} %pad_maximum_fusion.rec), channel_id=1, source_target_pairs={{0,63},{1,2},{2,1},{3,4},{4,3},{5,6},{6,5},{7,8},{8,7},{9,10},{10,... | collective-permute-start | bytes 737288 | tf_op jit(solution)/shard_map/ppermute | solution.py:321
  85.9 9.3 %copy-start.6 = (bf16[2,12,8,640]{3,2,1,0:T(8,128)(2,1)}, bf16[2,12,8,640]{3,2,1,0:T(8,128)(2,1)S(1)}, u32[]{:S(2)}) copy-start(bf16[2,12,8,640]{3,2,1,0:T(8,128)(2,1)S(1)} %collective-permute-done.4.rec_partner) | copy-start | bytes 737284
  94.1 1.2 copy-start.7
  94.1 15.5 %copy-start.1 = (bf16[8,4,12,8,128]{4,3,2,1,0:T(8,128)(2,1)}, bf16[8,4,12,8,128]{4,3,2,1,0:T(8,128)(2,1)S(1)}, u32[]{:S(2)}) copy-start(bf16[8,4,12,8,128]{4,3,2,1,0:T(8,128)(2,1)S(1)} %all-to-all-done.3.ss) | copy-start | bytes 2359300
  95.2 26.4 %all-to-all-start.4 = ((bf16[12,3,12,8,128]{4,3,2,1,0:T(8,128)(2,1)}), bf16[12,3,12,8,128]{4,3,2,1,0:T(8,128)(2,1)S(1)}, u32[]{:S(2)}, u32[]{:S(2)}) async-start(bf16[12,3,12,8,128]{4,3,2,1,0:T(8,128)(2,1)} %broadcast_in_dim.26), calls=%async_computation.4 | async-start | bytes 1769472 | tf_op jit(solution)/shard_map/all_to_all | solution.py:285
  105.3 4.2 %collective-permute-start.6 = (bf16[8,4,12,8,128]{4,3,2,1,0:T(8,128)(2,1)S(1)}, bf16[8,4,12,8,128]{4,3,2,1,0:T(8,128)(2,1)S(1)}, u32[]{:S(2)}, u32[]{:S(2)}) collective-permute-start(bf16[8,4,12,8,128]{4,3,2,1,0:T(8,128)(2,1)S(1)} %all-to-all-done.3.ss), channel_id=1, source_target_pairs={{0,1},{1,0},{2,3},{3,2},{4,5},{5,4},{6,7},{7,6},{8,9},{9,8},{10,11... | collective-permute-start | bytes 2359304 | tf_op jit(solution)/shard_map/ppermute | solution.py:328
  109.5 12.1 %copy-start.4 = (bf16[8,4,12,8,128]{4,3,2,1,0:T(8,128)(2,1)}, bf16[8,4,12,8,128]{4,3,2,1,0:T(8,128)(2,1)S(1)}, u32[]{:S(2)}) copy-start(bf16[8,4,12,8,128]{4,3,2,1,0:T(8,128)(2,1)S(1)} %collective-permute-done.6.sp) | copy-start | bytes 2359300
  109.5 6.5 %collective-permute-start.7 = (bf16[12,8,128]{2,1,0:T(8,128)(2,1)S(1)}, bf16[12,8,128]{2,1,0:T(8,128)(2,1)S(1)}, u32[]{:S(2)}, u32[]{:S(2)}) collective-permute-start(bf16[12,8,128]{2,1,0:T(8,128)(2,1)S(1)} %get-tuple-element.25), channel_id=1, source_target_pairs={{64,0},{128,64},{192,128},{256,192},{320,256},{384,320},{448,384},... | collective-permute-start | bytes 73736 | tf_op jit(solution)/shard_map/ppermute | solution.py:331
  114.1 7.5 %collective-permute-start.8 = (bf16[12,8,128]{2,1,0:T(8,128)(2,1)S(1)}, bf16[12,8,128]{2,1,0:T(8,128)(2,1)S(1)}, u32[]{:S(2)}, u32[]{:S(2)}) collective-permute-start(bf16[12,8,128]{2,1,0:T(8,128)(2,1)S(1)} %get-tuple-element.24), channel_id=1, source_target_pairs={{0,64},{64,128},{128,192},{192,256},{256,320},{320,384},{384,448},... | collective-permute-start | bytes 73736 | tf_op jit(solution)/shard_map/ppermute | solution.py:332
  116.0 5.6 %copy-start.10 = (bf16[12,8,128]{2,1,0:T(8,128)(2,1)}, bf16[12,8,128]{2,1,0:T(8,128)(2,1)S(1)}, u32[]{:S(2)}) copy-start(bf16[12,8,128]{2,1,0:T(8,128)(2,1)S(1)} %collective-permute-done.7.row_hi) | copy-start | bytes 73732
  121.6 0.6 copy-start.11
  122.2 0.9 copy-start

commit v3 on v2

--- a/solution.py
+++ b/solution.py
@@ -24,7 +24,20 @@
     return [pl.BlockSpec(memory_space=pltpu.SMEM)] * count
 
 
-def pick_behind_kernel(pos, panel, rec, to_src):
+def position():
+    return lax.axis_index("src"), lax.axis_index("rcv")
+
+
+def replicate(source, target, sems):
+    copies = [pltpu.make_async_copy(source, target.at[n], sems.at[n]) for n in range(target.shape[0])]
+    for copy in copies:
+        copy.start()
+    for copy in copies:
+        copy.wait()
+
+
+def pick_behind_kernel(panel, rec, to_src):
+    pos = position()
     lane = lax.broadcasted_iota(jnp.int32, (1, 128), 1)
     early = pos[0] < 8
     key_part = jnp.where(early, lane % 8 // 4, lane // 64)
@@ -41,7 +54,8 @@
     to_src[...] = total.astype(BF16).reshape(NA, 8, 128)
 
 
-def pick_front_kernel(pos, panel, rec, to_rcv):
+def pick_front_kernel(panel, rec, to_rcv):
+    pos = position()
     lane = lax.broadcasted_iota(jnp.int32, (1, 128), 1)
     kind, slot, run_z = lane % 32 // 8, lane % 8, lane // 32
     run = jnp.where(kind < 2, slot, jnp.where(kind == 2, 8 + slot % 4, NA))
@@ -86,7 +100,8 @@
             behind[6 * part + 3 * pair + 2] = acc.astype(BF16)
 
 
-def order_kernel(pos, from_rcv, behind, out):
+def order_kernel(from_rcv, behind, out):
+    pos = position()
     lane = lax.broadcasted_iota(jnp.int32, (8, 128), 1)
     tiles = [from_rcv[p].astype(F32) for p in range(NP)]
     odd = pos[1] // NP % 2 == 1
@@ -109,8 +124,9 @@
         out[copy, TILES:] = behind[...]
 
 
-def average_kernel(pos, pieces, rows, own):
-    low = lax.broadcasted_iota(jnp.int32, (8, 128), 1) < 64
+def average_kernel(pieces, rec, next_src, last_src, out, near, rows, sems):
+    lane = lax.broadcasted_iota(jnp.int32, (8, 128), 1)
+    low = lane < 64
     for z in range(NZ):
         for tile in range(TILES):
             part, pair, kind = tile // 6, tile % 6 // 3, tile % 3
@@ -120,7 +136,31 @@
                 even, odd = [pieces[2 * pair + n, 3 * z + 2].astype(F32) for n in range(2)]
                 front = pltpu.roll(jnp.where(low, odd, even), 64, 1) if part else jnp.where(low, even, odd)
             rows[z, tile] = ((front + pieces[z, TILES + tile].astype(F32)) * 0.5).astype(BF16)
-    own[...] = rows[pos[1] // NP]
+    copies = [pltpu.make_async_copy(rows, out.at[n], sems.at[n]) for n in range(NY)]
+    for copy in copies:
+        copy.start()
+    near[:TILES] = rows[position()[1] // NP]
+    for part in range(2):
+        for a in range(NA):
+            first = TILES + (part * NA + a) * (EXT // 128)
+            run = slice(8 * a, 8 * a + 8)
+            for n in range(EXT // 128 - 1):
+                near[first + n] = rec[part, run, 128 * n : 128 * n + 128]
+            after, before = next_src[part, run].astype(F32), last_src[part, run].astype(F32)
+            rim = jnp.where(lane < 8, after, jnp.where(lane >= 120, before, jnp.zeros_like(before)))
+            near[first + EXT // 128 - 1] = rim.astype(BF16)
+    for copy in copies:
+        copy.wait()
+
+
+def stack_kernel(near, partner, beyond, out, rows, sems):
+    core = position()[1] % 2
+    for t in range(TILES):
+        one, two = partner[t].astype(F32), beyond[t].astype(F32)
+        rows[0, t] = jnp.where(core == 0, two, one).astype(BF16)
+        rows[1, t] = near[t]
+        rows[2, t] = jnp.where(core == 0, one, two).astype(BF16)
+    replicate(rows, out, sems)
 
 
 def bounds(rcv):
@@ -161,25 +201,7 @@
         target[:, :, :, 128 * n : 128 * (n + width)] = total.reshape(*target.shape[:3], 128 * width)
 
 
-def final_kernel(pos, rec, rec_partner, rec_beyond, sr, ss, sp, row_hi, row_lo, prim, mult, a_rows, b_rows, pred, once, box):
-    rcv = pos[1]
-    core = rcv % 2
-    first, last = bounds(rcv)
-
-    def gather(z, _):
-        for t in range(TILES):
-            mine, theirs = ss[:, z, t].astype(F32), sp[:, z, t].astype(F32)
-            zero = jnp.where(core == 0, mine, theirs)
-            one = jnp.where(core == 0, theirs, mine)
-            x = jnp.stack([zero, one], axis=1).reshape(128, 128)
-            b_rows[z, :, 128 * t : 128 * t + 128] = x.astype(BF16)
-        return 0
-
-    lax.fori_loop(0, NZ, gather, 0)
-    for t in range(TILES):
-        x = jnp.concatenate([row_hi[t].astype(F32), jnp.zeros((112, 128), F32), row_lo[t].astype(F32)], axis=0)
-        b_rows[NZ, :, 128 * t : 128 * t + 128] = x.astype(BF16)
-
+def spread_rows(sr, a_rows, first, last):
     def spread(a, _):
         lo, hi, keep_lo, keep_hi = neighbours(a, first, last)
         for t in range(TILES):
@@ -190,28 +212,76 @@
         return 0
 
     lax.fori_loop(0, NA, spread, 0, unroll=2)
-    half = 64 * TILES
     left = a_rows[...].reshape(24 * NA, 128 * TILES)
-    left = left[:, :half], left[:, half:]
-
-    def times(x, y):
-        return lax.dot_general(x, y, (((1,), (1,)), ((), ())), preferred_element_type=F32)
-
-    for n in range(NZ + 1):
-        right = b_rows[n, :, :half], b_rows[n, :, half:]
-        value = times(left[0], right[0]) - times(left[1], right[1])
-        pred[0, :, :, 128 * n : 128 * n + 128] = value.reshape(NA, 24, 128)
-        value = times(left[0], right[1]) + times(left[1], right[0])
-        pred[1, :, :, 128 * n : 128 * n + 128] = value.reshape(NA, 24, 128)
+    return left[:, : 64 * TILES], left[:, 64 * TILES :]
+
+
+def times(x, y):
+    return lax.dot_general(x, y, (((1,), (1,)), ((), ())), preferred_element_type=F32)
+
+
+def predict_kernel(sr, ss, sp, guess, mult, a_rows, b_rows):
+    rcv = position()[1]
+    core = rcv % 2
+    left = spread_rows(sr, a_rows, *bounds(rcv))
+    for z in range(NZ):
+        for t in range(TILES):
+            mine, theirs = ss[:, z, t].astype(F32), sp[:, z, t].astype(F32)
+            zero = jnp.where(core == 0, mine, theirs)
+            one = jnp.where(core == 0, theirs, mine)
+            x = jnp.stack([zero, one], axis=1).reshape(128, 128)
+            b_rows[128 * z : 128 * z + 128, 128 * t : 128 * t + 128] = x.astype(BF16)
+    for n in range(NZ // 2):
+        cols = slice(256 * n, 256 * n + 256)
+        right = b_rows[cols, : 64 * TILES], b_rows[cols, 64 * TILES :]
+        value = (
+            times(left[0], right[0]) - times(left[1], right[1]),
+            times(left[0], right[1]) + times(left[1], right[0]),
+        )
+        for part in range(2):
+            full = value[part].reshape(NA, 24, 256)
+            guess[part, :, :, cols] = full.astype(BF16)
+            mult[part, :, :, cols] = (full[:, 8:16] * (768.0 ** -0.5)).astype(BF16)
+
+
+def subtract_kernel(near, near_partner, near_beyond, guess, sr, row_hi, row_lo, prim, a_rows, edge, once, box):
+    rcv = position()[1]
+    core = rcv % 2
+    first, last = bounds(rcv)
+    left = spread_rows(sr, a_rows, first, last)
+    right = []
+    for part in range(2):
+        tiles = range(6 * part, 6 * part + 6)
+        right.append(
+            jnp.concatenate(
+                [
+                    jnp.concatenate([row_hi[t].astype(F32) for t in tiles], axis=1),
+                    jnp.zeros((112, 64 * TILES), F32),
+                    jnp.concatenate([row_lo[t].astype(F32) for t in tiles], axis=1),
+                ],
+                axis=0,
+            ).astype(BF16)
+        )
+    straight = times(left[0], jnp.concatenate(right, axis=0))
+    crossed = times(left[1], jnp.concatenate(right[::-1], axis=0))
+    edge[0] = (straight[:, :128] - crossed[:, :128]).astype(BF16).astype(F32).reshape(NA, 24, 128)
+    edge[1] = (straight[:, 128:] + crossed[:, 128:]).astype(BF16).astype(F32).reshape(NA, 24, 128)
+
+    def run_of(ref, part, a):
+        start = TILES + (part * NA + a) * (EXT // 128)
+        return jnp.concatenate([ref[start + n].astype(F32) for n in range(EXT // 128)], axis=1)
 
     def data_of(a):
         lo, hi, keep_lo, keep_hi = neighbours(a, first, last)
         data = []
         for part in range(2):
-            below, _ = sides(core, rec_partner[part, lo].astype(F32), rec_beyond[part, lo].astype(F32))
-            _, above = sides(core, rec_partner[part, hi].astype(F32), rec_beyond[part, hi].astype(F32))
-            data.append(jnp.concatenate([below * keep_lo, rec[part, a].astype(F32), above * keep_hi], axis=0))
+            below, _ = sides(core, run_of(near_partner, part, lo), run_of(near_beyond, part, lo))
+            _, above = sides(core, run_of(near_partner, part, hi), run_of(near_beyond, part, hi))
+            data.append(jnp.concatenate([below * keep_lo, run_of(near, part, a), above * keep_hi], axis=0))
         return data
+
+    def guess_of(a):
+        return [jnp.concatenate([guess[part, a].astype(F32), edge[part, a]], axis=1) for part in range(2)]
 
     def terms_of(dr, di, pr, pi):
         return pr * dr + pi * di, pr * di - pi * dr, pr * pr + pi * pi
@@ -223,15 +293,8 @@
 
     def first_sweep(a, _):
         dr, di = data_of(a)
-        guess = []
-        for part in range(2):
-            full = pred[part, a]
-            mult[part, a] = (full[8:16, :512] * (768.0 ** -0.5)).astype(BF16)
-            full = full.astype(BF16).astype(F32)
-            pred[part, a] = full
-            guess.append(full)
         weight = 1.5 - jnp.tanh(dr * dr + di * di)
-        for n, q in enumerate(terms_of(dr, di, *guess)):
+        for n, q in enumerate(terms_of(dr, di, *guess_of(a))):
             once[n, a] = windows_rows(weight * q, 16)
         return 0
 
@@ -241,8 +304,7 @@
     windows_lanes(once, box, band, (0, 2, 4))
 
     def second_sweep(a, _):
-        dr, di = [v[4:20] for v in data_of(a)]
-        pr, pi = pred[0, a, 4:20], pred[1, a, 4:20]
+        dr, di, pr, pi = [v[4:20] for v in (*data_of(a), *guess_of(a))]
         er, ei = subtract(dr, di, pr, pi, [box[n, a] for n in range(3)])
         weight = 1.5 - jnp.tanh(er * er + ei * ei)
         for n, q in enumerate(terms_of(dr, di, pr, pi)):
@@ -253,8 +315,8 @@
     windows_lanes(once.at[:, :, :8], box.at[:, :, :8], band, (0, 2))
 
     def finish(a, _):
-        dr, di = rec[0, a, :, :512].astype(F32), rec[1, a, :, :512].astype(F32)
-        pr, pi = pred[0, a, 8:16, :512], pred[1, a, 8:16, :512]
+        dr, di = [run_of(near, part, a)[:, :512] for part in range(2)]
+        pr, pi = [guess[part, a].astype(F32)[8:16] for part in range(2)]
         er, ei = subtract(dr, di, pr, pi, [box[n, a, :8, :512] for n in range(3)])
         prim[0, a], prim[1, a] = er.astype(BF16), ei.astype(BF16)
         return 0
@@ -272,8 +334,7 @@
 
 def block(record, panel_offset):
     src_count, rcv_count = lax.axis_size("src"), lax.axis_size("rcv")
-    src, rcv = lax.axis_index("src"), lax.axis_index("rcv")
-    pos = jnp.stack([src, rcv]).astype(jnp.int32)
+    rcv = lax.axis_index("rcv")
     rec = record[0]
     plane = [[z * NP + p for p in range(NP)] for z in range(NZ)]
     column = [[z * NP + p for z in range(NZ)] for p in range(NP)]
@@ -284,64 +345,78 @@
     def exchange(x, axis, groups=None):
         return lax.all_to_all(x, axis, split_axis=0, concat_axis=0, tiled=True, axis_index_groups=groups)
 
-    def copies(x, count, axis, groups=None):
-        return exchange(jnp.broadcast_to(x, (count, *x.shape)), axis, groups)
-
-    def kernel(body, outs, scalars, arrays, scratch=(), flops=1 << 20, moved=1 << 20):
+    def kernel(body, outs, scalars, arrays, scratch=(), flops=1 << 20, limit=8 << 20, spaces=None):
+        spaces = spaces or jax.tree.map(lambda _: pltpu.VMEM, outs)
         return pl.pallas_call(
             body,
             out_shape=outs,
             in_specs=smem(len(scalars)) + vmem(len(arrays)),
-            out_specs=jax.tree.map(lambda _: vmem(1)[0], outs),
+            out_specs=jax.tree.map(lambda m: pl.BlockSpec(memory_space=m), spaces),
             scratch_shapes=scratch,
-            cost_estimate=pl.CostEstimate(flops=flops, bytes_accessed=moved, transcendentals=0),
+            compiler_params=pltpu.CompilerParams(vmem_limit_bytes=limit),
+            cost_estimate=pl.CostEstimate(flops=flops, bytes_accessed=1 << 20, transcendentals=0),
         )(*scalars, *arrays)
 
-    to_src = kernel(pick_behind_kernel, shape(NA, 8, 128), (pos, panel_offset), (rec,))
+    to_src = kernel(pick_behind_kernel, shape(NA, 8, 128), (panel_offset,), (rec,))
     from_src = exchange(to_src, "src")
-    to_rcv = kernel(pick_front_kernel, shape(NP, 8, 128), (pos, panel_offset), (rec,))
+    to_rcv = kernel(pick_front_kernel, shape(NP, 8, 128), (panel_offset,), (rec,))
     from_rcv = exchange(to_rcv, "rcv", plane)
     behind = kernel(order_behind_kernel, shape(TILES, 8, 128), (), (from_src,))
-    message = kernel(order_kernel, shape(NZ, 2 * TILES, 8, 128), (pos,), (from_rcv, behind))
+    message = kernel(order_kernel, shape(NZ, 2 * TILES, 8, 128), (), (from_rcv, behind))
     pieces = exchange(message, "rcv", column)
     held, _ = lax.optimization_barrier((rec, from_rcv))
     first_tile, last_tile = held[:, :, :128], held[:, :, 384:]
     next_src = lax.ppermute(first_tile, "src", ring(src_count, -1, False))
     last_src = lax.ppermute(last_tile, "src", ring(src_count, 1, False))
-    lane = lax.broadcasted_iota(jnp.int32, (1, 1, 128), 2)
-    rim = jnp.where(lane < 8, next_src, jnp.where(lane >= 120, last_src, jnp.zeros_like(last_src)))
-    wide = jnp.concatenate([rec, rim], axis=2).reshape(2, NA, 8, EXT)
-    pieces, wide = lax.optimization_barrier((pieces, wide))
-    rows, own = kernel(average_kernel, (shape(NZ, TILES, 8, 128), shape(TILES, 8, 128)), (pos,), (pieces,))
-    ss = copies(rows, NY, "rcv", line)
-    near = own
-    own_partner = lax.ppermute(near, "rcv", swap)
-    own_beyond = lax.ppermute(near, "rcv", beyond)
-    wide_partner = lax.ppermute(wide, "rcv", swap)
-    wide_beyond = lax.ppermute(wide, "rcv", beyond)
+    spread, near = kernel(
+        average_kernel,
+        (shape(NY, NZ, TILES, 8, 128), shape(TILES + 2 * NA * (EXT // 128), 8, 128)),
+        (),
+        (pieces, rec, next_src, last_src),
+        [pltpu.VMEM((NZ, TILES, 8, 128), BF16), pltpu.SemaphoreType.DMA((NY,))],
+        spaces=(pltpu.HBM, pltpu.VMEM),
+    )
+    ss = exchange(spread, "rcv", line)
+    near_partner = lax.ppermute(near, "rcv", swap)
+    near_beyond = lax.ppermute(near, "rcv", beyond)
+    stacked = kernel(
+        stack_kernel,
+        shape(src_count, 3, TILES, 8, 128),
+        (),
+        (near, near_partner, near_beyond),
+        [pltpu.VMEM((3, TILES, 8, 128), BF16), pltpu.SemaphoreType.DMA((src_count,))],
+        spaces=pltpu.HBM,
+    )
+    ss, stacked = lax.optimization_barrier((ss, stacked))
+    sr = exchange(stacked, "src")
+    sp = lax.ppermute(ss, "rcv", swap)
     even_core = rcv % 2 == 0
-    own = jnp.stack(
-        [jnp.where(even_core, own_beyond, own_partner), own, jnp.where(even_core, own_partner, own_beyond)]
-    )
-    ss, own, wide_partner, wide_beyond = lax.optimization_barrier((ss, own, wide_partner, wide_beyond))
-    sr = copies(own, src_count, "src")
-    sp = lax.ppermute(ss, "rcv", swap)
     row_first = jnp.where(even_core, ss[0, 0], sp[0, 0])
     row_last = jnp.where(even_core, sp[NY - 1, NZ - 1], ss[NY - 1, NZ - 1])
     row_hi = lax.ppermute(row_first, "src", ring(src_count, -1, False))
     row_lo = lax.ppermute(row_last, "src", ring(src_count, 1, False))
-    prim, mult = kernel(
-        final_kernel,
-        (shape(2, NA, 8, 512),) * 2,
-        (pos,),
-        (wide, wide_partner, wide_beyond, sr, ss, sp, row_hi, row_lo),
+    guess, mult = kernel(
+        predict_kernel,
+        (shape(2, NA, 24, 512), shape(2, NA, 8, 512)),
+        (),
+        (sr, ss, sp),
+        [pltpu.VMEM((NA, 24, 128 * TILES), BF16), pltpu.VMEM((512, 128 * TILES), BF16)],
+        flops=1 << 32,
+        limit=16 << 20,
+    )
+    prim = kernel(
+        subtract_kernel,
+        shape(2, NA, 8, 512),
+        (),
+        (near, near_partner, near_beyond, guess, sr, row_hi, row_lo),
         [
             pltpu.VMEM((NA, 24, 128 * TILES), BF16),
-            pltpu.VMEM((NZ + 1, 128, 128 * TILES), BF16),
-            pltpu.VMEM((2, NA, 24, EXT), F32),
+            pltpu.VMEM((2, NA, 24, 128), F32),
             pltpu.VMEM((3, NA, 16, EXT), F32),
             pltpu.VMEM((3, NA, 16, EXT), F32),
         ],
+        flops=1 << 32,
+        limit=20 << 20,
     )
     return prim.reshape(record.shape), mult.reshape(record.shape)
 

time: 135 us -> 121 us (0.90)
  the two profiles are of different devices: /device:TPU:6 before, /device:TPU:192 now
where the time goes in v3:
time: 121 us; the launch traced here: 120 us
  starting transfers between devices  53.6 us (44%)
  waiting for transfers between devices  50.2 us (41%)
  Pallas kernels  14 us (12%)
  local copies, waits for them, and re-layouts  1.63 us (1%)
    all_to_all x5, starting transfers between devices, exchange(): lax.all_to_all(x, axis, split_axis=0, concat_axis=0, tiled=True, axis_ind...  34.7 us
    all_to_all x5, waiting for transfers between devices, exchange(): lax.all_to_all(x, axis, split_axis=0, concat_axis=0, tiled=True, axis_ind...  29.8 us
    pallas_call x8, Pallas kernels, kernel(): pl.pallas_call(body, out_shape=outs, in_specs=smem(len(scalars)) + vmem(l...  14 us
    ppermute x1, waiting for transfers between devices, block(): near_beyond = lax.ppermute(near, 'rcv', beyond)  11.2 us
    ppermute x1, waiting for transfers between devices, block(): next_src = lax.ppermute(first_tile, 'src', ring(src_count, -1, False))  6.89 us
    ppermute x1, starting transfers between devices, block(): row_lo = lax.ppermute(row_last, 'src', ring(src_count, 1, False))  4.84 us
    ppermute x1, starting transfers between devices, block(): near_partner = lax.ppermute(near, 'rcv', swap)  3.87 us
    ppermute x1, starting transfers between devices, block(): last_src = lax.ppermute(last_tile, 'src', ring(src_count, 1, False))  3.1 us
  transfers between devices with their start and end apart: 12, of which 8 were waited for; matrix products, arithmetic and copies ran while one was open for 0% of the time, Pallas kernels for 4%

profile of v3, /device:TPU:192, one launch (start us, length us, event | category | flops | bytes accessed | tf_op | source)
XLA Modules:
  0.0 120.2 jit_solution(14764947427311830873)
XLA Ops:
  0.6 0.0 copy-start
  0.6 0.9 copy-done
  1.6 0.0 copy-start.2
  1.6 0.7 copy-done.2
  2.2 0.0 copy-start.1
  2.2 1.5 %shard_map.42 = bf16[12,8,128]{2,1,0:T(8,128)(2,1)} custom-call(s32[768]{0:T(1024)S(1)} %copy-done.2, bf16[2,96,512]{2,1,0:T(8,128)(2,1)S(1)} %bitcast.7), custom_call_target="tpu_custom_call" | custom-call | flops 1048576 | bytes 1048576 | tf_op jit(solution)/shard_map/pallas_call | solution.py:350
  3.7 0.0 copy-start.3
  3.7 9.3 %all-to-all-start.1 = ((bf16[12,8,128]{2,1,0:T(8,128)(2,1)}), bf16[12,8,128]{2,1,0:T(8,128)(2,1)S(1)}, u32[]{:S(2)}, u32[]{:S(2)}) async-start(bf16[12,8,128]{2,1,0:T(8,128)(2,1)} %shard_map.42), calls=%async_computation.1 | async-start | bytes 49152 | tf_op jit(solution)/shard_map/all_to_all | solution.py:346
  13.0 0.0 copy-done.1
  13.0 0.0 copy-done.3
  13.0 1.5 %shard_map.41 = bf16[16,8,128]{2,1,0:T(8,128)(2,1)} custom-call(s32[768]{0:T(1024)S(1)} %copy-done.3, bf16[2,96,512]{2,1,0:T(8,128)(2,1)S(1)} %bitcast.8), custom_call_target="tpu_custom_call" | custom-call | flops 1048576 | bytes 1048576 | tf_op jit(solution)/shard_map/pallas_call | solution.py:350
  14.5 6.9 %all-to-all-done.1.from_src = bf16[12,8,128]{2,1,0:T(8,128)(2,1)S(1)} async-done(((bf16[12,8,128]{2,1,0:T(8,128)(2,1)}), bf16[12,8,128]{2,1,0:T(8,128)(2,1)S(1)}, u32[]{:S(2)}, u32[]{:S(2)}) %all-to-all-start.1) | async-done | bytes 24608 | tf_op jit(solution)/shard_map/all_to_all | solution.py:346
  21.4 7.2 %all-to-all-start = ((bf16[16,8,128]{2,1,0:T(8,128)(2,1)}), bf16[16,8,128]{2,1,0:T(8,128)(2,1)S(1)}, u32[]{:S(2)}, u32[]{:S(2)}) async-start(bf16[16,8,128]{2,1,0:T(8,128)(2,1)} %shard_map.41), calls=%async_computation | async-start | bytes 65536 | tf_op jit(solution)/shard_map/all_to_all | solution.py:346
  28.6 0.1 shard_map.43.behind
  28.8 7.6 %all-to-all-done.from_rcv = bf16[16,8,128]{2,1,0:T(8,128)(2,1)S(1)} async-done(((bf16[16,8,128]{2,1,0:T(8,128)(2,1)}), bf16[16,8,128]{2,1,0:T(8,128)(2,1)S(1)}, u32[]{:S(2)}, u32[]{:S(2)}) %all-to-all-start) | async-done | bytes 32800 | tf_op jit(solution)/shard_map/all_to_all | solution.py:346
  36.3 1.0 shard_map.44
  37.3 9.9 %all-to-all-start.2 = ((bf16[4,24,8,128]{3,2,1,0:T(8,128)(2,1)}), bf16[4,24,8,128]{3,2,1,0:T(8,128)(2,1)S(1)}, u32[]{:S(2)}, u32[]{:S(2)}) async-start(bf16[4,24,8,128]{3,2,1,0:T(8,128)(2,1)} %shard_map.44), calls=%async_computation.2 | async-start | bytes 393216 | tf_op jit(solution)/shard_map/all_to_all | solution.py:346
  47.3 3.1 %collective-permute-start.1 = (bf16[2,96,128]{2,1,0:T(8,128)(2,1)S(1)}, bf16[2,96,128]{2,1,0:T(8,128)(2,1)S(1)}, u32[]{:S(2)}, u32[]{:S(2)}) collective-permute-start(bf16[2,96,128]{2,1,0:T(8,128)(2,1)S(1)} %get-tuple-element.18), channel_id=1, source_target_pairs={{0,64},{64,128},{128,192},{192,256},{256,320},{320,384},{384,448},... | collective-permute-start | bytes 147464 | tf_op jit(solution)/shard_map/ppermute | solution.py:370
  50.4 1.3 %collective-permute-start = (bf16[2,96,128]{2,1,0:T(8,128)(2,1)S(1)}, bf16[2,96,128]{2,1,0:T(8,128)(2,1)S(1)}, u32[]{:S(2)}, u32[]{:S(2)}) collective-permute-start(bf16[2,96,128]{2,1,0:T(8,128)(2,1)S(1)} %get-tuple-element.19), channel_id=1, source_target_pairs={{64,0},{128,64},{192,128},{256,192},{320,256},{384,320},{448,384},... | collective-permute-start | bytes 147464 | tf_op jit(solution)/shard_map/ppermute | solution.py:369
  51.7 0.5 collective-permute-done.1.last_src
  52.2 6.9 %collective-permute-done.next_src = bf16[2,96,128]{2,1,0:T(8,128)(2,1)S(1)} collective-permute-done((bf16[2,96,128]{2,1,0:T(8,128)(2,1)S(1)}, bf16[2,96,128]{2,1,0:T(8,128)(2,1)S(1)}, u32[]{:S(2)}, u32[]{:S(2)}) %collective-permute-start) | collective-permute-done | bytes 49184 | tf_op jit(solution)/shard_map/ppermute | solution.py:369
  59.1 0.0 all-to-all-done.2.pieces
  59.1 1.1 shard_map.45
  60.2 3.6 %all-to-all-start.3 = ((bf16[8,4,12,8,128]{4,3,2,1,0:T(8,128)(2,1)}), bf16[8,4,12,8,128]{4,3,2,1,0:T(8,128)(2,1)S(1)}, u32[]{:S(2)}, u32[]{:S(2)}) async-start(bf16[8,4,12,8,128]{4,3,2,1,0:T(8,128)(2,1)} %get-tuple-element.11), calls=%async_computation.3 | async-start | bytes 1572864 | tf_op jit(solution)/shard_map/all_to_all | solution.py:346
  63.8 2.0 %collective-permute-start.3 = (bf16[132,8,128]{2,1,0:T(8,128)(2,1)S(1)}, bf16[132,8,128]{2,1,0:T(8,128)(2,1)S(1)}, u32[]{:S(2)}, u32[]{:S(2)}) collective-permute-start(bf16[132,8,128]{2,1,0:T(8,128)(2,1)S(1)} %get-tuple-element.10.near), channel_id=1, source_target_pairs={{0,63},{1,2},{2,1},{3,4},{4,3},{5,6},{6,5},{7,8},{8,7},{9,10},{10,... | collective-permute-start | bytes 811016 | tf_op jit(solution)/shard_map/ppermute | solution.py:381
  65.7 3.9 %collective-permute-start.2 = (bf16[132,8,128]{2,1,0:T(8,128)(2,1)S(1)}, bf16[132,8,128]{2,1,0:T(8,128)(2,1)S(1)}, u32[]{:S(2)}, u32[]{:S(2)}) collective-permute-start(bf16[132,8,128]{2,1,0:T(8,128)(2,1)S(1)} %get-tuple-element.10.near), channel_id=1, source_target_pairs={{0,1},{1,0},{2,3},{3,2},{4,5},{5,4},{6,7},{7,6},{8,9},{9,8},{10,11... | collective-permute-start | bytes 811016 | tf_op jit(solution)/shard_map/ppermute | solution.py:380
  69.6 11.2 %collective-permute-done.3.beyond.near_beyond = bf16[132,8,128]{2,1,0:T(8,128)(2,1)S(1)} collective-permute-done((bf16[132,8,128]{2,1,0:T(8,128)(2,1)S(1)}, bf16[132,8,128]{2,1,0:T(8,128)(2,1)S(1)}, u32[]{:S(2)}, u32[]{:S(2)}) %collective-permute-start.3) | collective-permute-done | bytes 270368 | tf_op jit(solution)/shard_map/ppermute | solution.py:381
  80.8 0.0 collective-permute-done.2.partner.near_partner
  80.8 1.1 shard_map.46
  81.9 5.6 %all-to-all-done.3.ss = bf16[8,4,12,8,128]{4,3,2,1,0:T(8,128)(2,1)S(1)} async-done(((bf16[8,4,12,8,128]{4,3,2,1,0:T(8,128)(2,1)}), bf16[8,4,12,8,128]{4,3,2,1,0:T(8,128)(2,1)S(1)}, u32[]{:S(2)}, u32[]{:S(2)}) %all-to-all-start.3) | async-done | bytes 786464 | tf_op jit(solution)/shard_map/all_to_all | solution.py:346
  87.5 4.7 %all-to-all-start.4 = ((bf16[12,3,12,8,128]{4,3,2,1,0:T(8,128)(2,1)}), bf16[12,3,12,8,128]{4,3,2,1,0:T(8,128)(2,1)S(1)}, u32[]{:S(2)}, u32[]{:S(2)}) async-start(bf16[12,3,12,8,128]{4,3,2,1,0:T(8,128)(2,1)} %shard_map.46), calls=%async_computation.4 | async-start | bytes 1769472 | tf_op jit(solution)/shard_map/all_to_all | solution.py:346
  92.2 2.5 %collective-permute-start.4 = (bf16[8,4,12,8,128]{4,3,2,1,0:T(8,128)(2,1)S(1)}, bf16[8,4,12,8,128]{4,3,2,1,0:T(8,128)(2,1)S(1)}, u32[]{:S(2)}, u32[]{:S(2)}) collective-permute-start(bf16[8,4,12,8,128]{4,3,2,1,0:T(8,128)(2,1)S(1)} %all-to-all-done.3.ss), channel_id=1, source_target_pairs={{0,1},{1,0},{2,3},{3,2},{4,5},{5,4},{6,7},{7,6},{8,9},{9,8},{10,11... | collective-permute-start | bytes 2359304 | tf_op jit(solution)/shard_map/ppermute | solution.py:392
  94.7 1.9 %collective-permute-done.4.sp = bf16[8,4,12,8,128]{4,3,2,1,0:T(8,128)(2,1)S(1)} collective-permute-done((bf16[8,4,12,8,128]{4,3,2,1,0:T(8,128)(2,1)S(1)}, bf16[8,4,12,8,128]{4,3,2,1,0:T(8,128)(2,1)S(1)}, u32[]{:S(2)}, u32[]{:S(2)}) %collective-permute-start.4) | collective-permute-done | bytes 786464 | tf_op jit(solution)/shard_map/ppermute | solution.py:392
  96.6 4.8 %collective-permute-start.6 = (bf16[12,8,128]{2,1,0:T(8,128)(2,1)S(1)}, bf16[12,8,128]{2,1,0:T(8,128)(2,1)S(1)}, u32[]{:S(2)}, u32[]{:S(2)}) collective-permute-start(bf16[12,8,128]{2,1,0:T(8,128)(2,1)S(1)} %get-tuple-element.16), channel_id=1, source_target_pairs={{0,64},{64,128},{128,192},{192,256},{256,320},{320,384},{384,448},... | collective-permute-start | bytes 73736 | tf_op jit(solution)/shard_map/ppermute | solution.py:397
  101.5 1.3 %collective-permute-start.5 = (bf16[12,8,128]{2,1,0:T(8,128)(2,1)S(1)}, bf16[12,8,128]{2,1,0:T(8,128)(2,1)S(1)}, u32[]{:S(2)}, u32[]{:S(2)}) collective-permute-start(bf16[12,8,128]{2,1,0:T(8,128)(2,1)S(1)} %get-tuple-element.17), channel_id=1, source_target_pairs={{64,0},{128,64},{192,128},{256,192},{320,256},{384,320},{448,384},... | collective-permute-start | bytes 73736 | tf_op jit(solution)/shard_map/ppermute | solution.py:396
  102.8 9.7 %all-to-all-done.4.sr = bf16[12,3,12,8,128]{4,3,2,1,0:T(8,128)(2,1)S(1)} async-done(((bf16[12,3,12,8,128]{4,3,2,1,0:T(8,128)(2,1)}), bf16[12,3,12,8,128]{4,3,2,1,0:T(8,128)(2,1)S(1)}, u32[]{:S(2)}, u32[]{:S(2)}) %all-to-all-start.4) | async-done | bytes 884768 | tf_op jit(solution)/shard_map/all_to_all | solution.py:346
  112.4 2.0 %shard_map.47 = (bf16[2,12,24,512]{3,2,1,0:T(8,128)(2,1)S(1)}, bf16[2,12,8,512]{3,2,1,0:T(8,128)(2,1)}) custom-call(bf16[12,3,12,8,128]{4,3,2,1,0:T(8,128)(2,1)S(1)} %all-to-all-done.4.sr, bf16[8,4,12,8,128]{4,3,2,1,0:T(8,128)(2,1)S(1)} %all-to-all-done.3.ss, bf16[8,4,12,8,128]{4,3,2,1,0:T(8,128)(2,1)S(1)} %collective-permute-done.4.sp), custom_call_target="tpu_custom_call" | custom-call | flops 4294967296 | bytes 1048576 | tf_op jit(solution)/shard_map/pallas_call | solution.py:350
  114.4 0.0 collective-permute-done.6.row_lo
  114.4 0.0 collective-permute-done.5.row_hi
  114.4 5.8 %shard_map.48 = bf16[2,12,8,512]{3,2,1,0:T(8,128)(2,1)} custom-call(bf16[132,8,128]{2,1,0:T(8,128)(2,1)S(1)} %get-tuple-element.10.near, bf16[132,8,128]{2,1,0:T(8,128)(2,1)S(1)} %collective-permute-done.2.partner.near_partner, bf16[132,8,128]{2,1,0:T(8,128)(2,1)S(1)} %collective-permute-done.3.beyond.near_beyond, ...), custom_call_target="tpu_custom_call" | custom-call | flops 4294967296 | bytes 1048576 | tf_op jit(solution)/shard_map/pallas_call | solution.py:350
  (2 shorter events, 0.0 us)
Async XLA Ops:
  0.6 0.9 copy-start
  1.6 0.7 copy-start.2
  2.2 10.8 %copy-start.1 = (bf16[1,2,96,512]{3,2,1,0:T(8,128)(2,1)S(1)}, bf16[1,2,96,512]{3,2,1,0:T(8,128)(2,1)}, u32[]{:S(2)}) copy-start(bf16[1,2,96,512]{3,2,1,0:T(8,128)(2,1)} %param.2) | copy-start | bytes 589828
  3.7 9.3 %copy-start.3 = (s32[768]{0:T(1024)S(1)}, s32[768]{0:T(1024)}, u32[]{:S(2)}) copy-start(s32[768]{0:T(1024)} %panel.3) | copy-start | bytes 9220
  3.7 17.7 %all-to-all-start.1 = ((bf16[12,8,128]{2,1,0:T(8,128)(2,1)}), bf16[12,8,128]{2,1,0:T(8,128)(2,1)S(1)}, u32[]{:S(2)}, u32[]{:S(2)}) async-start(bf16[12,8,128]{2,1,0:T(8,128)(2,1)} %shard_map.42), calls=%async_computation.1 | async-start | bytes 49152 | tf_op jit(solution)/shard_map/all_to_all | solution.py:346
  21.4 14.9 %all-to-all-start = ((bf16[16,8,128]{2,1,0:T(8,128)(2,1)}), bf16[16,8,128]{2,1,0:T(8,128)(2,1)S(1)}, u32[]{:S(2)}, u32[]{:S(2)}) async-start(bf16[16,8,128]{2,1,0:T(8,128)(2,1)} %shard_map.41), calls=%async_computation | async-start | bytes 65536 | tf_op jit(solution)/shard_map/all_to_all | solution.py:346
  37.3 21.8 %all-to-all-start.2 = ((bf16[4,24,8,128]{3,2,1,0:T(8,128)(2,1)}), bf16[4,24,8,128]{3,2,1,0:T(8,128)(2,1)S(1)}, u32[]{:S(2)}, u32[]{:S(2)}) async-start(bf16[4,24,8,128]{3,2,1,0:T(8,128)(2,1)} %shard_map.44), calls=%async_computation.2 | async-start | bytes 393216 | tf_op jit(solution)/shard_map/all_to_all | solution.py:346
  47.3 4.9 %collective-permute-start.1 = (bf16[2,96,128]{2,1,0:T(8,128)(2,1)S(1)}, bf16[2,96,128]{2,1,0:T(8,128)(2,1)S(1)}, u32[]{:S(2)}, u32[]{:S(2)}) collective-permute-start(bf16[2,96,128]{2,1,0:T(8,128)(2,1)S(1)} %get-tuple-element.18), channel_id=1, source_target_pairs={{0,64},{64,128},{128,192},{192,256},{256,320},{320,384},{384,448},... | collective-permute-start | bytes 147464 | tf_op jit(solution)/shard_map/ppermute | solution.py:370
  50.4 8.7 %collective-permute-start = (bf16[2,96,128]{2,1,0:T(8,128)(2,1)S(1)}, bf16[2,96,128]{2,1,0:T(8,128)(2,1)S(1)}, u32[]{:S(2)}, u32[]{:S(2)}) collective-permute-start(bf16[2,96,128]{2,1,0:T(8,128)(2,1)S(1)} %get-tuple-element.19), channel_id=1, source_target_pairs={{64,0},{128,64},{192,128},{256,192},{320,256},{384,320},{448,384},... | collective-permute-start | bytes 147464 | tf_op jit(solution)/shard_map/ppermute | solution.py:369
  60.2 27.3 %all-to-all-start.3 = ((bf16[8,4,12,8,128]{4,3,2,1,0:T(8,128)(2,1)}), bf16[8,4,12,8,128]{4,3,2,1,0:T(8,128)(2,1)S(1)}, u32[]{:S(2)}, u32[]{:S(2)}) async-start(bf16[8,4,12,8,128]{4,3,2,1,0:T(8,128)(2,1)} %get-tuple-element.11), calls=%async_computation.3 | async-start | bytes 1572864 | tf_op jit(solution)/shard_map/all_to_all | solution.py:346
  63.8 17.0 %collective-permute-start.3 = (bf16[132,8,128]{2,1,0:T(8,128)(2,1)S(1)}, bf16[132,8,128]{2,1,0:T(8,128)(2,1)S(1)}, u32[]{:S(2)}, u32[]{:S(2)}) collective-permute-start(bf16[132,8,128]{2,1,0:T(8,128)(2,1)S(1)} %get-tuple-element.10.near), channel_id=1, source_target_pairs={{0,63},{1,2},{2,1},{3,4},{4,3},{5,6},{6,5},{7,8},{8,7},{9,10},{10,... | collective-permute-start | bytes 811016 | tf_op jit(solution)/shard_map/ppermute | solution.py:381
  65.7 15.1 %collective-permute-start.2 = (bf16[132,8,128]{2,1,0:T(8,128)(2,1)S(1)}, bf16[132,8,128]{2,1,0:T(8,128)(2,1)S(1)}, u32[]{:S(2)}, u32[]{:S(2)}) collective-permute-start(bf16[132,8,128]{2,1,0:T(8,128)(2,1)S(1)} %get-tuple-element.10.near), channel_id=1, source_target_pairs={{0,1},{1,0},{2,3},{3,2},{4,5},{5,4},{6,7},{7,6},{8,9},{9,8},{10,11... | collective-permute-start | bytes 811016 | tf_op jit(solution)/shard_map/ppermute | solution.py:380
  87.5 25.0 %all-to-all-start.4 = ((bf16[12,3,12,8,128]{4,3,2,1,0:T(8,128)(2,1)}), bf16[12,3,12,8,128]{4,3,2,1,0:T(8,128)(2,1)S(1)}, u32[]{:S(2)}, u32[]{:S(2)}) async-start(bf16[12,3,12,8,128]{4,3,2,1,0:T(8,128)(2,1)} %shard_map.46), calls=%async_computation.4 | async-start | bytes 1769472 | tf_op jit(solution)/shard_map/all_to_all | solution.py:346
  92.2 4.4 %collective-permute-start.4 = (bf16[8,4,12,8,128]{4,3,2,1,0:T(8,128)(2,1)S(1)}, bf16[8,4,12,8,128]{4,3,2,1,0:T(8,128)(2,1)S(1)}, u32[]{:S(2)}, u32[]{:S(2)}) collective-permute-start(bf16[8,4,12,8,128]{4,3,2,1,0:T(8,128)(2,1)S(1)} %all-to-all-done.3.ss), channel_id=1, source_target_pairs={{0,1},{1,0},{2,3},{3,2},{4,5},{5,4},{6,7},{7,6},{8,9},{9,8},{10,11... | collective-permute-start | bytes 2359304 | tf_op jit(solution)/shard_map/ppermute | solution.py:392
  96.6 17.8 %collective-permute-start.6 = (bf16[12,8,128]{2,1,0:T(8,128)(2,1)S(1)}, bf16[12,8,128]{2,1,0:T(8,128)(2,1)S(1)}, u32[]{:S(2)}, u32[]{:S(2)}) collective-permute-start(bf16[12,8,128]{2,1,0:T(8,128)(2,1)S(1)} %get-tuple-element.16), channel_id=1, source_target_pairs={{0,64},{64,128},{128,192},{192,256},{256,320},{320,384},{384,448},... | collective-permute-start | bytes 73736 | tf_op jit(solution)/shard_map/ppermute | solution.py:397
  101.5 13.0 %collective-permute-start.5 = (bf16[12,8,128]{2,1,0:T(8,128)(2,1)S(1)}, bf16[12,8,128]{2,1,0:T(8,128)(2,1)S(1)}, u32[]{:S(2)}, u32[]{:S(2)}) collective-permute-start(bf16[12,8,128]{2,1,0:T(8,128)(2,1)S(1)} %get-tuple-element.17), channel_id=1, source_target_pairs={{64,0},{128,64},{192,128},{256,192},{320,256},{384,320},{448,384},... | collective-permute-start | bytes 73736 | tf_op jit(solution)/shard_map/ppermute | solution.py:396

commit v4 on v3

--- a/solution.py
+++ b/solution.py
@@ -26,14 +26,6 @@
 
 def position():
     return lax.axis_index("src"), lax.axis_index("rcv")
-
-
-def replicate(source, target, sems):
-    copies = [pltpu.make_async_copy(source, target.at[n], sems.at[n]) for n in range(target.shape[0])]
-    for copy in copies:
-        copy.start()
-    for copy in copies:
-        copy.wait()
 
 
 def pick_behind_kernel(panel, rec, to_src):
@@ -124,9 +116,8 @@
         out[copy, TILES:] = behind[...]
 
 
-def average_kernel(pieces, rec, next_src, last_src, out, near, rows, sems):
-    lane = lax.broadcasted_iota(jnp.int32, (8, 128), 1)
-    low = lane < 64
+def average_kernel(pieces, out, own, rows, sems):
+    low = lax.broadcasted_iota(jnp.int32, (8, 128), 1) < 64
     for z in range(NZ):
         for tile in range(TILES):
             part, pair, kind = tile // 6, tile % 6 // 3, tile % 3
@@ -139,28 +130,21 @@
     copies = [pltpu.make_async_copy(rows, out.at[n], sems.at[n]) for n in range(NY)]
     for copy in copies:
         copy.start()
-    near[:TILES] = rows[position()[1] // NP]
+    own[...] = rows[position()[1] // NP]
+    for copy in copies:
+        copy.wait()
+
+
+def widen_kernel(rec, next_src, last_src, wide):
+    lane = lax.broadcasted_iota(jnp.int32, (8, 128), 1)
     for part in range(2):
         for a in range(NA):
-            first = TILES + (part * NA + a) * (EXT // 128)
             run = slice(8 * a, 8 * a + 8)
             for n in range(EXT // 128 - 1):
-                near[first + n] = rec[part, run, 128 * n : 128 * n + 128]
+                wide[part, a, n] = rec[part, run, 128 * n : 128 * n + 128]
             after, before = next_src[part, run].astype(F32), last_src[part, run].astype(F32)
             rim = jnp.where(lane < 8, after, jnp.where(lane >= 120, before, jnp.zeros_like(before)))
-            near[first + EXT // 128 - 1] = rim.astype(BF16)
-    for copy in copies:
-        copy.wait()
-
-
-def stack_kernel(near, partner, beyond, out, rows, sems):
-    core = position()[1] % 2
-    for t in range(TILES):
-        one, two = partner[t].astype(F32), beyond[t].astype(F32)
-        rows[0, t] = jnp.where(core == 0, two, one).astype(BF16)
-        rows[1, t] = near[t]
-        rows[2, t] = jnp.where(core == 0, one, two).astype(BF16)
-    replicate(rows, out, sems)
+            wide[part, a, EXT // 128 - 1] = rim.astype(BF16)
 
 
 def bounds(rcv):
@@ -201,17 +185,27 @@
         target[:, :, :, 128 * n : 128 * (n + width)] = total.reshape(*target.shape[:3], 128 * width)
 
 
-def spread_rows(sr, a_rows, first, last):
+def spread_rows(sr, partner, beyond, a_rows):
+    src, rcv = position()
+    first, last = bounds(rcv)
+
+    def held(a):
+        return 4 * ((src + 3 - a % 3) % 3) + (src // 3 + 4 - a // 3) % 4
+
     def spread(a, _):
         lo, hi, keep_lo, keep_hi = neighbours(a, first, last)
+        lo, hi, mid = held(lo), held(hi), held(a)
         for t in range(TILES):
-            x = jnp.concatenate(
-                [sr[lo, 0, t].astype(F32) * keep_lo, sr[a, 1, t].astype(F32), sr[hi, 2, t].astype(F32) * keep_hi], axis=0
-            )
+            below, _ = sides(rcv % 2, partner[lo, t].astype(F32), beyond[lo, t].astype(F32))
+            _, above = sides(rcv % 2, partner[hi, t].astype(F32), beyond[hi, t].astype(F32))
+            x = jnp.concatenate([below * keep_lo, sr[mid, t].astype(F32), above * keep_hi], axis=0)
             a_rows[a, :, 128 * t : 128 * t + 128] = x.astype(BF16)
         return 0
 
     lax.fori_loop(0, NA, spread, 0, unroll=2)
+
+
+def halves(a_rows):
     left = a_rows[...].reshape(24 * NA, 128 * TILES)
     return left[:, : 64 * TILES], left[:, 64 * TILES :]
 
@@ -220,10 +214,10 @@
     return lax.dot_general(x, y, (((1,), (1,)), ((), ())), preferred_element_type=F32)
 
 
-def predict_kernel(sr, ss, sp, guess, mult, a_rows, b_rows):
-    rcv = position()[1]
-    core = rcv % 2
-    left = spread_rows(sr, a_rows, *bounds(rcv))
+def predict_kernel(sr, partner, beyond, ss, sp, guess, mult, a_rows, b_rows):
+    core = position()[1] % 2
+    spread_rows(sr, partner, beyond, a_rows)
+    left = halves(a_rows)
     for z in range(NZ):
         for t in range(TILES):
             mine, theirs = ss[:, z, t].astype(F32), sp[:, z, t].astype(F32)
@@ -244,20 +238,22 @@
             mult[part, :, :, cols] = (full[:, 8:16] * (768.0 ** -0.5)).astype(BF16)
 
 
-def subtract_kernel(near, near_partner, near_beyond, guess, sr, row_hi, row_lo, prim, a_rows, edge, once, box):
+def subtract_kernel(wide, partner, beyond, guess, a_rows, row_same, row_cross, prim, data, edge, once, box):
     rcv = position()[1]
-    core = rcv % 2
     first, last = bounds(rcv)
-    left = spread_rows(sr, a_rows, first, last)
+    left = halves(a_rows)
+    rims = [(row_same[t].astype(F32), row_cross[t].astype(F32)) for t in range(TILES)]
+    row_hi = [jnp.where(rcv % 2 == 0, same, cross) for same, cross in rims]
+    row_lo = [jnp.where(rcv % 2 == 0, cross, same) for same, cross in rims]
     right = []
     for part in range(2):
         tiles = range(6 * part, 6 * part + 6)
         right.append(
             jnp.concatenate(
                 [
-                    jnp.concatenate([row_hi[t].astype(F32) for t in tiles], axis=1),
+                    jnp.concatenate([row_hi[t] for t in tiles], axis=1),
                     jnp.zeros((112, 64 * TILES), F32),
-                    jnp.concatenate([row_lo[t].astype(F32) for t in tiles], axis=1),
+                    jnp.concatenate([row_lo[t] for t in tiles], axis=1),
                 ],
                 axis=0,
             ).astype(BF16)
@@ -268,17 +264,7 @@
     edge[1] = (straight[:, 128:] + crossed[:, 128:]).astype(BF16).astype(F32).reshape(NA, 24, 128)
 
     def run_of(ref, part, a):
-        start = TILES + (part * NA + a) * (EXT // 128)
-        return jnp.concatenate([ref[start + n].astype(F32) for n in range(EXT // 128)], axis=1)
-
-    def data_of(a):
-        lo, hi, keep_lo, keep_hi = neighbours(a, first, last)
-        data = []
-        for part in range(2):
-            below, _ = sides(core, run_of(near_partner, part, lo), run_of(near_beyond, part, lo))
-            _, above = sides(core, run_of(near_partner, part, hi), run_of(near_beyond, part, hi))
-            data.append(jnp.concatenate([below * keep_lo, run_of(near, part, a), above * keep_hi], axis=0))
-        return data
+        return jnp.concatenate([ref[part, a, n].astype(F32) for n in range(EXT // 128)], axis=1)
 
     def guess_of(a):
         return [jnp.concatenate([guess[part, a].astype(F32), edge[part, a]], axis=1) for part in range(2)]
@@ -292,7 +278,12 @@
         return dr - (gain_re * pr - gain_im * pi), di - (gain_re * pi + gain_im * pr)
 
     def first_sweep(a, _):
-        dr, di = data_of(a)
+        lo, hi, keep_lo, keep_hi = neighbours(a, first, last)
+        for part in range(2):
+            below, _ = sides(rcv % 2, run_of(partner, part, lo), run_of(beyond, part, lo))
+            _, above = sides(rcv % 2, run_of(partner, part, hi), run_of(beyond, part, hi))
+            data[part, a] = jnp.concatenate([below * keep_lo, run_of(wide, part, a), above * keep_hi], axis=0)
+        dr, di = data[0, a], data[1, a]
         weight = 1.5 - jnp.tanh(dr * dr + di * di)
         for n, q in enumerate(terms_of(dr, di, *guess_of(a))):
             once[n, a] = windows_rows(weight * q, 16)
@@ -304,18 +295,19 @@
     windows_lanes(once, box, band, (0, 2, 4))
 
     def second_sweep(a, _):
-        dr, di, pr, pi = [v[4:20] for v in (*data_of(a), *guess_of(a))]
+        dr, di = data[0, a, 4:20], data[1, a, 4:20]
+        pr, pi = [v[4:20] for v in guess_of(a)]
         er, ei = subtract(dr, di, pr, pi, [box[n, a] for n in range(3)])
-        weight = 1.5 - jnp.tanh(er * er + ei * ei)
+        again = 1.5 - jnp.tanh(er * er + ei * ei)
         for n, q in enumerate(terms_of(dr, di, pr, pi)):
-            once[n, a, :8] = windows_rows(weight * q, 8)
+            once[n, a, :8] = windows_rows(again * q, 8)
         return 0
 
     lax.fori_loop(0, NA, second_sweep, 0, unroll=2)
     windows_lanes(once.at[:, :, :8], box.at[:, :, :8], band, (0, 2))
 
     def finish(a, _):
-        dr, di = [run_of(near, part, a)[:, :512] for part in range(2)]
+        dr, di = [data[part, a, 8:16, :512] for part in range(2)]
         pr, pi = [guess[part, a].astype(F32)[8:16] for part in range(2)]
         er, ei = subtract(dr, di, pr, pi, [box[n, a, :8, :512] for n in range(3)])
         prim[0, a], prim[1, a] = er.astype(BF16), ei.astype(BF16)
@@ -334,7 +326,6 @@
 
 def block(record, panel_offset):
     src_count, rcv_count = lax.axis_size("src"), lax.axis_size("rcv")
-    rcv = lax.axis_index("rcv")
     rec = record[0]
     plane = [[z * NP + p for p in range(NP)] for z in range(NZ)]
     column = [[z * NP + p for z in range(NZ)] for p in range(NP)]
@@ -357,50 +348,57 @@
             cost_estimate=pl.CostEstimate(flops=flops, bytes_accessed=1 << 20, transcendentals=0),
         )(*scalars, *arrays)
 
-    to_src = kernel(pick_behind_kernel, shape(NA, 8, 128), (panel_offset,), (rec,))
+    to_src = kernel(pick_behind_kernel, shape(NA, 8, 128), (panel_offset,), (rec,), limit=60 << 20)
     from_src = exchange(to_src, "src")
     to_rcv = kernel(pick_front_kernel, shape(NP, 8, 128), (panel_offset,), (rec,))
     from_rcv = exchange(to_rcv, "rcv", plane)
     behind = kernel(order_behind_kernel, shape(TILES, 8, 128), (), (from_src,))
     message = kernel(order_kernel, shape(NZ, 2 * TILES, 8, 128), (), (from_rcv, behind))
     pieces = exchange(message, "rcv", column)
-    held, _ = lax.optimization_barrier((rec, from_rcv))
+    held, _ = lax.optimization_barrier((rec, from_src))
     first_tile, last_tile = held[:, :, :128], held[:, :, 384:]
     next_src = lax.ppermute(first_tile, "src", ring(src_count, -1, False))
     last_src = lax.ppermute(last_tile, "src", ring(src_count, 1, False))
-    spread, near = kernel(
+    wide = kernel(widen_kernel, shape(2, NA, EXT // 128, 8, 128), (), (rec, next_src, last_src))
+    wide_beyond = lax.ppermute(wide, "rcv", beyond)
+    wide_partner = lax.ppermute(wide, "rcv", swap)
+    spread, own = kernel(
         average_kernel,
-        (shape(NY, NZ, TILES, 8, 128), shape(TILES + 2 * NA * (EXT // 128), 8, 128)),
+        (shape(NY, NZ, TILES, 8, 128), shape(TILES, 8, 128)),
         (),
-        (pieces, rec, next_src, last_src),
+        (pieces,),
         [pltpu.VMEM((NZ, TILES, 8, 128), BF16), pltpu.SemaphoreType.DMA((NY,))],
         spaces=(pltpu.HBM, pltpu.VMEM),
     )
     ss = exchange(spread, "rcv", line)
-    near_partner = lax.ppermute(near, "rcv", swap)
-    near_beyond = lax.ppermute(near, "rcv", beyond)
-    stacked = kernel(
-        stack_kernel,
-        shape(src_count, 3, TILES, 8, 128),
+    moved = [lax.ppermute(own, "src", ring(src_count, 3 * d, True)) for d in range(1, 4)]
+    sr = jnp.stack([own, *moved])
+    moved = [
+        lax.ppermute(sr, "src", [(n, n - n % 3 + (n + e) % 3) for n in range(src_count)]) for e in range(1, 3)
+    ]
+    sr = jnp.concatenate([sr, *moved])
+    sr_beyond = lax.ppermute(sr, "rcv", beyond)
+    sr_partner = lax.ppermute(sr, "rcv", swap)
+    row = jnp.where(lax.axis_index("rcv") % 2 == 0, ss[0, 0], ss[NY - 1, NZ - 1])
+    same, cross = [
+        [
+            (n * rcv_count + k, to * rcv_count + (k ^ flip))
+            for n in range(src_count)
+            for k in range(rcv_count)
+            for to in (n + (1 if k % 2 else -1),)
+            if 0 <= to < src_count
+        ]
+        for flip in range(2)
+    ]
+    row_same = lax.ppermute(row, ("src", "rcv"), same)
+    row_cross = lax.ppermute(row, ("src", "rcv"), cross)
+    sp = lax.ppermute(ss, "rcv", swap)
+    guess, mult, left = kernel(
+        predict_kernel,
+        (shape(2, NA, 24, 512), shape(2, NA, 8, 512), shape(NA, 24, 128 * TILES)),
         (),
-        (near, near_partner, near_beyond),
-        [pltpu.VMEM((3, TILES, 8, 128), BF16), pltpu.SemaphoreType.DMA((src_count,))],
-        spaces=pltpu.HBM,
-    )
-    ss, stacked = lax.optimization_barrier((ss, stacked))
-    sr = exchange(stacked, "src")
-    sp = lax.ppermute(ss, "rcv", swap)
-    even_core = rcv % 2 == 0
-    row_first = jnp.where(even_core, ss[0, 0], sp[0, 0])
-    row_last = jnp.where(even_core, sp[NY - 1, NZ - 1], ss[NY - 1, NZ - 1])
-    row_hi = lax.ppermute(row_first, "src", ring(src_count, -1, False))
-    row_lo = lax.ppermute(row_last, "src", ring(src_count, 1, False))
-    guess, mult = kernel(
-        predict_kernel,
-        (shape(2, NA, 24, 512), shape(2, NA, 8, 512)),
-        (),
-        (sr, ss, sp),
-        [pltpu.VMEM((NA, 24, 128 * TILES), BF16), pltpu.VMEM((512, 128 * TILES), BF16)],
+        (sr, sr_partner, sr_beyond, ss, sp),
+        [pltpu.VMEM((512, 128 * TILES), BF16)],
         flops=1 << 32,
         limit=16 << 20,
     )
@@ -408,9 +406,9 @@
         subtract_kernel,
         shape(2, NA, 8, 512),
         (),
-        (near, near_partner, near_beyond, guess, sr, row_hi, row_lo),
+        (wide, wide_partner, wide_beyond, guess, left, row_same, row_cross),
         [
-            pltpu.VMEM((NA, 24, 128 * TILES), BF16),
+            pltpu.VMEM((2, NA, 24, EXT), F32),
             pltpu.VMEM((2, NA, 24, 128), F32),
             pltpu.VMEM((3, NA, 16, EXT), F32),
             pltpu.VMEM((3, NA, 16, EXT), F32),

time: 121 us -> 131 us (1.083)
  the two profiles are of different devices: /device:TPU:192 before, /device:TPU:61 now
where the time goes in v4:
time: 131 us
  starting transfers between devices  75 us (57%)
  blocking collectives  23.4 us (18%)
  waiting for transfers between devices  18.3 us (14%)
  Pallas kernels  12.9 us (10%)
    all_to_all x1, blocking collectives, exchange(): lax.all_to_all(x, axis, split_axis=0, concat_axis=0, tiled=True, axis_ind...  23.4 us
    all_to_all x3, starting transfers between devices, exchange(): lax.all_to_all(x, axis, split_axis=0, concat_axis=0, tiled=True, axis_ind...  23 us
    pallas_call x8, Pallas kernels, kernel(): pl.pallas_call(body, out_shape=outs, in_specs=smem(len(scalars)) + vmem(l...  12.9 us
    ppermute x3, starting transfers between devices, block(): lax.ppermute(own, 'src', ring(src_count, 3 * d, True))  10.1 us
    ppermute x1, starting transfers between devices, block(): sr_beyond = lax.ppermute(sr, 'rcv', beyond)  7.73 us
    all_to_all x3, waiting for transfers between devices, exchange(): lax.all_to_all(x, axis, split_axis=0, concat_axis=0, tiled=True, axis_ind...  7.56 us
    ppermute x1, starting transfers between devices, block(): sp = lax.ppermute(ss, 'rcv', swap)  6.99 us
    ppermute x2, starting transfers between devices, block(): lax.ppermute(sr, 'src', [(n, n - n % 3 + (n + e) % 3) for n in range(src_...  6.18 us
  transfers between devices with their start and end apart: 17, of which 5 were waited for; matrix products, arithmetic and copies ran while one was open for 0% of the time, Pallas kernels for 3%

profile of v4, /device:TPU:61, one launch (start us, length us, event | category | flops | bytes accessed | tf_op | source)
XLA Modules:
  0.0 130.6 jit_solution(1063014456989541173)
XLA Ops:
  0.6 0.0 copy-start
  0.6 1.9 %shard_map.41 = bf16[12,8,128]{2,1,0:T(8,128)(2,1)} custom-call(s32[768]{0:T(1024)} %panel.3, bf16[2,96,512]{2,1,0:T(8,128)(2,1)} %bitcast.13), custom_call_target="tpu_custom_call" | custom-call | flops 1048576 | bytes 1048576 | tf_op jit(solution)/shard_map/pallas_call | solution.py:341
  2.5 0.0 copy-start.1
  2.5 8.0 %all-to-all-start = ((bf16[12,8,128]{2,1,0:T(8,128)(2,1)}), bf16[12,8,128]{2,1,0:T(8,128)(2,1)S(1)}, u32[]{:S(2)}, u32[]{:S(2)}) async-start(bf16[12,8,128]{2,1,0:T(8,128)(2,1)} %shard_map.41), calls=%async_computation | async-start | bytes 49152 | tf_op jit(solution)/shard_map/all_to_all | solution.py:337
  10.5 0.0 copy-done
  10.5 0.0 copy-done.1
  10.5 1.5 %shard_map.43 = bf16[16,8,128]{2,1,0:T(8,128)(2,1)} custom-call(s32[768]{0:T(1024)S(1)} %copy-done.1, bf16[2,96,512]{2,1,0:T(8,128)(2,1)S(1)} %bitcast.14), custom_call_target="tpu_custom_call" | custom-call | flops 1048576 | bytes 1048576 | tf_op jit(solution)/shard_map/pallas_call | solution.py:341
  12.0 2.7 %all-to-all-done.from_src = bf16[12,8,128]{2,1,0:T(8,128)(2,1)S(1)} async-done(((bf16[12,8,128]{2,1,0:T(8,128)(2,1)}), bf16[12,8,128]{2,1,0:T(8,128)(2,1)S(1)}, u32[]{:S(2)}, u32[]{:S(2)}) %all-to-all-start) | async-done | bytes 24608 | tf_op jit(solution)/shard_map/all_to_all | solution.py:337
  14.7 9.1 %all-to-all-start.1 = ((bf16[16,8,128]{2,1,0:T(8,128)(2,1)}), bf16[16,8,128]{2,1,0:T(8,128)(2,1)S(1)}, u32[]{:S(2)}, u32[]{:S(2)}) async-start(bf16[16,8,128]{2,1,0:T(8,128)(2,1)} %shard_map.43), calls=%async_computation.1 | async-start | bytes 65536 | tf_op jit(solution)/shard_map/all_to_all | solution.py:337
  23.7 0.1 shard_map.44.behind
  23.8 4.9 %all-to-all-done.1.from_rcv = bf16[16,8,128]{2,1,0:T(8,128)(2,1)S(1)} async-done(((bf16[16,8,128]{2,1,0:T(8,128)(2,1)}), bf16[16,8,128]{2,1,0:T(8,128)(2,1)S(1)}, u32[]{:S(2)}, u32[]{:S(2)}) %all-to-all-start.1) | async-done | bytes 32800 | tf_op jit(solution)/shard_map/all_to_all | solution.py:337
  28.7 0.3 shard_map.45
  29.0 23.4 %all_to_all.20.pieces = bf16[4,24,8,128]{3,2,1,0:T(8,128)(2,1)S(1)} all-to-all(bf16[4,24,8,128]{3,2,1,0:T(8,128)(2,1)S(1)} %shard_map.45), channel_id=1, replica_groups={{0,16,32,48},{1,17,33,49},{2,18,34,50},{3,19,35,51},{4,20,36,52},{5,21,..., dimensions={0} | all-to-all | bytes 393216 | tf_op jit(solution)/shard_map/all_to_all | solution.py:337
  52.4 1.0 shard_map.46
  53.4 5.9 %all-to-all-start.3 = ((bf16[8,4,12,8,128]{4,3,2,1,0:T(8,128)(2,1)}), bf16[8,4,12,8,128]{4,3,2,1,0:T(8,128)(2,1)S(1)}, u32[]{:S(2)}, u32[]{:S(2)}) async-start(bf16[8,4,12,8,128]{4,3,2,1,0:T(8,128)(2,1)} %get-tuple-element.10), calls=%async_computation.3 | async-start | bytes 1572864 | tf_op jit(solution)/shard_map/all_to_all | solution.py:337
  59.4 3.3 %collective-permute-start.4 = (bf16[12,8,128]{2,1,0:T(8,128)(2,1)S(1)}, bf16[12,8,128]{2,1,0:T(8,128)(2,1)S(1)}, u32[]{:S(2)}, u32[]{:S(2)}) collective-permute-start(bf16[12,8,128]{2,1,0:T(8,128)(2,1)S(1)} %get-tuple-element.9), channel_id=1, source_target_pairs={{0,192},{64,256},{128,320},{192,384},{256,448},{320,512},{384,576}... | collective-permute-start | bytes 73736 | tf_op jit(solution)/shard_map/ppermute | solution.py:374
  62.7 3.1 %collective-permute-start.5 = (bf16[12,8,128]{2,1,0:T(8,128)(2,1)S(1)}, bf16[12,8,128]{2,1,0:T(8,128)(2,1)S(1)}, u32[]{:S(2)}, u32[]{:S(2)}) collective-permute-start(bf16[12,8,128]{2,1,0:T(8,128)(2,1)S(1)} %get-tuple-element.9), channel_id=1, source_target_pairs={{0,384},{64,448},{128,512},{192,576},{256,640},{320,704},{384,0},{... | collective-permute-start | bytes 73736 | tf_op jit(solution)/shard_map/ppermute | solution.py:374
  65.8 3.7 %collective-permute-start.6 = (bf16[12,8,128]{2,1,0:T(8,128)(2,1)S(1)}, bf16[12,8,128]{2,1,0:T(8,128)(2,1)S(1)}, u32[]{:S(2)}, u32[]{:S(2)}) collective-permute-start(bf16[12,8,128]{2,1,0:T(8,128)(2,1)S(1)} %get-tuple-element.9), channel_id=1, source_target_pairs={{0,576},{64,640},{128,704},{192,0},{256,64},{320,128},{384,192},{4... | collective-permute-start | bytes 73736 | tf_op jit(solution)/shard_map/ppermute | solution.py:374
  69.5 0.0 collective-permute-done.4
  69.5 0.0 collective-permute-done.5
  69.5 1.1 collective-permute-done.6
  70.7 2.7 %collective-permute-start.7 = (bf16[4,12,8,128]{3,2,1,0:T(8,128)(2,1)S(1)}, bf16[4,12,8,128]{3,2,1,0:T(8,128)(2,1)S(1)}, u32[]{:S(2)}, u32[]{:S(2)}) collective-permute-start(bf16[4,12,8,128]{3,2,1,0:T(8,128)(2,1)S(1)} %pad_maximum_fusion), channel_id=1, source_target_pairs={{0,64},{64,128},{128,0},{192,256},{256,320},{320,192},{384,448},{4... | collective-permute-start | bytes 294920 | tf_op jit(solution)/shard_map/ppermute | solution.py:377
  73.4 3.4 %collective-permute-start.8 = (bf16[4,12,8,128]{3,2,1,0:T(8,128)(2,1)S(1)}, bf16[4,12,8,128]{3,2,1,0:T(8,128)(2,1)S(1)}, u32[]{:S(2)}, u32[]{:S(2)}) collective-permute-start(bf16[4,12,8,128]{3,2,1,0:T(8,128)(2,1)S(1)} %pad_maximum_fusion), channel_id=1, source_target_pairs={{0,128},{64,0},{128,64},{192,320},{256,192},{320,256},{384,512},{4... | collective-permute-start | bytes 294920 | tf_op jit(solution)/shard_map/ppermute | solution.py:377
  76.9 0.0 all-to-all-done.3.ss
  76.9 7.0 %collective-permute-start.11 = (bf16[8,4,12,8,128]{4,3,2,1,0:T(8,128)(2,1)S(1)}, bf16[8,4,12,8,128]{4,3,2,1,0:T(8,128)(2,1)S(1)}, u32[]{:S(2)}, u32[]{:S(2)}) collective-permute-start(bf16[8,4,12,8,128]{4,3,2,1,0:T(8,128)(2,1)S(1)} %all-to-all-done.3.ss), channel_id=1, source_target_pairs={{0,1},{1,0},{2,3},{3,2},{4,5},{5,4},{6,7},{7,6},{8,9},{9,8},{10,11... | collective-permute-start | bytes 2359304 | tf_op jit(solution)/shard_map/ppermute | solution.py:395
  83.9 0.0 collective-permute-done.7
  84.0 0.0 collective-permute-done.8
  84.0 7.7 %collective-permute-start.10 = (bf16[12,12,8,128]{3,2,1,0:T(8,128)(2,1)S(1)}, bf16[12,12,8,128]{3,2,1,0:T(8,128)(2,1)S(1)}, u32[]{:S(2)}, u32[]{:S(2)}) collective-permute-start(bf16[12,12,8,128]{3,2,1,0:T(8,128)(2,1)S(1)} %constant_dynamic-update-slice_fusion.sr), channel_id=1, source_target_pairs={{0,63},{1,2},{2,1},{3,4},{4,3},{5,6},{6,5},{7,8},{8,7},{9,10},{10,... | collective-permute-start | bytes 884744 | tf_op jit(solution)/shard_map/ppermute | solution.py:380
  91.8 1.9 %collective-permute-start.9 = (bf16[12,12,8,128]{3,2,1,0:T(8,128)(2,1)S(1)}, bf16[12,12,8,128]{3,2,1,0:T(8,128)(2,1)S(1)}, u32[]{:S(2)}, u32[]{:S(2)}) collective-permute-start(bf16[12,12,8,128]{3,2,1,0:T(8,128)(2,1)S(1)} %constant_dynamic-update-slice_fusion.sr), channel_id=1, source_target_pairs={{0,1},{1,0},{2,3},{3,2},{4,5},{5,4},{6,7},{7,6},{8,9},{9,8},{10,11... | collective-permute-start | bytes 884744 | tf_op jit(solution)/shard_map/ppermute | solution.py:381
  93.7 4.9 %collective-permute-start = (bf16[2,96,128]{2,1,0:T(8,128)(2,1)S(1)}, bf16[2,96,128]{2,1,0:T(8,128)(2,1)S(1)}, u32[]{:S(2)}, u32[]{:S(2)}) collective-permute-start(bf16[2,96,128]{2,1,0:T(8,128)(2,1)S(1)} %get-tuple-element.15), channel_id=1, source_target_pairs={{64,0},{128,64},{192,128},{256,192},{320,256},{384,320},{448,384},... | collective-permute-start | bytes 147464 | tf_op jit(solution)/shard_map/ppermute | solution.py:360
  98.6 1.9 %collective-permute-start.1 = (bf16[2,96,128]{2,1,0:T(8,128)(2,1)S(1)}, bf16[2,96,128]{2,1,0:T(8,128)(2,1)S(1)}, u32[]{:S(2)}, u32[]{:S(2)}) collective-permute-start(bf16[2,96,128]{2,1,0:T(8,128)(2,1)S(1)} %get-tuple-element.14), channel_id=1, source_target_pairs={{0,64},{64,128},{128,192},{192,256},{256,320},{320,384},{384,448},... | collective-permute-start | bytes 147464 | tf_op jit(solution)/shard_map/ppermute | solution.py:361
  100.5 0.0 collective-permute-done.next_src
  100.5 4.7 %collective-permute-done.1.last_src = bf16[2,96,128]{2,1,0:T(8,128)(2,1)S(1)} collective-permute-done((bf16[2,96,128]{2,1,0:T(8,128)(2,1)S(1)}, bf16[2,96,128]{2,1,0:T(8,128)(2,1)S(1)}, u32[]{:S(2)}, u32[]{:S(2)}) %collective-permute-start.1) | collective-permute-done | bytes 49184 | tf_op jit(solution)/shard_map/ppermute | solution.py:361
  105.2 3.8 %collective-permute-start.2 = (bf16[2,12,5,8,128]{4,3,2,1,0:T(8,128)(2,1)S(1)}, bf16[2,12,5,8,128]{4,3,2,1,0:T(8,128)(2,1)S(1)}, u32[]{:S(2)}, u32[]{:S(2)}) collective-permute-start(bf16[2,12,5,8,128]{4,3,2,1,0:T(8,128)(2,1)S(1)} %shard_map.42.wide), channel_id=1, source_target_pairs={{0,1},{1,0},{2,3},{3,2},{4,5},{5,4},{6,7},{7,6},{8,9},{9,8},{10,11... | collective-permute-start | bytes 737288 | tf_op jit(solution)/shard_map/ppermute | solution.py:364
  109.1 4.6 %collective-permute-start.3 = (bf16[2,12,5,8,128]{4,3,2,1,0:T(8,128)(2,1)S(1)}, bf16[2,12,5,8,128]{4,3,2,1,0:T(8,128)(2,1)S(1)}, u32[]{:S(2)}, u32[]{:S(2)}) collective-permute-start(bf16[2,12,5,8,128]{4,3,2,1,0:T(8,128)(2,1)S(1)} %shard_map.42.wide), channel_id=1, source_target_pairs={{0,63},{1,2},{2,1},{3,4},{4,3},{5,6},{6,5},{7,8},{8,7},{9,10},{10,... | collective-permute-start | bytes 737288 | tf_op jit(solution)/shard_map/ppermute | solution.py:363
  113.7 0.0 collective-permute-done.10.beyond
  113.8 1.9 %collective-permute-start.12 = (bf16[12,8,128]{2,1,0:T(8,128)(2,1)S(1)}, bf16[12,8,128]{2,1,0:T(8,128)(2,1)S(1)}, u32[]{:S(2)}, u32[]{:S(2)}) collective-permute-start(bf16[12,8,128]{2,1,0:T(8,128)(2,1)S(1)} %fusion), channel_id=1, source_target_pairs={{1,65},{3,67},{5,69},{7,71},{9,73},{11,75},{13,77},{15,79},{17,81}... | collective-permute-start | bytes 73736 | tf_op jit(solution)/shard_map/ppermute | solution.py:393
  115.7 0.0 collective-permute-done.9.partner
  115.7 1.9 %collective-permute-start.13 = (bf16[12,8,128]{2,1,0:T(8,128)(2,1)S(1)}, bf16[12,8,128]{2,1,0:T(8,128)(2,1)S(1)}, u32[]{:S(2)}, u32[]{:S(2)}) collective-permute-start(bf16[12,8,128]{2,1,0:T(8,128)(2,1)S(1)} %fusion), channel_id=1, source_target_pairs={{1,64},{3,66},{5,68},{7,70},{9,72},{11,74},{13,76},{15,78},{17,80}... | collective-permute-start | bytes 73736 | tf_op jit(solution)/shard_map/ppermute | solution.py:394
  117.6 0.0 collective-permute-done.11.sp
  117.6 2.5 %shard_map.47 = (bf16[2,12,24,512]{3,2,1,0:T(8,128)(2,1)S(1)}, bf16[2,12,8,512]{3,2,1,0:T(8,128)(2,1)}, bf16[12,24,1536]{2,1,0:T(8,128)(2,1)S(1)}) custom-call(bf16[12,12,8,128]{3,2,1,0:T(8,128)(2,1)S(1)} %constant_dynamic-update-slice_fusion.sr, bf16[12,12,8,128]{3,2,1,0:T(8,128)(2,1)S(1)} %collective-permute-done.9.partner, ...), custom_call_target="tpu_custom_call" | custom-call | flops 4294967296 | bytes 1048576 | tf_op jit(solution)/shard_map/pallas_call | solution.py:341
  120.1 0.0 collective-permute-done.2.partner
  120.1 5.0 %collective-permute-done.3.beyond = bf16[2,12,5,8,128]{4,3,2,1,0:T(8,128)(2,1)S(1)} collective-permute-done((bf16[2,12,5,8,128]{4,3,2,1,0:T(8,128)(2,1)S(1)}, bf16[2,12,5,8,128]{4,3,2,1,0:T(8,128)(2,1)S(1)}, u32[]{:S(2)}, u32[]{:S(2)}) %collective-permute-start.3) | collective-permute-done | bytes 245792 | tf_op jit(solution)/shard_map/ppermute | solution.py:363
  125.1 0.0 collective-permute-done.12.row_same
  125.1 0.0 collective-permute-done.13.row_cross
  125.1 5.6 %shard_map.48 = bf16[2,12,8,512]{3,2,1,0:T(8,128)(2,1)} custom-call(bf16[2,12,5,8,128]{4,3,2,1,0:T(8,128)(2,1)S(1)} %shard_map.42.wide, bf16[2,12,5,8,128]{4,3,2,1,0:T(8,128)(2,1)S(1)} %collective-permute-done.2.partner, bf16[2,12,5,8,128]{4,3,2,1,0:T(8,128)(2,1)S(1)} %collective-permute-done.3.beyond, bf16[2,12,24,512]{3,2,1,0:T(8,128)(2,1)S(1)} %get-tuple-element.11.guess, ...), custom_call_target="tpu_custom_call" | custom-call | flops 4294967296 | bytes 1048576 | tf_op jit(solution)/shard_map/pallas_call | solution.py:341
  (10 shorter events, 0.1 us)
Async XLA Ops:
  0.6 9.9 %copy-start = (bf16[1,2,96,512]{3,2,1,0:T(8,128)(2,1)S(1)}, bf16[1,2,96,512]{3,2,1,0:T(8,128)(2,1)}, u32[]{:S(2)}) copy-start(bf16[1,2,96,512]{3,2,1,0:T(8,128)(2,1)} %param.2) | copy-start | bytes 589828
  2.5 8.0 %copy-start.1 = (s32[768]{0:T(1024)S(1)}, s32[768]{0:T(1024)}, u32[]{:S(2)}) copy-start(s32[768]{0:T(1024)} %panel.3) | copy-start | bytes 9220
  2.5 12.1 %all-to-all-start = ((bf16[12,8,128]{2,1,0:T(8,128)(2,1)}), bf16[12,8,128]{2,1,0:T(8,128)(2,1)S(1)}, u32[]{:S(2)}, u32[]{:S(2)}) async-start(bf16[12,8,128]{2,1,0:T(8,128)(2,1)} %shard_map.41), calls=%async_computation | async-start | bytes 49152 | tf_op jit(solution)/shard_map/all_to_all | solution.py:337
  14.7 14.1 %all-to-all-start.1 = ((bf16[16,8,128]{2,1,0:T(8,128)(2,1)}), bf16[16,8,128]{2,1,0:T(8,128)(2,1)S(1)}, u32[]{:S(2)}, u32[]{:S(2)}) async-start(bf16[16,8,128]{2,1,0:T(8,128)(2,1)} %shard_map.43), calls=%async_computation.1 | async-start | bytes 65536 | tf_op jit(solution)/shard_map/all_to_all | solution.py:337
  53.4 23.5 %all-to-all-start.3 = ((bf16[8,4,12,8,128]{4,3,2,1,0:T(8,128)(2,1)}), bf16[8,4,12,8,128]{4,3,2,1,0:T(8,128)(2,1)S(1)}, u32[]{:S(2)}, u32[]{:S(2)}) async-start(bf16[8,4,12,8,128]{4,3,2,1,0:T(8,128)(2,1)} %get-tuple-element.10), calls=%async_computation.3 | async-start | bytes 1572864 | tf_op jit(solution)/shard_map/all_to_all | solution.py:337
  59.4 10.2 %collective-permute-start.4 = (bf16[12,8,128]{2,1,0:T(8,128)(2,1)S(1)}, bf16[12,8,128]{2,1,0:T(8,128)(2,1)S(1)}, u32[]{:S(2)}, u32[]{:S(2)}) collective-permute-start(bf16[12,8,128]{2,1,0:T(8,128)(2,1)S(1)} %get-tuple-element.9), channel_id=1, source_target_pairs={{0,192},{64,256},{128,320},{192,384},{256,448},{320,512},{384,576}... | collective-permute-start | bytes 73736 | tf_op jit(solution)/shard_map/ppermute | solution.py:374
  62.7 6.8 %collective-permute-start.5 = (bf16[12,8,128]{2,1,0:T(8,128)(2,1)S(1)}, bf16[12,8,128]{2,1,0:T(8,128)(2,1)S(1)}, u32[]{:S(2)}, u32[]{:S(2)}) collective-permute-start(bf16[12,8,128]{2,1,0:T(8,128)(2,1)S(1)} %get-tuple-element.9), channel_id=1, source_target_pairs={{0,384},{64,448},{128,512},{192,576},{256,640},{320,704},{384,0},{... | collective-permute-start | bytes 73736 | tf_op jit(solution)/shard_map/ppermute | solution.py:374
  65.8 4.9 %collective-permute-start.6 = (bf16[12,8,128]{2,1,0:T(8,128)(2,1)S(1)}, bf16[12,8,128]{2,1,0:T(8,128)(2,1)S(1)}, u32[]{:S(2)}, u32[]{:S(2)}) collective-permute-start(bf16[12,8,128]{2,1,0:T(8,128)(2,1)S(1)} %get-tuple-element.9), channel_id=1, source_target_pairs={{0,576},{64,640},{128,704},{192,0},{256,64},{320,128},{384,192},{4... | collective-permute-start | bytes 73736 | tf_op jit(solution)/shard_map/ppermute | solution.py:374
  70.7 13.3 %collective-permute-start.7 = (bf16[4,12,8,128]{3,2,1,0:T(8,128)(2,1)S(1)}, bf16[4,12,8,128]{3,2,1,0:T(8,128)(2,1)S(1)}, u32[]{:S(2)}, u32[]{:S(2)}) collective-permute-start(bf16[4,12,8,128]{3,2,1,0:T(8,128)(2,1)S(1)} %pad_maximum_fusion), channel_id=1, source_target_pairs={{0,64},{64,128},{128,0},{192,256},{256,320},{320,192},{384,448},{4... | collective-permute-start | bytes 294920 | tf_op jit(solution)/shard_map/ppermute | solution.py:377
  73.4 10.5 %collective-permute-start.8 = (bf16[4,12,8,128]{3,2,1,0:T(8,128)(2,1)S(1)}, bf16[4,12,8,128]{3,2,1,0:T(8,128)(2,1)S(1)}, u32[]{:S(2)}, u32[]{:S(2)}) collective-permute-start(bf16[4,12,8,128]{3,2,1,0:T(8,128)(2,1)S(1)} %pad_maximum_fusion), channel_id=1, source_target_pairs={{0,128},{64,0},{128,64},{192,320},{256,192},{320,256},{384,512},{4... | collective-permute-start | bytes 294920 | tf_op jit(solution)/shard_map/ppermute | solution.py:377
  76.9 40.7 %collective-permute-start.11 = (bf16[8,4,12,8,128]{4,3,2,1,0:T(8,128)(2,1)S(1)}, bf16[8,4,12,8,128]{4,3,2,1,0:T(8,128)(2,1)S(1)}, u32[]{:S(2)}, u32[]{:S(2)}) collective-permute-start(bf16[8,4,12,8,128]{4,3,2,1,0:T(8,128)(2,1)S(1)} %all-to-all-done.3.ss), channel_id=1, source_target_pairs={{0,1},{1,0},{2,3},{3,2},{4,5},{5,4},{6,7},{7,6},{8,9},{9,8},{10,11... | collective-permute-start | bytes 2359304 | tf_op jit(solution)/shard_map/ppermute | solution.py:395
  84.0 29.7 %collective-permute-start.10 = (bf16[12,12,8,128]{3,2,1,0:T(8,128)(2,1)S(1)}, bf16[12,12,8,128]{3,2,1,0:T(8,128)(2,1)S(1)}, u32[]{:S(2)}, u32[]{:S(2)}) collective-permute-start(bf16[12,12,8,128]{3,2,1,0:T(8,128)(2,1)S(1)} %constant_dynamic-update-slice_fusion.sr), channel_id=1, source_target_pairs={{0,63},{1,2},{2,1},{3,4},{4,3},{5,6},{6,5},{7,8},{8,7},{9,10},{10,... | collective-permute-start | bytes 884744 | tf_op jit(solution)/shard_map/ppermute | solution.py:380
  91.8 23.9 %collective-permute-start.9 = (bf16[12,12,8,128]{3,2,1,0:T(8,128)(2,1)S(1)}, bf16[12,12,8,128]{3,2,1,0:T(8,128)(2,1)S(1)}, u32[]{:S(2)}, u32[]{:S(2)}) collective-permute-start(bf16[12,12,8,128]{3,2,1,0:T(8,128)(2,1)S(1)} %constant_dynamic-update-slice_fusion.sr), channel_id=1, source_target_pairs={{0,1},{1,0},{2,3},{3,2},{4,5},{5,4},{6,7},{7,6},{8,9},{9,8},{10,11... | collective-permute-start | bytes 884744 | tf_op jit(solution)/shard_map/ppermute | solution.py:381
  93.7 6.8 %collective-permute-start = (bf16[2,96,128]{2,1,0:T(8,128)(2,1)S(1)}, bf16[2,96,128]{2,1,0:T(8,128)(2,1)S(1)}, u32[]{:S(2)}, u32[]{:S(2)}) collective-permute-start(bf16[2,96,128]{2,1,0:T(8,128)(2,1)S(1)} %get-tuple-element.15), channel_id=1, source_target_pairs={{64,0},{128,64},{192,128},{256,192},{320,256},{384,320},{448,384},... | collective-permute-start | bytes 147464 | tf_op jit(solution)/shard_map/ppermute | solution.py:360
  98.6 6.6 %collective-permute-start.1 = (bf16[2,96,128]{2,1,0:T(8,128)(2,1)S(1)}, bf16[2,96,128]{2,1,0:T(8,128)(2,1)S(1)}, u32[]{:S(2)}, u32[]{:S(2)}) collective-permute-start(bf16[2,96,128]{2,1,0:T(8,128)(2,1)S(1)} %get-tuple-element.14), channel_id=1, source_target_pairs={{0,64},{64,128},{128,192},{192,256},{256,320},{320,384},{384,448},... | collective-permute-start | bytes 147464 | tf_op jit(solution)/shard_map/ppermute | solution.py:361
  105.2 14.9 %collective-permute-start.2 = (bf16[2,12,5,8,128]{4,3,2,1,0:T(8,128)(2,1)S(1)}, bf16[2,12,5,8,128]{4,3,2,1,0:T(8,128)(2,1)S(1)}, u32[]{:S(2)}, u32[]{:S(2)}) collective-permute-start(bf16[2,12,5,8,128]{4,3,2,1,0:T(8,128)(2,1)S(1)} %shard_map.42.wide), channel_id=1, source_target_pairs={{0,1},{1,0},{2,3},{3,2},{4,5},{5,4},{6,7},{7,6},{8,9},{9,8},{10,11... | collective-permute-start | bytes 737288 | tf_op jit(solution)/shard_map/ppermute | solution.py:364
  109.1 16.0 %collective-permute-start.3 = (bf16[2,12,5,8,128]{4,3,2,1,0:T(8,128)(2,1)S(1)}, bf16[2,12,5,8,128]{4,3,2,1,0:T(8,128)(2,1)S(1)}, u32[]{:S(2)}, u32[]{:S(2)}) collective-permute-start(bf16[2,12,5,8,128]{4,3,2,1,0:T(8,128)(2,1)S(1)} %shard_map.42.wide), channel_id=1, source_target_pairs={{0,63},{1,2},{2,1},{3,4},{4,3},{5,6},{6,5},{7,8},{8,7},{9,10},{10,... | collective-permute-start | bytes 737288 | tf_op jit(solution)/shard_map/ppermute | solution.py:363
  113.8 11.3 %collective-permute-start.12 = (bf16[12,8,128]{2,1,0:T(8,128)(2,1)S(1)}, bf16[12,8,128]{2,1,0:T(8,128)(2,1)S(1)}, u32[]{:S(2)}, u32[]{:S(2)}) collective-permute-start(bf16[12,8,128]{2,1,0:T(8,128)(2,1)S(1)} %fusion), channel_id=1, source_target_pairs={{1,65},{3,67},{5,69},{7,71},{9,73},{11,75},{13,77},{15,79},{17,81}... | collective-permute-start | bytes 73736 | tf_op jit(solution)/shard_map/ppermute | solution.py:393
  115.7 9.4 %collective-permute-start.13 = (bf16[12,8,128]{2,1,0:T(8,128)(2,1)S(1)}, bf16[12,8,128]{2,1,0:T(8,128)(2,1)S(1)}, u32[]{:S(2)}, u32[]{:S(2)}) collective-permute-start(bf16[12,8,128]{2,1,0:T(8,128)(2,1)S(1)} %fusion), channel_id=1, source_target_pairs={{1,64},{3,66},{5,68},{7,70},{9,72},{11,74},{13,76},{15,78},{17,80}... | collective-permute-start | bytes 73736 | tf_op jit(solution)/shard_map/ppermute | solution.py:394

commit v5 on v4

--- a/solution.py
+++ b/solution.py
@@ -185,39 +185,46 @@
         target[:, :, :, 128 * n : 128 * (n + width)] = total.reshape(*target.shape[:3], 128 * width)
 
 
-def spread_rows(sr, partner, beyond, a_rows):
-    src, rcv = position()
-    first, last = bounds(rcv)
-
-    def held(a):
-        return 4 * ((src + 3 - a % 3) % 3) + (src // 3 + 4 - a // 3) % 4
+def place(a):
+    src = position()[0]
+    return 4 * ((src + 3 - a % 3) % 3) + (src // 3 + 4 - a // 3) % 4
+
+
+def halves(a_rows):
+    left = a_rows[...].reshape(a_rows.shape[0] * a_rows.shape[1], 128 * TILES)
+    return left[:, : 64 * TILES], left[:, 64 * TILES :]
+
+
+def times(x, y):
+    return lax.dot_general(x, y, (((1,), (1,)), ((), ())), preferred_element_type=F32)
+
+
+def products(a_rows, b_rows, guess):
+    left = halves(a_rows)
+    values = []
+    for n in range(NZ // 2):
+        cols = slice(256 * n, 256 * n + 256)
+        right = b_rows[cols, : 64 * TILES], b_rows[cols, 64 * TILES :]
+        value = (
+            times(left[0], right[0]) - times(left[1], right[1]),
+            times(left[0], right[1]) + times(left[1], right[0]),
+        )
+        values.append([v.reshape(*a_rows.shape[:2], 256) for v in value])
+        for part in range(2):
+            guess[part, :, :, cols] = values[-1][part].astype(BF16)
+    return values
+
+
+def predict_kernel(sr, partner, ss, sp, guess, mult, a_rows, b_rows):
+    core = position()[1] % 2
 
     def spread(a, _):
-        lo, hi, keep_lo, keep_hi = neighbours(a, first, last)
-        lo, hi, mid = held(lo), held(hi), held(a)
         for t in range(TILES):
-            below, _ = sides(rcv % 2, partner[lo, t].astype(F32), beyond[lo, t].astype(F32))
-            _, above = sides(rcv % 2, partner[hi, t].astype(F32), beyond[hi, t].astype(F32))
-            x = jnp.concatenate([below * keep_lo, sr[mid, t].astype(F32), above * keep_hi], axis=0)
+            x = jnp.concatenate([sr[place(a), t].astype(F32), partner[place(a), t].astype(F32)], axis=0)
             a_rows[a, :, 128 * t : 128 * t + 128] = x.astype(BF16)
         return 0
 
     lax.fori_loop(0, NA, spread, 0, unroll=2)
-
-
-def halves(a_rows):
-    left = a_rows[...].reshape(24 * NA, 128 * TILES)
-    return left[:, : 64 * TILES], left[:, 64 * TILES :]
-
-
-def times(x, y):
-    return lax.dot_general(x, y, (((1,), (1,)), ((), ())), preferred_element_type=F32)
-
-
-def predict_kernel(sr, partner, beyond, ss, sp, guess, mult, a_rows, b_rows):
-    core = position()[1] % 2
-    spread_rows(sr, partner, beyond, a_rows)
-    left = halves(a_rows)
     for z in range(NZ):
         for t in range(TILES):
             mine, theirs = ss[:, z, t].astype(F32), sp[:, z, t].astype(F32)
@@ -225,23 +232,29 @@
             one = jnp.where(core == 0, theirs, mine)
             x = jnp.stack([zero, one], axis=1).reshape(128, 128)
             b_rows[128 * z : 128 * z + 128, 128 * t : 128 * t + 128] = x.astype(BF16)
-    for n in range(NZ // 2):
-        cols = slice(256 * n, 256 * n + 256)
-        right = b_rows[cols, : 64 * TILES], b_rows[cols, 64 * TILES :]
-        value = (
-            times(left[0], right[0]) - times(left[1], right[1]),
-            times(left[0], right[1]) + times(left[1], right[0]),
-        )
+    for n, value in enumerate(products(a_rows, b_rows, guess)):
         for part in range(2):
-            full = value[part].reshape(NA, 24, 256)
-            guess[part, :, :, cols] = full.astype(BF16)
-            mult[part, :, :, cols] = (full[:, 8:16] * (768.0 ** -0.5)).astype(BF16)
-
-
-def subtract_kernel(wide, partner, beyond, guess, a_rows, row_same, row_cross, prim, data, edge, once, box):
+            mult[part, :, :, 256 * n : 256 * n + 256] = (value[part][:, :8] * (768.0 ** -0.5)).astype(BF16)
+
+
+def predict_far_kernel(beyond, b_rows, guess, a_rows):
     rcv = position()[1]
     first, last = bounds(rcv)
-    left = halves(a_rows)
+
+    def spread(a, _):
+        lo, hi, keep_lo, keep_hi = neighbours(a, first, last)
+        run, keep = jnp.where(rcv % 2 == 0, lo, hi), jnp.where(rcv % 2 == 0, keep_lo, keep_hi)
+        for t in range(TILES):
+            a_rows[a, :, 128 * t : 128 * t + 128] = (beyond[place(run), t].astype(F32) * keep).astype(BF16)
+        return 0
+
+    lax.fori_loop(0, NA, spread, 0, unroll=2)
+    products(a_rows, b_rows, guess)
+
+
+def subtract_kernel(wide, partner, beyond, near, far, near_rows, far_rows, row_same, row_cross, prim, data, guess, edge, edge_far, once, box):
+    rcv = position()[1]
+    first, last = bounds(rcv)
     rims = [(row_same[t].astype(F32), row_cross[t].astype(F32)) for t in range(TILES)]
     row_hi = [jnp.where(rcv % 2 == 0, same, cross) for same, cross in rims]
     row_lo = [jnp.where(rcv % 2 == 0, cross, same) for same, cross in rims]
@@ -258,16 +271,22 @@
                 axis=0,
             ).astype(BF16)
         )
-    straight = times(left[0], jnp.concatenate(right, axis=0))
-    crossed = times(left[1], jnp.concatenate(right[::-1], axis=0))
-    edge[0] = (straight[:, :128] - crossed[:, :128]).astype(BF16).astype(F32).reshape(NA, 24, 128)
-    edge[1] = (straight[:, 128:] + crossed[:, 128:]).astype(BF16).astype(F32).reshape(NA, 24, 128)
+    for a_rows, target in ((near_rows, edge), (far_rows, edge_far)):
+        left = halves(a_rows)
+        straight = times(left[0], jnp.concatenate(right, axis=0))
+        crossed = times(left[1], jnp.concatenate(right[::-1], axis=0))
+        real, imag = straight[:, :128] - crossed[:, :128], straight[:, 128:] + crossed[:, 128:]
+        target[0] = real.astype(BF16).astype(F32).reshape(*a_rows.shape[:2], 128)
+        target[1] = imag.astype(BF16).astype(F32).reshape(*a_rows.shape[:2], 128)
 
     def run_of(ref, part, a):
         return jnp.concatenate([ref[part, a, n].astype(F32) for n in range(EXT // 128)], axis=1)
 
-    def guess_of(a):
-        return [jnp.concatenate([guess[part, a].astype(F32), edge[part, a]], axis=1) for part in range(2)]
+    def guess_of(part, a):
+        inner = jnp.concatenate([near[part, a].astype(F32), edge[part, a]], axis=1)
+        outer = jnp.concatenate([far[part, a].astype(F32), edge_far[part, a]], axis=1)
+        below, above = sides(rcv % 2, inner[8:], outer)
+        return jnp.concatenate([below, inner[:8], above], axis=0)
 
     def terms_of(dr, di, pr, pi):
         return pr * dr + pi * di, pr * di - pi * dr, pr * pr + pi * pi
@@ -283,9 +302,10 @@
             below, _ = sides(rcv % 2, run_of(partner, part, lo), run_of(beyond, part, lo))
             _, above = sides(rcv % 2, run_of(partner, part, hi), run_of(beyond, part, hi))
             data[part, a] = jnp.concatenate([below * keep_lo, run_of(wide, part, a), above * keep_hi], axis=0)
+            guess[part, a] = guess_of(part, a)
         dr, di = data[0, a], data[1, a]
         weight = 1.5 - jnp.tanh(dr * dr + di * di)
-        for n, q in enumerate(terms_of(dr, di, *guess_of(a))):
+        for n, q in enumerate(terms_of(dr, di, guess[0, a], guess[1, a])):
             once[n, a] = windows_rows(weight * q, 16)
         return 0
 
@@ -296,7 +316,7 @@
 
     def second_sweep(a, _):
         dr, di = data[0, a, 4:20], data[1, a, 4:20]
-        pr, pi = [v[4:20] for v in guess_of(a)]
+        pr, pi = guess[0, a, 4:20], guess[1, a, 4:20]
         er, ei = subtract(dr, di, pr, pi, [box[n, a] for n in range(3)])
         again = 1.5 - jnp.tanh(er * er + ei * ei)
         for n, q in enumerate(terms_of(dr, di, pr, pi)):
@@ -308,7 +328,7 @@
 
     def finish(a, _):
         dr, di = [data[part, a, 8:16, :512] for part in range(2)]
-        pr, pi = [guess[part, a].astype(F32)[8:16] for part in range(2)]
+        pr, pi = [guess[part, a, 8:16, :512] for part in range(2)]
         er, ei = subtract(dr, di, pr, pi, [box[n, a, :8, :512] for n in range(3)])
         prim[0, a], prim[1, a] = er.astype(BF16), ei.astype(BF16)
         return 0
@@ -393,28 +413,38 @@
     row_same = lax.ppermute(row, ("src", "rcv"), same)
     row_cross = lax.ppermute(row, ("src", "rcv"), cross)
     sp = lax.ppermute(ss, "rcv", swap)
-    guess, mult, left = kernel(
+    wide_rows = (512, 128 * TILES)
+    guess, mult, left, right = kernel(
         predict_kernel,
-        (shape(2, NA, 24, 512), shape(2, NA, 8, 512), shape(NA, 24, 128 * TILES)),
+        (shape(2, NA, 16, 512), shape(2, NA, 8, 512), shape(NA, 16, 128 * TILES), shape(*wide_rows)),
         (),
-        (sr, sr_partner, sr_beyond, ss, sp),
-        [pltpu.VMEM((512, 128 * TILES), BF16)],
+        (sr, sr_partner, ss, sp),
         flops=1 << 32,
         limit=16 << 20,
+    )
+    guess_far, left_far = kernel(
+        predict_far_kernel,
+        (shape(2, NA, 8, 512), shape(NA, 8, 128 * TILES)),
+        (),
+        (sr_beyond, right),
+        flops=1 << 31,
+        limit=12 << 20,
     )
     prim = kernel(
         subtract_kernel,
         shape(2, NA, 8, 512),
         (),
-        (wide, wide_partner, wide_beyond, guess, left, row_same, row_cross),
+        (wide, wide_partner, wide_beyond, guess, guess_far, left, left_far, row_same, row_cross),
         [
             pltpu.VMEM((2, NA, 24, EXT), F32),
-            pltpu.VMEM((2, NA, 24, 128), F32),
+            pltpu.VMEM((2, NA, 24, EXT), F32),
+            pltpu.VMEM((2, NA, 16, 128), F32),
+            pltpu.VMEM((2, NA, 8, 128), F32),
             pltpu.VMEM((3, NA, 16, EXT), F32),
             pltpu.VMEM((3, NA, 16, EXT), F32),
         ],
         flops=1 << 32,
-        limit=20 << 20,
+        limit=24 << 20,
     )
     return prim.reshape(record.shape), mult.reshape(record.shape)
 

time: 131 us -> 137 us (1.046)
  the two profiles are of different devices: /device:TPU:61 before, /device:TPU:121 now
where the time goes in v5:
time: 137 us
  starting transfers between devices  72.2 us (53%)
  blocking collectives  24 us (18%)
  waiting for transfers between devices  23.6 us (17%)
  Pallas kernels  14.2 us (10%)
  local copies, waits for them, and re-layouts  1.7 us (1%)
    all_to_all x1, blocking collectives, exchange(): lax.all_to_all(x, axis, split_axis=0, concat_axis=0, tiled=True, axis_ind...  24 us
    all_to_all x3, starting transfers between devices, exchange(): lax.all_to_all(x, axis, split_axis=0, concat_axis=0, tiled=True, axis_ind...  22.3 us
    pallas_call x9, Pallas kernels, kernel(): pl.pallas_call(body, out_shape=outs, in_specs=smem(len(scalars)) + vmem(l...  14.2 us
    ppermute x1, waiting for transfers between devices, block(): sr_beyond = lax.ppermute(sr, 'rcv', beyond)  12.6 us
    ppermute x1, starting transfers between devices, block(): wide_beyond = lax.ppermute(wide, 'rcv', beyond)  9.65 us
    ppermute x3, starting transfers between devices, block(): lax.ppermute(own, 'src', ring(src_count, 3 * d, True))  8.55 us
    ppermute x1, starting transfers between devices, block(): sp = lax.ppermute(ss, 'rcv', swap)  7.51 us
    all_to_all x3, waiting for transfers between devices, exchange(): lax.all_to_all(x, axis, split_axis=0, concat_axis=0, tiled=True, axis_ind...  6.72 us
  transfers between devices with their start and end apart: 17, of which 6 were waited for; matrix products, arithmetic and copies ran while one was open for 0% of the time, Pallas kernels for 4%

profile of v5, /device:TPU:121, one launch (start us, length us, event | category | flops | bytes accessed | tf_op | source)
XLA Modules:
  0.0 136.7 jit_solution(16523391656191116964)
XLA Ops:
  0.6 1.8 %shard_map.41 = bf16[12,8,128]{2,1,0:T(8,128)(2,1)} custom-call(s32[768]{0:T(1024)} %panel.3, bf16[2,96,512]{2,1,0:T(8,128)(2,1)} %bitcast.13), custom_call_target="tpu_custom_call" | custom-call | flops 1048576 | bytes 1048576 | tf_op jit(solution)/shard_map/pallas_call | solution.py:361
  2.5 7.0 %all-to-all-start = ((bf16[12,8,128]{2,1,0:T(8,128)(2,1)}), bf16[12,8,128]{2,1,0:T(8,128)(2,1)S(1)}, u32[]{:S(2)}, u32[]{:S(2)}) async-start(bf16[12,8,128]{2,1,0:T(8,128)(2,1)} %shard_map.41), calls=%async_computation | async-start | bytes 49152 | tf_op jit(solution)/shard_map/all_to_all | solution.py:357
  9.5 0.0 copy-start
  9.5 0.9 copy-done
  10.4 0.0 copy-start.2
  10.4 0.7 copy-done.2
  11.1 1.5 %shard_map.43 = bf16[16,8,128]{2,1,0:T(8,128)(2,1)} custom-call(s32[768]{0:T(1024)S(1)} %copy-done.2, bf16[2,96,512]{2,1,0:T(8,128)(2,1)S(1)} %bitcast.14), custom_call_target="tpu_custom_call" | custom-call | flops 1048576 | bytes 1048576 | tf_op jit(solution)/shard_map/pallas_call | solution.py:361
  12.5 1.8 %all-to-all-done.from_src = bf16[12,8,128]{2,1,0:T(8,128)(2,1)S(1)} async-done(((bf16[12,8,128]{2,1,0:T(8,128)(2,1)}), bf16[12,8,128]{2,1,0:T(8,128)(2,1)S(1)}, u32[]{:S(2)}, u32[]{:S(2)}) %all-to-all-start) | async-done | bytes 24608 | tf_op jit(solution)/shard_map/all_to_all | solution.py:357
  14.4 9.3 %all-to-all-start.1 = ((bf16[16,8,128]{2,1,0:T(8,128)(2,1)}), bf16[16,8,128]{2,1,0:T(8,128)(2,1)S(1)}, u32[]{:S(2)}, u32[]{:S(2)}) async-start(bf16[16,8,128]{2,1,0:T(8,128)(2,1)} %shard_map.43), calls=%async_computation.1 | async-start | bytes 65536 | tf_op jit(solution)/shard_map/all_to_all | solution.py:357
  23.7 0.1 shard_map.44.behind
  23.8 0.0 copy-start.1
  23.8 4.9 %all-to-all-done.1.from_rcv = bf16[16,8,128]{2,1,0:T(8,128)(2,1)S(1)} async-done(((bf16[16,8,128]{2,1,0:T(8,128)(2,1)}), bf16[16,8,128]{2,1,0:T(8,128)(2,1)S(1)}, u32[]{:S(2)}, u32[]{:S(2)}) %all-to-all-start.1) | async-done | bytes 32800 | tf_op jit(solution)/shard_map/all_to_all | solution.py:357
  28.7 0.3 shard_map.45
  29.0 24.0 %all_to_all.20.pieces = bf16[4,24,8,128]{3,2,1,0:T(8,128)(2,1)S(1)} all-to-all(bf16[4,24,8,128]{3,2,1,0:T(8,128)(2,1)S(1)} %shard_map.45), channel_id=1, replica_groups={{0,16,32,48},{1,17,33,49},{2,18,34,50},{3,19,35,51},{4,20,36,52},{5,21,..., dimensions={0} | all-to-all | bytes 393216 | tf_op jit(solution)/shard_map/all_to_all | solution.py:357
  53.0 1.0 shard_map.46
  54.1 5.9 %all-to-all-start.3 = ((bf16[8,4,12,8,128]{4,3,2,1,0:T(8,128)(2,1)}), bf16[8,4,12,8,128]{4,3,2,1,0:T(8,128)(2,1)S(1)}, u32[]{:S(2)}, u32[]{:S(2)}) async-start(bf16[8,4,12,8,128]{4,3,2,1,0:T(8,128)(2,1)} %get-tuple-element.13), calls=%async_computation.3 | async-start | bytes 1572864 | tf_op jit(solution)/shard_map/all_to_all | solution.py:357
  60.0 2.2 %collective-permute-start.4 = (bf16[12,8,128]{2,1,0:T(8,128)(2,1)S(1)}, bf16[12,8,128]{2,1,0:T(8,128)(2,1)S(1)}, u32[]{:S(2)}, u32[]{:S(2)}) collective-permute-start(bf16[12,8,128]{2,1,0:T(8,128)(2,1)S(1)} %get-tuple-element.12), channel_id=1, source_target_pairs={{0,192},{64,256},{128,320},{192,384},{256,448},{320,512},{384,576}... | collective-permute-start | bytes 73736 | tf_op jit(solution)/shard_map/ppermute | solution.py:394
  62.2 3.7 %collective-permute-start.5 = (bf16[12,8,128]{2,1,0:T(8,128)(2,1)S(1)}, bf16[12,8,128]{2,1,0:T(8,128)(2,1)S(1)}, u32[]{:S(2)}, u32[]{:S(2)}) collective-permute-start(bf16[12,8,128]{2,1,0:T(8,128)(2,1)S(1)} %get-tuple-element.12), channel_id=1, source_target_pairs={{0,384},{64,448},{128,512},{192,576},{256,640},{320,704},{384,0},{... | collective-permute-start | bytes 73736 | tf_op jit(solution)/shard_map/ppermute | solution.py:394
  65.9 2.7 %collective-permute-start.6 = (bf16[12,8,128]{2,1,0:T(8,128)(2,1)S(1)}, bf16[12,8,128]{2,1,0:T(8,128)(2,1)S(1)}, u32[]{:S(2)}, u32[]{:S(2)}) collective-permute-start(bf16[12,8,128]{2,1,0:T(8,128)(2,1)S(1)} %get-tuple-element.12), channel_id=1, source_target_pairs={{0,576},{64,640},{128,704},{192,0},{256,64},{320,128},{384,192},{4... | collective-permute-start | bytes 73736 | tf_op jit(solution)/shard_map/ppermute | solution.py:394
  68.6 0.0 collective-permute-done.4
  68.6 0.0 collective-permute-done.5
  68.6 2.2 %collective-permute-done.6 = bf16[12,8,128]{2,1,0:T(8,128)(2,1)S(1)} collective-permute-done((bf16[12,8,128]{2,1,0:T(8,128)(2,1)S(1)}, bf16[12,8,128]{2,1,0:T(8,128)(2,1)S(1)}, u32[]{:S(2)}, u32[]{:S(2)}) %collective-permute-start.6) | collective-permute-done | bytes 24608 | tf_op jit(solution)/shard_map/ppermute | solution.py:394
  70.8 1.9 %collective-permute-start.7 = (bf16[4,12,8,128]{3,2,1,0:T(8,128)(2,1)S(1)}, bf16[4,12,8,128]{3,2,1,0:T(8,128)(2,1)S(1)}, u32[]{:S(2)}, u32[]{:S(2)}) collective-permute-start(bf16[4,12,8,128]{3,2,1,0:T(8,128)(2,1)S(1)} %pad_maximum_fusion), channel_id=1, source_target_pairs={{0,64},{64,128},{128,0},{192,256},{256,320},{320,192},{384,448},{4... | collective-permute-start | bytes 294920 | tf_op jit(solution)/shard_map/ppermute | solution.py:397
  72.7 3.4 %collective-permute-start.8 = (bf16[4,12,8,128]{3,2,1,0:T(8,128)(2,1)S(1)}, bf16[4,12,8,128]{3,2,1,0:T(8,128)(2,1)S(1)}, u32[]{:S(2)}, u32[]{:S(2)}) collective-permute-start(bf16[4,12,8,128]{3,2,1,0:T(8,128)(2,1)S(1)} %pad_maximum_fusion), channel_id=1, source_target_pairs={{0,128},{64,0},{128,64},{192,320},{256,192},{320,256},{384,512},{4... | collective-permute-start | bytes 294920 | tf_op jit(solution)/shard_map/ppermute | solution.py:397
  76.1 0.0 all-to-all-done.3.ss
  76.1 7.5 %collective-permute-start.10 = (bf16[8,4,12,8,128]{4,3,2,1,0:T(8,128)(2,1)S(1)}, bf16[8,4,12,8,128]{4,3,2,1,0:T(8,128)(2,1)S(1)}, u32[]{:S(2)}, u32[]{:S(2)}) collective-permute-start(bf16[8,4,12,8,128]{4,3,2,1,0:T(8,128)(2,1)S(1)} %all-to-all-done.3.ss), channel_id=1, source_target_pairs={{0,1},{1,0},{2,3},{3,2},{4,5},{5,4},{6,7},{7,6},{8,9},{9,8},{10,11... | collective-permute-start | bytes 2359304 | tf_op jit(solution)/shard_map/ppermute | solution.py:415
  83.7 0.0 collective-permute-done.7
  83.7 0.0 collective-permute-done.8
  83.7 2.5 %collective-permute-start.9 = (bf16[12,12,8,128]{3,2,1,0:T(8,128)(2,1)S(1)}, bf16[12,12,8,128]{3,2,1,0:T(8,128)(2,1)S(1)}, u32[]{:S(2)}, u32[]{:S(2)}) collective-permute-start(bf16[12,12,8,128]{3,2,1,0:T(8,128)(2,1)S(1)} %constant_dynamic-update-slice_fusion.sr), channel_id=1, source_target_pairs={{0,1},{1,0},{2,3},{3,2},{4,5},{5,4},{6,7},{7,6},{8,9},{9,8},{10,11... | collective-permute-start | bytes 884744 | tf_op jit(solution)/shard_map/ppermute | solution.py:401
  86.2 0.0 copy-done.1
  86.2 3.6 %collective-permute-start = (bf16[2,96,128]{2,1,0:T(8,128)(2,1)S(1)}, bf16[2,96,128]{2,1,0:T(8,128)(2,1)S(1)}, u32[]{:S(2)}, u32[]{:S(2)}) collective-permute-start(bf16[2,96,128]{2,1,0:T(8,128)(2,1)S(1)} %get-tuple-element.21), channel_id=1, source_target_pairs={{64,0},{128,64},{192,128},{256,192},{320,256},{384,320},{448,384},... | collective-permute-start | bytes 147464 | tf_op jit(solution)/shard_map/ppermute | solution.py:380
  89.9 2.7 %collective-permute-start.1 = (bf16[2,96,128]{2,1,0:T(8,128)(2,1)S(1)}, bf16[2,96,128]{2,1,0:T(8,128)(2,1)S(1)}, u32[]{:S(2)}, u32[]{:S(2)}) collective-permute-start(bf16[2,96,128]{2,1,0:T(8,128)(2,1)S(1)} %get-tuple-element.20), channel_id=1, source_target_pairs={{0,64},{64,128},{128,192},{192,256},{256,320},{320,384},{384,448},... | collective-permute-start | bytes 147464 | tf_op jit(solution)/shard_map/ppermute | solution.py:381
  92.6 0.1 collective-permute-done.next_src
  92.7 2.0 %collective-permute-done.1.last_src = bf16[2,96,128]{2,1,0:T(8,128)(2,1)S(1)} collective-permute-done((bf16[2,96,128]{2,1,0:T(8,128)(2,1)S(1)}, bf16[2,96,128]{2,1,0:T(8,128)(2,1)S(1)}, u32[]{:S(2)}, u32[]{:S(2)}) %collective-permute-start.1) | collective-permute-done | bytes 49184 | tf_op jit(solution)/shard_map/ppermute | solution.py:381
  94.8 3.4 %collective-permute-start.2 = (bf16[2,12,5,8,128]{4,3,2,1,0:T(8,128)(2,1)S(1)}, bf16[2,12,5,8,128]{4,3,2,1,0:T(8,128)(2,1)S(1)}, u32[]{:S(2)}, u32[]{:S(2)}) collective-permute-start(bf16[2,12,5,8,128]{4,3,2,1,0:T(8,128)(2,1)S(1)} %shard_map.42.wide), channel_id=1, source_target_pairs={{0,1},{1,0},{2,3},{3,2},{4,5},{5,4},{6,7},{7,6},{8,9},{9,8},{10,11... | collective-permute-start | bytes 737288 | tf_op jit(solution)/shard_map/ppermute | solution.py:384
  98.1 9.7 %collective-permute-start.3 = (bf16[2,12,5,8,128]{4,3,2,1,0:T(8,128)(2,1)S(1)}, bf16[2,12,5,8,128]{4,3,2,1,0:T(8,128)(2,1)S(1)}, u32[]{:S(2)}, u32[]{:S(2)}) collective-permute-start(bf16[2,12,5,8,128]{4,3,2,1,0:T(8,128)(2,1)S(1)} %shard_map.42.wide), channel_id=1, source_target_pairs={{0,63},{1,2},{2,1},{3,4},{4,3},{5,6},{6,5},{7,8},{8,7},{9,10},{10,... | collective-permute-start | bytes 737288 | tf_op jit(solution)/shard_map/ppermute | solution.py:383
  107.8 1.9 %collective-permute-start.11 = (bf16[12,12,8,128]{3,2,1,0:T(8,128)(2,1)S(1)}, bf16[12,12,8,128]{3,2,1,0:T(8,128)(2,1)S(1)}, u32[]{:S(2)}, u32[]{:S(2)}) collective-permute-start(bf16[12,12,8,128]{3,2,1,0:T(8,128)(2,1)S(1)} %constant_dynamic-update-slice_fusion.sr), channel_id=1, source_target_pairs={{0,63},{1,2},{2,1},{3,4},{4,3},{5,6},{6,5},{7,8},{8,7},{9,10},{10,... | collective-permute-start | bytes 884744 | tf_op jit(solution)/shard_map/ppermute | solution.py:400
  109.7 0.0 collective-permute-done.9.partner
  109.7 3.0 %collective-permute-start.12 = (bf16[12,8,128]{2,1,0:T(8,128)(2,1)S(1)}, bf16[12,8,128]{2,1,0:T(8,128)(2,1)S(1)}, u32[]{:S(2)}, u32[]{:S(2)}) collective-permute-start(bf16[12,8,128]{2,1,0:T(8,128)(2,1)S(1)} %fusion), channel_id=1, source_target_pairs={{1,65},{3,67},{5,69},{7,71},{9,73},{11,75},{13,77},{15,79},{17,81}... | collective-permute-start | bytes 73736 | tf_op jit(solution)/shard_map/ppermute | solution.py:413
  112.7 0.0 collective-permute-done.10.sp
  112.7 1.9 %collective-permute-start.13 = (bf16[12,8,128]{2,1,0:T(8,128)(2,1)S(1)}, bf16[12,8,128]{2,1,0:T(8,128)(2,1)S(1)}, u32[]{:S(2)}, u32[]{:S(2)}) collective-permute-start(bf16[12,8,128]{2,1,0:T(8,128)(2,1)S(1)} %fusion), channel_id=1, source_target_pairs={{1,64},{3,66},{5,68},{7,70},{9,72},{11,74},{13,76},{15,78},{17,80}... | collective-permute-start | bytes 73736 | tf_op jit(solution)/shard_map/ppermute | solution.py:414
  114.6 2.2 %shard_map.47 = (bf16[2,12,16,512]{3,2,1,0:T(8,128)(2,1)S(1)}, bf16[2,12,8,512]{3,2,1,0:T(8,128)(2,1)}, bf16[12,16,1536]{2,1,0:T(8,128)(2,1)S(1)}, bf16[512,1536]{1,0:T(8,128)(2,1)S(1)}) custom-call(bf16[12,12,8,128]{3,2,1,0:T(8,128)(2,1)S(1)} %constant_dynamic-update-slice_fusion.sr, bf16[12,12,8,128]{3,2,1,0:T(8,128)(2,1)S(1)} %collective-permute-done.9.partner, ...), custom_call_target="tpu_custom_call" | custom-call | flops 4294967296 | bytes 1048576 | tf_op jit(solution)/shard_map/pallas_call | solution.py:361
  116.9 12.6 %collective-permute-done.11.beyond = bf16[12,12,8,128]{3,2,1,0:T(8,128)(2,1)S(1)} collective-permute-done((bf16[12,12,8,128]{3,2,1,0:T(8,128)(2,1)S(1)}, bf16[12,12,8,128]{3,2,1,0:T(8,128)(2,1)S(1)}, u32[]{:S(2)}, u32[]{:S(2)}) %collective-permute-start.11) | collective-permute-done | bytes 294944 | tf_op jit(solution)/shard_map/ppermute | solution.py:400
  129.5 1.4 shard_map.48
  130.8 0.0 collective-permute-done.2.partner
  130.8 0.0 collective-permute-done.3.beyond
  130.8 0.0 collective-permute-done.12.row_same
  130.8 0.0 collective-permute-done.13.row_cross
  130.9 5.9 %shard_map.49 = bf16[2,12,8,512]{3,2,1,0:T(8,128)(2,1)} custom-call(bf16[2,12,5,8,128]{4,3,2,1,0:T(8,128)(2,1)S(1)} %shard_map.42.wide, bf16[2,12,5,8,128]{4,3,2,1,0:T(8,128)(2,1)S(1)} %collective-permute-done.2.partner, bf16[2,12,5,8,128]{4,3,2,1,0:T(8,128)(2,1)S(1)} %collective-permute-done.3.beyond, bf16[2,12,16,512]{3,2,1,0:T(8,128)(2,1)S(1)} %get-tuple-element.14.near, ...), custom_call_target="tpu_custom_call" | custom-call | flops 4294967296 | bytes 1048576 | tf_op jit(solution)/shard_map/pallas_call | solution.py:361
  (10 shorter events, 0.1 us)
Async XLA Ops:
  2.5 11.9 %all-to-all-start = ((bf16[12,8,128]{2,1,0:T(8,128)(2,1)}), bf16[12,8,128]{2,1,0:T(8,128)(2,1)S(1)}, u32[]{:S(2)}, u32[]{:S(2)}) async-start(bf16[12,8,128]{2,1,0:T(8,128)(2,1)} %shard_map.41), calls=%async_computation | async-start | bytes 49152 | tf_op jit(solution)/shard_map/all_to_all | solution.py:357
  9.5 0.9 copy-start
  10.4 0.7 copy-start.2
  14.4 14.3 %all-to-all-start.1 = ((bf16[16,8,128]{2,1,0:T(8,128)(2,1)}), bf16[16,8,128]{2,1,0:T(8,128)(2,1)S(1)}, u32[]{:S(2)}, u32[]{:S(2)}) async-start(bf16[16,8,128]{2,1,0:T(8,128)(2,1)} %shard_map.43), calls=%async_computation.1 | async-start | bytes 65536 | tf_op jit(solution)/shard_map/all_to_all | solution.py:357
  23.8 62.4 %copy-start.1 = (bf16[1,2,96,512]{3,2,1,0:T(8,128)(2,1)S(1)}, bf16[1,2,96,512]{3,2,1,0:T(8,128)(2,1)}, u32[]{:S(2)}) copy-start(bf16[1,2,96,512]{3,2,1,0:T(8,128)(2,1)} %param.2) | copy-start | bytes 589828
  54.1 22.0 %all-to-all-start.3 = ((bf16[8,4,12,8,128]{4,3,2,1,0:T(8,128)(2,1)}), bf16[8,4,12,8,128]{4,3,2,1,0:T(8,128)(2,1)S(1)}, u32[]{:S(2)}, u32[]{:S(2)}) async-start(bf16[8,4,12,8,128]{4,3,2,1,0:T(8,128)(2,1)} %get-tuple-element.13), calls=%async_computation.3 | async-start | bytes 1572864 | tf_op jit(solution)/shard_map/all_to_all | solution.py:357
  60.0 8.6 %collective-permute-start.4 = (bf16[12,8,128]{2,1,0:T(8,128)(2,1)S(1)}, bf16[12,8,128]{2,1,0:T(8,128)(2,1)S(1)}, u32[]{:S(2)}, u32[]{:S(2)}) collective-permute-start(bf16[12,8,128]{2,1,0:T(8,128)(2,1)S(1)} %get-tuple-element.12), channel_id=1, source_target_pairs={{0,192},{64,256},{128,320},{192,384},{256,448},{320,512},{384,576}... | collective-permute-start | bytes 73736 | tf_op jit(solution)/shard_map/ppermute | solution.py:394
  62.2 6.4 %collective-permute-start.5 = (bf16[12,8,128]{2,1,0:T(8,128)(2,1)S(1)}, bf16[12,8,128]{2,1,0:T(8,128)(2,1)S(1)}, u32[]{:S(2)}, u32[]{:S(2)}) collective-permute-start(bf16[12,8,128]{2,1,0:T(8,128)(2,1)S(1)} %get-tuple-element.12), channel_id=1, source_target_pairs={{0,384},{64,448},{128,512},{192,576},{256,640},{320,704},{384,0},{... | collective-permute-start | bytes 73736 | tf_op jit(solution)/shard_map/ppermute | solution.py:394
  65.9 4.9 %collective-permute-start.6 = (bf16[12,8,128]{2,1,0:T(8,128)(2,1)S(1)}, bf16[12,8,128]{2,1,0:T(8,128)(2,1)S(1)}, u32[]{:S(2)}, u32[]{:S(2)}) collective-permute-start(bf16[12,8,128]{2,1,0:T(8,128)(2,1)S(1)} %get-tuple-element.12), channel_id=1, source_target_pairs={{0,576},{64,640},{128,704},{192,0},{256,64},{320,128},{384,192},{4... | collective-permute-start | bytes 73736 | tf_op jit(solution)/shard_map/ppermute | solution.py:394
  70.8 12.9 %collective-permute-start.7 = (bf16[4,12,8,128]{3,2,1,0:T(8,128)(2,1)S(1)}, bf16[4,12,8,128]{3,2,1,0:T(8,128)(2,1)S(1)}, u32[]{:S(2)}, u32[]{:S(2)}) collective-permute-start(bf16[4,12,8,128]{3,2,1,0:T(8,128)(2,1)S(1)} %pad_maximum_fusion), channel_id=1, source_target_pairs={{0,64},{64,128},{128,0},{192,256},{256,320},{320,192},{384,448},{4... | collective-permute-start | bytes 294920 | tf_op jit(solution)/shard_map/ppermute | solution.py:397
  72.7 11.0 %collective-permute-start.8 = (bf16[4,12,8,128]{3,2,1,0:T(8,128)(2,1)S(1)}, bf16[4,12,8,128]{3,2,1,0:T(8,128)(2,1)S(1)}, u32[]{:S(2)}, u32[]{:S(2)}) collective-permute-start(bf16[4,12,8,128]{3,2,1,0:T(8,128)(2,1)S(1)} %pad_maximum_fusion), channel_id=1, source_target_pairs={{0,128},{64,0},{128,64},{192,320},{256,192},{320,256},{384,512},{4... | collective-permute-start | bytes 294920 | tf_op jit(solution)/shard_map/ppermute | solution.py:397
  76.1 36.6 %collective-permute-start.10 = (bf16[8,4,12,8,128]{4,3,2,1,0:T(8,128)(2,1)S(1)}, bf16[8,4,12,8,128]{4,3,2,1,0:T(8,128)(2,1)S(1)}, u32[]{:S(2)}, u32[]{:S(2)}) collective-permute-start(bf16[8,4,12,8,128]{4,3,2,1,0:T(8,128)(2,1)S(1)} %all-to-all-done.3.ss), channel_id=1, source_target_pairs={{0,1},{1,0},{2,3},{3,2},{4,5},{5,4},{6,7},{7,6},{8,9},{9,8},{10,11... | collective-permute-start | bytes 2359304 | tf_op jit(solution)/shard_map/ppermute | solution.py:415
  83.7 26.0 %collective-permute-start.9 = (bf16[12,12,8,128]{3,2,1,0:T(8,128)(2,1)S(1)}, bf16[12,12,8,128]{3,2,1,0:T(8,128)(2,1)S(1)}, u32[]{:S(2)}, u32[]{:S(2)}) collective-permute-start(bf16[12,12,8,128]{3,2,1,0:T(8,128)(2,1)S(1)} %constant_dynamic-update-slice_fusion.sr), channel_id=1, source_target_pairs={{0,1},{1,0},{2,3},{3,2},{4,5},{5,4},{6,7},{7,6},{8,9},{9,8},{10,11... | collective-permute-start | bytes 884744 | tf_op jit(solution)/shard_map/ppermute | solution.py:401
  86.2 6.5 %collective-permute-start = (bf16[2,96,128]{2,1,0:T(8,128)(2,1)S(1)}, bf16[2,96,128]{2,1,0:T(8,128)(2,1)S(1)}, u32[]{:S(2)}, u32[]{:S(2)}) collective-permute-start(bf16[2,96,128]{2,1,0:T(8,128)(2,1)S(1)} %get-tuple-element.21), channel_id=1, source_target_pairs={{64,0},{128,64},{192,128},{256,192},{320,256},{384,320},{448,384},... | collective-permute-start | bytes 147464 | tf_op jit(solution)/shard_map/ppermute | solution.py:380
  89.9 4.8 %collective-permute-start.1 = (bf16[2,96,128]{2,1,0:T(8,128)(2,1)S(1)}, bf16[2,96,128]{2,1,0:T(8,128)(2,1)S(1)}, u32[]{:S(2)}, u32[]{:S(2)}) collective-permute-start(bf16[2,96,128]{2,1,0:T(8,128)(2,1)S(1)} %get-tuple-element.20), channel_id=1, source_target_pairs={{0,64},{64,128},{128,192},{192,256},{256,320},{320,384},{384,448},... | collective-permute-start | bytes 147464 | tf_op jit(solution)/shard_map/ppermute | solution.py:381
  94.8 36.1 %collective-permute-start.2 = (bf16[2,12,5,8,128]{4,3,2,1,0:T(8,128)(2,1)S(1)}, bf16[2,12,5,8,128]{4,3,2,1,0:T(8,128)(2,1)S(1)}, u32[]{:S(2)}, u32[]{:S(2)}) collective-permute-start(bf16[2,12,5,8,128]{4,3,2,1,0:T(8,128)(2,1)S(1)} %shard_map.42.wide), channel_id=1, source_target_pairs={{0,1},{1,0},{2,3},{3,2},{4,5},{5,4},{6,7},{7,6},{8,9},{9,8},{10,11... | collective-permute-start | bytes 737288 | tf_op jit(solution)/shard_map/ppermute | solution.py:384
  98.1 32.7 %collective-permute-start.3 = (bf16[2,12,5,8,128]{4,3,2,1,0:T(8,128)(2,1)S(1)}, bf16[2,12,5,8,128]{4,3,2,1,0:T(8,128)(2,1)S(1)}, u32[]{:S(2)}, u32[]{:S(2)}) collective-permute-start(bf16[2,12,5,8,128]{4,3,2,1,0:T(8,128)(2,1)S(1)} %shard_map.42.wide), channel_id=1, source_target_pairs={{0,63},{1,2},{2,1},{3,4},{4,3},{5,6},{6,5},{7,8},{8,7},{9,10},{10,... | collective-permute-start | bytes 737288 | tf_op jit(solution)/shard_map/ppermute | solution.py:383
  107.8 21.7 %collective-permute-start.11 = (bf16[12,12,8,128]{3,2,1,0:T(8,128)(2,1)S(1)}, bf16[12,12,8,128]{3,2,1,0:T(8,128)(2,1)S(1)}, u32[]{:S(2)}, u32[]{:S(2)}) collective-permute-start(bf16[12,12,8,128]{3,2,1,0:T(8,128)(2,1)S(1)} %constant_dynamic-update-slice_fusion.sr), channel_id=1, source_target_pairs={{0,63},{1,2},{2,1},{3,4},{4,3},{5,6},{6,5},{7,8},{8,7},{9,10},{10,... | collective-permute-start | bytes 884744 | tf_op jit(solution)/shard_map/ppermute | solution.py:400
  109.7 21.1 %collective-permute-start.12 = (bf16[12,8,128]{2,1,0:T(8,128)(2,1)S(1)}, bf16[12,8,128]{2,1,0:T(8,128)(2,1)S(1)}, u32[]{:S(2)}, u32[]{:S(2)}) collective-permute-start(bf16[12,8,128]{2,1,0:T(8,128)(2,1)S(1)} %fusion), channel_id=1, source_target_pairs={{1,65},{3,67},{5,69},{7,71},{9,73},{11,75},{13,77},{15,79},{17,81}... | collective-permute-start | bytes 73736 | tf_op jit(solution)/shard_map/ppermute | solution.py:413
  112.7 18.1 %collective-permute-start.13 = (bf16[12,8,128]{2,1,0:T(8,128)(2,1)S(1)}, bf16[12,8,128]{2,1,0:T(8,128)(2,1)S(1)}, u32[]{:S(2)}, u32[]{:S(2)}) collective-permute-start(bf16[12,8,128]{2,1,0:T(8,128)(2,1)S(1)} %fusion), channel_id=1, source_target_pairs={{1,64},{3,66},{5,68},{7,70},{9,72},{11,74},{13,76},{15,78},{17,80}... | collective-permute-start | bytes 73736 | tf_op jit(solution)/shard_map/ppermute | solution.py:414
